TPU v7x, 128 devices: a whole 4x4x4 slice. The times are simulated.
128 devices in a mesh: pts: 8 (over y, z_lo), lmk: 16 (over z_hi, x, core).
Axes of the slice: x: 4, y: 4, z: 4 (z_hi: 2, z_lo: 2; z = z_hi * 2 + z_lo), core: 2. Of those that a mesh axis runs over, the one named last changes fastest.
Arguments:
- points: float32 [32768, 384], P('pts'), may hold values from -8 to 8
- labels: int32 [32768], P('pts'), may hold values from 0 to 127
- landmarks: float32 [32768, 384], P('lmk'), may hold values from -8 to 8
- coefficients: float32 [32768, 128], P('lmk'), may hold values from -3 to 3
Outputs:
- gradient: float32 [32768, 128], P('lmk')
All inputs are finite; a program needn't handle non-finite values.
Results may differ from a plain program's by a relative error of at most 0.0003.
Values sent between devices are 32-bit elements; how exact they have to be, the bound alone decides.
No kernel may reach another device: no remote copies, remote signals or barrier semaphores. Data moves between devices by JAX's collectives and lax.ppermute only.
A program may use at most 128 MiB of HBM per device.

v0:
```python
import functools
import math

import jax
import jax.numpy as jnp
from jax import lax
from jax.experimental import pallas as pl
from jax.experimental.pallas import tpu as pltpu
from jax.sharding import Mesh
from jax.sharding import PartitionSpec as P

LOSS_SCALE = 8192.0
RIDGE = 0.5
LANES = 128
AXES = ("y", "zl", "zh", "x", "core")
PTS = ("y", "zl")
CHIPS = ("zh", "x")
LMK = ("zh", "x", "core")
NT = (((1,), (1,)), ((), ()))
f32, bf16 = jnp.float32, jnp.bfloat16


def dot(a, b):
    return jnp.dot(a, b, preferred_element_type=f32)


def halves(x):
    high = x.astype(bf16)
    return high, (x - high.astype(f32)).astype(bf16)


def thirds(x):
    a = x.astype(bf16).astype(f32)
    b = (x - a).astype(bf16).astype(f32)
    return a, b, x - a - b


def norm_lanes(rows, columns):
    lane = lax.broadcasted_iota(jnp.int32, (rows, LANES), 1)
    out = jnp.zeros((rows, LANES), f32)
    for i, column in enumerate(columns):
        out = jnp.where(lane == i, column, out)
    return out.astype(bf16)


def prep_body(l_ref, c_ref, b_ref, cc_ref):
    rows, feats = l_ref.shape
    unit = math.log2(math.e) / feats
    mark = l_ref[...]
    high, low = halves(mark * (2.0 * unit))
    b_ref[:, :feats] = high
    b_ref[:, feats : 2 * feats] = low
    b_ref[:, 2 * feats : 3 * feats] = high
    norm = thirds(-unit * jnp.sum(mark * mark, axis=1, keepdims=True))
    b_ref[:, 3 * feats :] = norm_lanes(rows, [1.0, 1.0, 1.0, *norm])
    high, low = halves(c_ref[...])
    cc_ref[:, : high.shape[1]] = high
    cc_ref[:, high.shape[1] :] = low


def prep(landmarks, coefficients, block=512):
    marks, feats = landmarks.shape
    classes = coefficients.shape[1]
    wide = 3 * feats + LANES
    return pl.pallas_call(
        prep_body,
        grid=(marks // block,),
        in_specs=[
            pl.BlockSpec((block, feats), lambda i: (i, 0)),
            pl.BlockSpec((block, classes), lambda i: (i, 0)),
        ],
        out_specs=[
            pl.BlockSpec((block, wide), lambda i: (i, 0)),
            pl.BlockSpec((block, 2 * classes), lambda i: (i, 0)),
        ],
        out_shape=[
            jax.ShapeDtypeStruct((marks, wide), bf16),
            jax.ShapeDtypeStruct((marks, 2 * classes), bf16),
        ],
        name="prep",
    )(landmarks, coefficients)


def logits_body(first_ref, p_ref, b_ref, c_ref, hi_ref, lo_ref, out_ref, a_ref, *, tile):
    rows, feats = p_ref.shape
    marks = b_ref.shape[0]
    unit = math.log2(math.e) / feats
    point = p_ref[...]
    high, low = halves(point)
    a_ref[:, :feats] = high
    a_ref[:, feats : 2 * feats] = high
    a_ref[:, 2 * feats : 3 * feats] = low
    norm = thirds(-unit * jnp.sum(point * point, axis=1, keepdims=True))
    a_ref[:, 3 * feats :] = norm_lanes(rows, [*norm, 1.0, 1.0, 1.0])
    for j in range(marks // tile):
        cols = slice(j * tile, (j + 1) * tile)
        power = lax.dot_general(a_ref[...], b_ref[cols, :], NT, preferred_element_type=f32)
        kernel = jnp.exp2(power)
        high, low = halves(kernel)
        hi_ref[:, cols] = high
        lo_ref[:, cols] = low
    for u in range(2):
        part = slice(u * rows // 2, (u + 1) * rows // 2)
        both = dot(hi_ref[part, :], c_ref[...]) + dot(lo_ref[part, :], c_ref[...])
        out_ref[part, :] = both[:, : both.shape[1] // 2] + both[:, both.shape[1] // 2 :]


def kernel_and_logits(first_row, points, wide_marks, wide_coefs, rows, block=512, tile=512):
    feats = points.shape[1]
    marks, wide = wide_marks.shape
    classes = wide_coefs.shape[1] // 2
    fixed = pl.Buffered(1)
    first = (first_row // block).astype(jnp.int32).reshape(1)
    return pl.pallas_call(
        functools.partial(logits_body, tile=tile),
        grid_spec=pltpu.PrefetchScalarGridSpec(
            num_scalar_prefetch=1,
            grid=(rows // block,),
            in_specs=[
                pl.BlockSpec((block, feats), lambda i, s: (s[0] + i, 0)),
                pl.BlockSpec((marks, wide), lambda i, s: (0, 0), pipeline_mode=fixed),
                pl.BlockSpec((marks, 2 * classes), lambda i, s: (0, 0), pipeline_mode=fixed),
            ],
            out_specs=[
                pl.BlockSpec((block, marks), lambda i, s: (i, 0)),
                pl.BlockSpec((block, marks), lambda i, s: (i, 0)),
                pl.BlockSpec((block, classes), lambda i, s: (i, 0)),
            ],
            scratch_shapes=[pltpu.VMEM((block, wide), bf16)],
        ),
        out_shape=[
            jax.ShapeDtypeStruct((rows, marks), bf16),
            jax.ShapeDtypeStruct((rows, marks), bf16),
            jax.ShapeDtypeStruct((rows, classes), f32),
        ],
        cost_estimate=pl.CostEstimate(
            flops=2 * rows * marks * (wide + 4 * classes),
            bytes_accessed=4 * rows * (feats + marks + classes) + 2 * marks * (wide + 2 * classes),
            transcendentals=rows * marks,
        ),
        name="kernel_and_logits",
    )(first, points, wide_marks, wide_coefs)


def terms_body(*refs):
    r_ref, hi_ref, lo_ref, *before, out_ref, rt_ref = refs
    classes = r_ref.shape[1]

    @pl.when(pl.program_id(0) == 0)
    def _():
        resid = r_ref[...]
        high = resid.astype(bf16).astype(f32)
        rt_ref[:classes, :] = high.T.astype(bf16)
        rt_ref[classes:, :] = (resid - high).T.astype(bf16)

    both = dot(rt_ref[...], hi_ref[...]) + dot(rt_ref[...], lo_ref[...])
    out = (both[:classes, :] + both[classes:, :]).T
    for ref in before:
        out = out + ref[...]
    out_ref[...] = out


def terms(resid, high, low, before=None, block=512):
    rows, marks = high.shape
    classes = resid.shape[1]
    ins = [
        pl.BlockSpec((rows, classes), lambda i: (0, 0), pipeline_mode=pl.Buffered(1)),
        pl.BlockSpec((rows, block), lambda i: (0, i)),
        pl.BlockSpec((rows, block), lambda i: (0, i)),
    ]
    args = [resid, high, low]
    out_spec = pl.BlockSpec((block, classes), lambda i: (i, 0))
    if before is not None:
        ins.append(out_spec)
        args.append(before)
    return pl.pallas_call(
        terms_body,
        grid=(marks // block,),
        in_specs=ins,
        out_specs=out_spec,
        out_shape=jax.ShapeDtypeStruct((marks, classes), f32),
        scratch_shapes=[pltpu.VMEM((2 * classes, rows), bf16)],
        cost_estimate=pl.CostEstimate(
            flops=8 * rows * marks * classes,
            bytes_accessed=4 * rows * (marks + classes) + 8 * marks * classes,
            transcendentals=0,
        ),
        name="terms",
    )(*args)


def swapped(x):
    return lax.ppermute(x, "core", [(0, 1), (1, 0)])


def summed_share(x, axes):
    devices = lax.axis_size(axes)
    parts = x.reshape(devices, x.shape[0] // devices, x.shape[1])
    return lax.all_to_all(parts, axes, split_axis=0, concat_axis=0, tiled=True).sum(axis=0)


def all_shares(x, axes):
    devices = lax.axis_size(axes)
    copies = jnp.broadcast_to(x, (devices, *x.shape))
    parts = lax.all_to_all(copies, axes, split_axis=0, concat_axis=0, tiled=True)
    return parts.reshape(devices * x.shape[0], x.shape[1])


def residual_rows(logits, labels):
    classes = logits.shape[1]
    expo = jnp.exp(logits)
    onehot = (labels[:, None] == jnp.arange(classes, dtype=jnp.int32)[None, :]).astype(f32)
    return expo / jnp.sum(expo, axis=1, keepdims=True) - onehot


def per_device(points, labels, landmarks, coefficients):
    rows = points.shape[0] // 2
    core = lax.axis_index("core")
    wide_marks, wide_coefs = prep(landmarks, coefficients)
    far_hi, far_lo, far_logits = kernel_and_logits((1 - core) * rows, points, wide_marks, wide_coefs, rows)
    arrived = swapped(far_logits)
    own_hi, own_lo, own_logits = kernel_and_logits(core * rows, points, wide_marks, wide_coefs, rows)
    shares = summed_share(own_logits + arrived, CHIPS)
    share_rows = shares.shape[0]
    first = core * rows + lax.axis_index(CHIPS) * share_rows
    mine = lax.dynamic_slice_in_dim(labels, first, share_rows, 0)
    own_resid = all_shares(residual_rows(shares, mine), CHIPS)
    far_resid = swapped(own_resid)
    local = terms(own_resid, own_hi, own_lo)
    local = terms(far_resid, far_hi, far_lo, local)
    total_points = labels.shape[0] * lax.axis_size(PTS)
    share = summed_share(local, PTS)
    kept = share.shape[0]
    own_coefs = lax.dynamic_slice_in_dim(coefficients, lax.axis_index(PTS) * kept, kept, 0)
    return all_shares(share * (LOSS_SCALE / total_points) + RIDGE * own_coefs, PTS)


def solution(mesh):
    fine = Mesh(mesh.devices.reshape(4, 2, 2, 4, 2), AXES)
    in_specs = (P(PTS, None), P(PTS), P(LMK, None), P(LMK, None))
    return jax.shard_map(
        per_device, mesh=fine, in_specs=in_specs, out_specs=P(LMK, None), check_vma=False
    )
```

profile of v0, /device:TPU:0, one launch (start us, length us, event | category | flops | bytes accessed | tf_op | source)
XLA Modules:
  0.0 157.6 jit_solution(862183643585279374)
XLA Ops:
  0.0 5.6 %prep.1 = (bf16[2048,1280]{1,0:T(8,128)(2,1)}, bf16[2048,256]{1,0:T(8,128)(2,1)}) custom-call(f32[2048,384]{1,0:T(8,128)} %l_ref.1, f32[2048,128]{1,0:T(8,128)} %c_ref.1), custom_call_target="tpu_custom_call" | custom-call | tf_op jit(solution)/shard_map/prep/pallas_call | solution.py:65
  5.6 20.5 %kernel_and_logits.3 = (bf16[2048,2048]{1,0:T(8,128)(2,1)}, bf16[2048,2048]{1,0:T(8,128)(2,1)}, f32[2048,128]{1,0:T(8,128)}) custom-call(s32[1]{0:T(128)} %bitcast.1.first_ref, f32[4096,384]{1,0:T(8,128)} %p_ref.3, bf16[2048,1280]{1,0:T(8,128)(2,1)} %get-tuple-element.13.b_ref, bf16[2048,256]{1,0:T(8,128)(2,1)} %get-tuple-element.14.c_ref), custom_call_target="tpu_custom_call" | custom-call | flops 15032385536 | bytes 27262976 | tf_op jit(solution)/shard_map/kernel_and_logits/pallas_call | solution.py:114
  26.0 0.0 collective-permute-start
  26.0 20.5 %kernel_and_logits.2 = (bf16[2048,2048]{1,0:T(8,128)(2,1)}, bf16[2048,2048]{1,0:T(8,128)(2,1)}, f32[2048,128]{1,0:T(8,128)}) custom-call(s32[1]{0:T(128)} %bitcast.first_ref, f32[4096,384]{1,0:T(8,128)} %p_ref.3, bf16[2048,1280]{1,0:T(8,128)(2,1)} %get-tuple-element.13.b_ref, bf16[2048,256]{1,0:T(8,128)(2,1)} %get-tuple-element.14.c_ref), custom_call_target="tpu_custom_call" | custom-call | flops 15032385536 | bytes 27262976 | tf_op jit(solution)/shard_map/kernel_and_logits/pallas_call | solution.py:114
  46.5 2.3 %add.23 = f32[2048,128]{1,0:T(8,128)} add(f32[2048,128]{1,0:T(8,128)} %get-tuple-element.15, f32[2048,128]{1,0:T(8,128)S(1)} %collective-permute-done) | non-fusion elementwise | flops 262144 | bytes 3145728 | tf_op jit(solution)/shard_map/add | solution.py:223
  48.8 7.7 %all-to-all-start = ((f32[8,256,128]{2,1,0:T(8,128)}), f32[8,256,128]{2,1,0:T(8,128)S(1)}, u32[]{:S(2)}, u32[]{:S(2)}) async-start(f32[8,256,128]{2,1,0:T(8,128)} %bitcast.2), calls=%async_computation | async-start | bytes 2097152 | tf_op jit(solution)/shard_map/all_to_all | solution.py:199
  56.5 0.8 dynamic_slice.6
  57.3 17.1 %all-to-all-done = f32[8,256,128]{2,1,0:T(8,128)S(1)} async-done(((f32[8,256,128]{2,1,0:T(8,128)}), f32[8,256,128]{2,1,0:T(8,128)S(1)}, u32[]{:S(2)}, u32[]{:S(2)}) %all-to-all-start) | async-done | bytes 1048608 | tf_op jit(solution)/shard_map/all_to_all | solution.py:199
  74.4 0.1 reduce_sum.27
  74.4 0.1 exponential_reduce_fusion
  74.6 0.1 convert_subtract_fusion
  74.7 0.1 broadcast_in_dim.4
  74.8 19.8 %all_to_all.20 = f32[8,256,128]{2,1,0:T(8,128)S(1)} all-to-all(f32[8,256,128]{2,1,0:T(8,128)S(1)} %broadcast_in_dim.4), channel_id=1, replica_groups=mesh['y'=4,'zl'=2,'zh'=2,'x'=4,'core'=2] {'zh','x'}, dimensions={0} | all-to-all | bytes 2097152 | tf_op jit(solution)/shard_map/all_to_all | solution.py:205
  94.6 1.0 copy-done
  95.6 10.2 %terms.2.refs_3_ = f32[2048,128]{1,0:T(8,128)} custom-call(f32[2048,128]{1,0:T(8,128)} %bitcast.8, bf16[2048,2048]{1,0:T(8,128)(2,1)} %get-tuple-element.19.refs_1_, bf16[2048,2048]{1,0:T(8,128)(2,1)} %get-tuple-element.20.refs_2_), custom_call_target="tpu_custom_call" | custom-call | flops 4294967296 | bytes 19922944 | tf_op jit(solution)/shard_map/terms/pallas_call | solution.py:176
  105.8 1.0 copy-done.1
  106.8 11.0 %terms.3 = f32[2048,128]{1,0:T(8,128)} custom-call(f32[2048,128]{1,0:T(8,128)} %copy-done.1, bf16[2048,2048]{1,0:T(8,128)(2,1)} %get-tuple-element.17.refs_1_, bf16[2048,2048]{1,0:T(8,128)(2,1)} %get-tuple-element.18.refs_2_, f32[2048,128]{1,0:T(8,128)} %terms.2.refs_3_), custom_call_target="tpu_custom_call" | custom-call | flops 4294967296 | bytes 19922944 | tf_op jit(solution)/shard_map/terms/pallas_call | solution.py:176
  117.7 4.9 %all-to-all-start.2 = ((f32[8,256,128]{2,1,0:T(8,128)}), f32[8,256,128]{2,1,0:T(8,128)S(1)}, u32[]{:S(2)}, u32[]{:S(2)}) async-start(f32[8,256,128]{2,1,0:T(8,128)} %bitcast.6), calls=%async_computation.2 | async-start | bytes 2097152 | tf_op jit(solution)/shard_map/all_to_all | solution.py:199
  122.7 15.3 %all-to-all-done.2 = f32[8,256,128]{2,1,0:T(8,128)S(1)} async-done(((f32[8,256,128]{2,1,0:T(8,128)}), f32[8,256,128]{2,1,0:T(8,128)S(1)}, u32[]{:S(2)}, u32[]{:S(2)}) %all-to-all-start.2) | async-done | bytes 1048608 | tf_op jit(solution)/shard_map/all_to_all | solution.py:199
  138.0 0.1 reduce_sum.29
  138.1 0.9 multiply_add_fusion
  139.0 0.1 broadcast_in_dim.10
  139.1 17.5 %all_to_all.21 = f32[8,256,128]{2,1,0:T(8,128)S(1)} all-to-all(f32[8,256,128]{2,1,0:T(8,128)S(1)} %broadcast_in_dim.10), channel_id=1, replica_groups=mesh['y'=4,'zl'=2,'zh'=2,'x'=4,'core'=2] {'y','zl'}, dimensions={0} | all-to-all | bytes 2097152 | tf_op jit(solution)/shard_map/all_to_all | solution.py:205
  156.6 1.0 copy.6
  (5 shorter events, 0.0 us)
Async XLA Ops:
  26.0 20.5 %collective-permute-start = (f32[2048,128]{1,0:T(8,128)}, f32[2048,128]{1,0:T(8,128)S(1)}, u32[]{:S(2)}, u32[]{:S(2)}) collective-permute-start(f32[2048,128]{1,0:T(8,128)} %get-tuple-element.16), channel_id=1, source_target_pairs={{0,1},{1,0},{2,3},{3,2},{4,5},{5,4},{6,7},{7,6},{8,9},{9,8},{10,11... | collective-permute-start | bytes 3145736 | tf_op jit(solution)/shard_map/ppermute | solution.py:193
  48.8 25.6 %all-to-all-start = ((f32[8,256,128]{2,1,0:T(8,128)}), f32[8,256,128]{2,1,0:T(8,128)S(1)}, u32[]{:S(2)}, u32[]{:S(2)}) async-start(f32[8,256,128]{2,1,0:T(8,128)} %bitcast.2), calls=%async_computation | async-start | bytes 2097152 | tf_op jit(solution)/shard_map/all_to_all | solution.py:199
  94.6 1.0 copy-start
  94.6 11.2 %collective-permute-start.1 = (f32[2048,128]{1,0:T(8,128)S(1)}, f32[2048,128]{1,0:T(8,128)S(1)}, u32[]{:S(2)}, u32[]{:S(2)}) collective-permute-start(f32[2048,128]{1,0:T(8,128)S(1)} %bitcast.7), channel_id=1, source_target_pairs={{0,1},{1,0},{2,3},{3,2},{4,5},{5,4},{6,7},{7,6},{8,9},{9,8},{10,11... | collective-permute-start | bytes 3145736 | tf_op jit(solution)/shard_map/ppermute | solution.py:193
  105.8 1.0 copy-start.1
  117.7 20.3 %all-to-all-start.2 = ((f32[8,256,128]{2,1,0:T(8,128)}), f32[8,256,128]{2,1,0:T(8,128)S(1)}, u32[]{:S(2)}, u32[]{:S(2)}) async-start(f32[8,256,128]{2,1,0:T(8,128)} %bitcast.6), calls=%async_computation.2 | async-start | bytes 2097152 | tf_op jit(solution)/shard_map/all_to_all | solution.py:199
where the time goes:
time: 158 us
  Pallas kernels  67.7 us (43%)
  blocking collectives  37.4 us (24%)
  waiting for transfers between devices  32.4 us (21%)
  starting transfers between devices  12.6 us (8%)
  local copies, waits for them, and re-layouts  3.8 us (2%)
  other arithmetic  3.6 us (2%)
    pallas_call x2, Pallas kernels, kernel_and_logits(): pl.pallas_call(functools.partial(logits_body, tile=tile), grid_spec=pltpu...  40.9 us
    all_to_all x2, blocking collectives, all_shares(): lax.all_to_all(copies, axes, split_axis=0, concat_axis=0, tiled=True)  37.4 us
    all_to_all x2, waiting for transfers between devices, summed_share(): lax.all_to_all(parts, axes, split_axis=0, concat_axis=0, tiled=True)  32.4 us
    pallas_call x2, Pallas kernels, terms(): pl.pallas_call(terms_body, grid=(marks // block,), in_specs=ins, out_spec...  21.2 us
    all_to_all x2, starting transfers between devices, summed_share(): lax.all_to_all(parts, axes, split_axis=0, concat_axis=0, tiled=True)  12.6 us
    pallas_call x1, Pallas kernels, prep(): pl.pallas_call(prep_body, grid=(marks // block,), in_specs=[pl.BlockSpec(...  5.56 us
  transfers between devices with their start and end apart: 4, of which 2 were waited for; matrix products, arithmetic and copies ran while one was open for 0% of the time, Pallas kernels for 19%

commit v1 on v0

v1 whole, which is shorter than its diff:
```python
import functools
import math

import jax
import jax.numpy as jnp
from jax import lax
from jax.experimental import pallas as pl
from jax.experimental.pallas import tpu as pltpu
from jax.sharding import Mesh
from jax.sharding import PartitionSpec as P

LOSS_SCALE = 8192.0
RIDGE = 0.5
LIMIT_K1, LIMIT_K2 = 9, 9
LANES = 128
AXES = ("y", "zl", "zh", "x", "core")
PTS = ("y", "zl")
LMK = ("zh", "x", "core")
NT = (((1,), (1,)), ((), ()))
f32, bf16 = jnp.float32, jnp.bfloat16


def dot(a, b):
    return jnp.dot(a, b, preferred_element_type=f32)


def halves(x):
    high = x.astype(bf16)
    return high, (x - high.astype(f32)).astype(bf16)


def thirds(x):
    a = x.astype(bf16).astype(f32)
    b = (x - a).astype(bf16).astype(f32)
    return a, b, x - a - b


def norm_lanes(rows, columns):
    lane = lax.broadcasted_iota(jnp.int32, (rows, LANES), 1)
    out = jnp.zeros((rows, LANES), f32)
    for i, column in enumerate(columns):
        out = jnp.where(lane == i, column, out)
    return out.astype(bf16)


def prep_body(l_ref, c_ref, b_ref, cc_ref):
    rows, feats = l_ref.shape
    unit = math.log2(math.e) / feats
    mark = l_ref[...]
    high, low = halves(mark * (2.0 * unit))
    b_ref[:, :feats] = high
    b_ref[:, feats : 2 * feats] = low
    b_ref[:, 2 * feats : 3 * feats] = high
    norm = thirds(-unit * jnp.sum(mark * mark, axis=1, keepdims=True))
    b_ref[:, 3 * feats :] = norm_lanes(rows, [1.0, 1.0, 1.0, *norm])
    high, low = halves(c_ref[...])
    cc_ref[:, : high.shape[1]] = high
    cc_ref[:, high.shape[1] :] = low


def prep(landmarks, coefficients, block=512):
    marks, feats = landmarks.shape
    classes = coefficients.shape[1]
    wide = 3 * feats + LANES
    return pl.pallas_call(
        prep_body,
        grid=(marks // block,),
        in_specs=[
            pl.BlockSpec((block, feats), lambda i: (i, 0)),
            pl.BlockSpec((block, classes), lambda i: (i, 0)),
        ],
        out_specs=[
            pl.BlockSpec((block, wide), lambda i: (i, 0)),
            pl.BlockSpec((block, 2 * classes), lambda i: (i, 0)),
        ],
        out_shape=[
            pltpu.VMEM((marks, wide), bf16),
            pltpu.VMEM((marks, 2 * classes), bf16),
        ],
        compiler_params=pltpu.CompilerParams(vmem_limit_bytes=12 << 20),
        name="prep",
    )(landmarks, coefficients)


def logits_body(at_ref, p_ref, b_ref, c_ref, hi_ref, lo_ref, far_ref, own_ref, a_ref, *, tile):
    rows, feats = p_ref.shape
    marks = b_ref.shape[0]
    unit = math.log2(math.e) / feats
    point = p_ref[...]
    high, low = halves(point)
    a_ref[:, :feats] = high
    a_ref[:, feats : 2 * feats] = high
    a_ref[:, 2 * feats : 3 * feats] = low
    norm = thirds(-unit * jnp.sum(point * point, axis=1, keepdims=True))
    a_ref[:, 3 * feats :] = norm_lanes(rows, [*norm, 1.0, 1.0, 1.0])
    for j in range(marks // tile):
        cols = slice(j * tile, (j + 1) * tile)
        power = lax.dot_general(a_ref[...], b_ref[cols, :], NT, preferred_element_type=f32)
        kernel = jnp.exp2(power)
        high, low = halves(kernel)
        hi_ref[:, cols] = high
        lo_ref[:, cols] = low
    sums = []
    for u in range(2):
        part = slice(u * rows // 2, (u + 1) * rows // 2)
        both = dot(hi_ref[part, :], c_ref[...]) + dot(lo_ref[part, :], c_ref[...])
        sums.append(both[:, : both.shape[1] // 2] + both[:, both.shape[1] // 2 :])

    @pl.when(pl.program_id(0) == 0)
    def _():
        far_ref[...] = jnp.concatenate(sums, axis=0)

    @pl.when(pl.program_id(0) == 1)
    def _():
        own_ref[...] = jnp.concatenate(sums, axis=0)


def kernel_and_logits(at, shift, points, wide_marks, wide_coefs, block, tile=512):
    feats = points.shape[1]
    marks, wide = wide_marks.shape
    classes = wide_coefs.shape[1] // 2
    chips = points.shape[0] // (2 * block)
    fixed = pl.Buffered(1)
    return pl.pallas_call(
        functools.partial(logits_body, tile=tile),
        grid_spec=pltpu.PrefetchScalarGridSpec(
            num_scalar_prefetch=1,
            grid=(2,),
            in_specs=[
                pl.BlockSpec(
                    (block, feats),
                    lambda i, s: (lax.rem(s[0] + shift, chips) * 2 + lax.rem(s[1] + 1 + i, 2), 0),
                ),
                pl.BlockSpec((marks, wide), lambda i, s: (0, 0), pipeline_mode=fixed),
                pl.BlockSpec((marks, 2 * classes), lambda i, s: (0, 0), pipeline_mode=fixed),
            ],
            out_specs=[
                pl.BlockSpec((block, marks), lambda i, s: (i, 0)),
                pl.BlockSpec((block, marks), lambda i, s: (i, 0)),
                pl.BlockSpec((block, classes), lambda i, s: (0, 0)),
                pl.BlockSpec((block, classes), lambda i, s: (0, 0)),
            ],
            scratch_shapes=[pltpu.VMEM((block, wide), bf16)],
        ),
        out_shape=[
            pltpu.VMEM((2 * block, marks), bf16),
            pltpu.VMEM((2 * block, marks), bf16),
            pltpu.VMEM((block, classes), f32),
            pltpu.VMEM((block, classes), f32),
        ],
        compiler_params=pltpu.CompilerParams(vmem_limit_bytes=LIMIT_K1 << 20),
        cost_estimate=pl.CostEstimate(
            flops=4 * block * marks * (wide + 4 * classes),
            bytes_accessed=8 * block * (feats + marks + classes) + 2 * marks * (wide + 2 * classes),
            transcendentals=2 * block * marks,
        ),
        name="kernel_and_logits",
    )(at, points, wide_marks, wide_coefs)


def small_kernel(body, at, args, outs, name):
    whole = [pl.BlockSpec(x.shape, lambda i, s: (0, 0)) for x in (*args, *outs)]
    return pl.pallas_call(
        body,
        grid_spec=pltpu.PrefetchScalarGridSpec(
            num_scalar_prefetch=1,
            grid=(1,),
            in_specs=whole[: len(args)],
            out_specs=whole[len(args) :],
        ),
        out_shape=outs,
        compiler_params=pltpu.CompilerParams(vmem_limit_bytes=6 << 20),
        name=name,
    )(at, *args)


def split_body(at_ref, *refs):
    *ins, send_ref, keep_ref = refs
    rows = keep_ref.shape[0]
    for ref, which in ((send_ref, 1 - at_ref[2]), (keep_ref, at_ref[2])):
        part = pl.ds(pl.multiple_of(which * rows, rows), rows)
        total = ins[0][part, :]
        for x in ins[1:]:
            total = total + x[part, :]
        ref[...] = total


def residual_body(at_ref, labels_ref, a_ref, b_ref, out_ref):
    logits = a_ref[...] + b_ref[...]
    rows, classes = logits.shape
    groups = rows // LANES
    expo = jnp.exp(logits)
    share = expo / jnp.sum(expo, axis=1, keepdims=True)
    base = (at_ref[0] * 4 + at_ref[1] * 2 + at_ref[2]) * groups
    for g in range(groups):
        label = jnp.broadcast_to(labels_ref[pl.ds(base + g, 1), :], (LANES, LANES)).T
        hot = label == lax.broadcasted_iota(jnp.int32, (LANES, classes), 1)
        part = slice(g * LANES, (g + 1) * LANES)
        out_ref[part, :] = share[part, :] - hot.astype(f32)


def join_body(at_ref, own_ref, other_ref, out_ref):
    rows = own_ref.shape[0]
    for ref, which in ((own_ref, at_ref[2]), (other_ref, 1 - at_ref[2])):
        out_ref[pl.ds(pl.multiple_of(which * rows, rows), rows), :] = ref[...]


def terms_body(*refs, sets, tile):
    parts, (*before, out_ref, rt_ref) = refs[: 4 * sets], refs[4 * sets :]
    classes = parts[0].shape[1]
    block = parts[0].shape[0]
    marks = parts[2].shape[1]
    for n in range(sets):
        for h in range(2):
            resid = parts[4 * n + h][...]
            high = resid.astype(bf16).astype(f32)
            rows = slice((2 * n + h) * block, (2 * n + h + 1) * block)
            rt_ref[:classes, rows] = high.T.astype(bf16)
            rt_ref[classes:, rows] = (resid - high).T.astype(bf16)
    for j in range(marks // tile):
        cols = slice(j * tile, (j + 1) * tile)
        both = None
        for n in range(sets):
            left = rt_ref[:, 2 * n * block : 2 * (n + 1) * block]
            for ref in parts[4 * n + 2 : 4 * n + 4]:
                term = dot(left, ref[:, cols])
                both = term if both is None else both + term
        out = (both[:classes, :] + both[classes:, :]).T
        for ref in before:
            out = out + ref[cols, :]
        out_ref[cols, :] = out


def terms(sets, before=None, tile=512):
    args = [x for one in sets for x in one]
    block, classes = args[0].shape
    marks = args[2].shape[1]
    rows = 2 * block * len(sets)
    if before is not None:
        args.append(before)
    return pl.pallas_call(
        functools.partial(terms_body, sets=len(sets), tile=tile),
        in_specs=[pl.BlockSpec(memory_space=pltpu.VMEM)] * len(args),
        out_specs=pl.BlockSpec(memory_space=pltpu.VMEM),
        out_shape=pltpu.VMEM((marks, classes), f32),
        scratch_shapes=[pltpu.VMEM((2 * classes, rows), bf16)],
        compiler_params=pltpu.CompilerParams(vmem_limit_bytes=LIMIT_K2 << 20),
        cost_estimate=pl.CostEstimate(
            flops=8 * rows * marks * classes,
            bytes_accessed=4 * rows * (marks + classes) + 8 * marks * classes,
            transcendentals=0,
        ),
        name="terms",
    )(*args)


def swapped(x):
    return lax.ppermute(x, "core", [(0, 1), (1, 0)])


def summed_share(x, axes):
    devices = lax.axis_size(axes)
    parts = x.reshape(devices, x.shape[0] // devices, x.shape[1])
    return lax.all_to_all(parts, axes, split_axis=0, concat_axis=0, tiled=True).sum(axis=0)


def all_shares(x, axes):
    devices = lax.axis_size(axes)
    copies = jnp.broadcast_to(x, (devices, *x.shape))
    parts = lax.all_to_all(copies, axes, split_axis=0, concat_axis=0, tiled=True)
    return parts.reshape(devices * x.shape[0], x.shape[1])


def along_x(x, shift):
    chips = lax.axis_size("x")
    return lax.ppermute(x, "x", [(i, (i + shift) % chips) for i in range(chips)])


def across_z(x):
    return lax.ppermute(x, "zh", [(0, 1), (1, 0)])


def per_device(points, labels, landmarks, coefficients):
    chips, layers = lax.axis_size("x"), lax.axis_size("zh")
    classes = coefficients.shape[1]
    block = points.shape[0] // (2 * chips)
    rows = block // layers
    at = jnp.stack([lax.axis_index(n) for n in ("x", "core", "zh")]).astype(jnp.int32)
    points, landmarks, first_coefs = (
        pltpu.with_memory_space_constraint(x, pltpu.HBM) for x in (points, landmarks, coefficients)
    )
    at, landmarks = lax.optimization_barrier((at, landmarks))
    wide_marks, wide_coefs = prep(landmarks, first_coefs)
    made, sums, waiting = {}, [], None
    for shift in (2, 1, 3, 0):
        hi, lo, far, own = kernel_and_logits(at, shift, points, wide_marks, wide_coefs, block)
        made[shift] = hi, lo
        if waiting is not None:
            there, mine, arrived = waiting
            ready = mine + arrived
            at, ready = lax.optimization_barrier((at, ready))
            sums.append(along_x(ready, there))
        waiting = shift, own, swapped(far)
    sums += waiting[1:]
    half = jax.ShapeDtypeStruct((rows, classes), f32)
    send, keep = small_kernel(split_body, at, sums, [half, half], "split")
    by_group = labels.reshape(-1, LANES)
    (resid,) = small_kernel(residual_body, at, [by_group, keep, across_z(send)], [half], "residual")
    full = jax.ShapeDtypeStruct((block, classes), f32)
    (own,) = small_kernel(join_body, at, [resid, across_z(resid)], [full], "join")
    resids = {3: along_x(own, 1), 1: along_x(own, 3), 2: along_x(own, 2)}
    local = terms([(swapped(own), own, *made[0])])
    local, resids = lax.optimization_barrier((local, resids))
    local = terms([(swapped(resids[n]), resids[n], *made[n]) for n in (3, 1, 2)], local)
    total_points = labels.shape[0] * lax.axis_size(PTS)
    share = summed_share(local, PTS)
    kept = share.shape[0]
    own_coefs = lax.dynamic_slice_in_dim(coefficients, lax.axis_index(PTS) * kept, kept, 0)
    return all_shares(share * (LOSS_SCALE / total_points) + RIDGE * own_coefs, PTS)


def solution(mesh):
    fine = Mesh(mesh.devices.reshape(4, 2, 2, 4, 2), AXES)
    in_specs = (P(PTS, None), P(PTS), P(LMK, None), P(LMK, None))
    return jax.shard_map(
        per_device, mesh=fine, in_specs=in_specs, out_specs=P(LMK, None), check_vma=False
    )
```

time: 158 us -> 143 us (0.905)
  blocking collectives: 37.4 us -> 17.3 us
  starting transfers between devices: 12.6 us -> 25.1 us
  Pallas kernels: 67.7 us -> 55.4 us
  waiting for transfers between devices: 32.4 us -> 42.9 us
  local copies, waits for them, and re-layouts: 3.8 us -> 1.05 us
  other arithmetic: 3.6 us -> 1.16 us
    ppermute x0 -> x8, waiting for transfers between devices: none -> 24.6 us  [the longest x6 18 us: along_x(): lax.ppermute(x, 'x', [(i, (i + shift) % chips) for i in range(chips)])]
    all_to_all x2 -> x1, blocking collectives: 37.4 us -> 17.3 us  [all_shares(): lax.all_to_all(copies, axes, split_axis=0, concat_axis=0, tiled=True)]
    ppermute x0 -> x8, starting transfers between devices: none -> 18.5 us  [the longest x6 11.2 us: along_x(): lax.ppermute(x, 'x', [(i, (i + shift) % chips) for i in range(chips)])]
    all_to_all x2 -> x1, waiting for transfers between devices: 32.4 us -> 16.5 us  [summed_share(): lax.all_to_all(parts, axes, split_axis=0, concat_axis=0, tiled=True)]
    pallas_call x2 -> x5, Pallas kernels: 21.2 us -> 12.2 us  [the longest x2 10.3 us: terms(): pl.pallas_call(functools.partial(terms_body, sets=len(sets), tile=tile),...]
    all_to_all x2 -> x1, starting transfers between devices: 12.6 us -> 5.18 us  [summed_share(): lax.all_to_all(parts, axes, split_axis=0, concat_axis=0, tiled=True)]
    add x1 -> x3, other arithmetic: 2.3 us -> 0.1 us  [per_device(): ready = mine + arrived]
    pallas_call x1, Pallas kernels: 5.56 us -> 3.46 us  [prep(): pl.pallas_call(prep_body, grid=(marks // block,), in_specs=[pl.BlockSpec(...]
  transfers between devices with their start and end apart: 4 -> 17, of which waited for: 2 -> 9; matrix products, arithmetic and copies ran while one was open for 0% -> 0% of each run, Pallas kernels for 19% -> 23%
where the time goes in v1:
time: 143 us
  Pallas kernels  55.4 us (39%)
  waiting for transfers between devices  42.9 us (30%)
  starting transfers between devices  25.1 us (18%)
  blocking collectives  17.3 us (12%)
    pallas_call x4, Pallas kernels, kernel_and_logits(): pl.pallas_call(functools.partial(logits_body, tile=tile), grid_spec=pltpu...  39.7 us
    ppermute x6, waiting for transfers between devices, along_x(): lax.ppermute(x, 'x', [(i, (i + shift) % chips) for i in range(chips)])  18 us
    all_to_all x1, blocking collectives, all_shares(): lax.all_to_all(copies, axes, split_axis=0, concat_axis=0, tiled=True)  17.3 us
    all_to_all x1, waiting for transfers between devices, summed_share(): lax.all_to_all(parts, axes, split_axis=0, concat_axis=0, tiled=True)  16.5 us
    ppermute x6, starting transfers between devices, along_x(): lax.ppermute(x, 'x', [(i, (i + shift) % chips) for i in range(chips)])  11.2 us
    pallas_call x2, Pallas kernels, terms(): pl.pallas_call(functools.partial(terms_body, sets=len(sets), tile=tile),...  10.3 us
    ppermute x2, starting transfers between devices, across_z(): return lax.ppermute(x, 'zh', [(0, 1), (1, 0)])  7.29 us
    ppermute x2, waiting for transfers between devices, across_z(): return lax.ppermute(x, 'zh', [(0, 1), (1, 0)])  6.6 us
  transfers between devices with their start and end apart: 17, of which 9 were waited for; matrix products, arithmetic and copies ran while one was open for 0% of the time, Pallas kernels for 23%

profile of v1, /device:TPU:0, one launch (start us, length us, event | category | flops | bytes accessed | tf_op | source)
XLA Modules:
  0.0 143.0 jit_solution(4014226785902056270)
XLA Ops:
  0.1 3.5 %prep.1 = (bf16[2048,1280]{1,0:T(8,128)(2,1)S(1)}, bf16[2048,256]{1,0:T(8,128)(2,1)S(1)}) custom-call(f32[2048,384]{1,0:T(8,128)} %l_ref, f32[2048,128]{1,0:T(8,128)} %c_ref.1), custom_call_target="tpu_custom_call" | custom-call | tf_op jit(solution)/shard_map/prep/pallas_call | solution.py:65
  3.5 9.9 %kernel_and_logits.4 = (bf16[1024,2048]{1,0:T(8,128)(2,1)S(1)}, bf16[1024,2048]{1,0:T(8,128)(2,1)S(1)}, f32[512,128]{1,0:T(8,128)S(1)}, f32[512,128]{1,0:T(8,128)S(1)}) custom-call(s32[3]{0:T(128)S(1)} %pad_add_fusion.at_ref, f32[4096,384]{1,0:T(8,128)} %p_ref.7, bf16[2048,1280]{1,0:T(8,128)(2,1)S(1)} %get-tuple-element.39.b_ref, ...), custom_call_target="tpu_custom_call" | custom-call | flops 7516192768 | bytes 16777216 | tf_op jit(solution)/shard_map/kernel_and_logits/pallas_call | solution.py:124
  13.6 9.9 %kernel_and_logits.5 = (bf16[1024,2048]{1,0:T(8,128)(2,1)S(1)}, bf16[1024,2048]{1,0:T(8,128)(2,1)S(1)}, f32[512,128]{1,0:T(8,128)S(1)}, f32[512,128]{1,0:T(8,128)S(1)}) custom-call(s32[3]{0:T(128)S(1)} %pad_add_fusion.at_ref, f32[4096,384]{1,0:T(8,128)} %p_ref.7, bf16[2048,1280]{1,0:T(8,128)(2,1)S(1)} %get-tuple-element.39.b_ref, ...), custom_call_target="tpu_custom_call" | custom-call | flops 7516192768 | bytes 16777216 | tf_op jit(solution)/shard_map/kernel_and_logits/pallas_call | solution.py:124
  24.1 10.0 %kernel_and_logits.6 = (bf16[1024,2048]{1,0:T(8,128)(2,1)S(1)}, bf16[1024,2048]{1,0:T(8,128)(2,1)S(1)}, f32[512,128]{1,0:T(8,128)S(1)}, f32[512,128]{1,0:T(8,128)S(1)}) custom-call(s32[3]{0:T(128)S(1)} %pad_add_fusion.at_ref, f32[4096,384]{1,0:T(8,128)} %p_ref.7, bf16[2048,1280]{1,0:T(8,128)(2,1)S(1)} %get-tuple-element.39.b_ref, ...), custom_call_target="tpu_custom_call" | custom-call | flops 7516192768 | bytes 16777216 | tf_op jit(solution)/shard_map/kernel_and_logits/pallas_call | solution.py:124
  34.2 3.2 %collective-permute-start.3 = (f32[512,128]{1,0:T(8,128)S(1)}, f32[512,128]{1,0:T(8,128)S(1)}, u32[]{:S(2)}, u32[]{:S(2)}) collective-permute-start(f32[512,128]{1,0:T(8,128)S(1)} %add.18), channel_id=1, source_target_pairs={{0,4},{2,6},{4,0},{6,2},{1,5},{3,7},{5,1},{7,3},{8,12},{10,14},{12... | collective-permute-start | bytes 786440 | tf_op jit(solution)/shard_map/ppermute | solution.py:276
  38.0 9.9 %kernel_and_logits.7 = (bf16[1024,2048]{1,0:T(8,128)(2,1)S(1)}, bf16[1024,2048]{1,0:T(8,128)(2,1)S(1)}, f32[512,128]{1,0:T(8,128)S(1)}, f32[512,128]{1,0:T(8,128)S(1)}) custom-call(s32[3]{0:T(128)S(1)} %pad_add_fusion.at_ref, f32[4096,384]{1,0:T(8,128)} %p_ref.7, bf16[2048,1280]{1,0:T(8,128)(2,1)S(1)} %get-tuple-element.39.b_ref, ...), custom_call_target="tpu_custom_call" | custom-call | flops 7516192768 | bytes 16777216 | tf_op jit(solution)/shard_map/kernel_and_logits/pallas_call | solution.py:124
  48.1 2.7 %collective-permute-start.5 = (f32[512,128]{1,0:T(8,128)S(1)}, f32[512,128]{1,0:T(8,128)S(1)}, u32[]{:S(2)}, u32[]{:S(2)}) collective-permute-start(f32[512,128]{1,0:T(8,128)S(1)} %add.20), channel_id=1, source_target_pairs={{0,6},{2,0},{4,2},{6,4},{1,7},{3,1},{5,3},{7,5},{8,14},{10,8},{12,... | collective-permute-start | bytes 786440 | tf_op jit(solution)/shard_map/ppermute | solution.py:276
  50.8 6.2 %collective-permute-done.5.refs_2_ = f32[512,128]{1,0:T(8,128)S(1)} collective-permute-done((f32[512,128]{1,0:T(8,128)S(1)}, f32[512,128]{1,0:T(8,128)S(1)}, u32[]{:S(2)}, u32[]{:S(2)}) %collective-permute-start.5) | collective-permute-done | bytes 262176 | tf_op jit(solution)/shard_map/ppermute | solution.py:276
  57.6 4.0 %collective-permute-start.7 = (f32[256,128]{1,0:T(8,128)S(1)}, f32[256,128]{1,0:T(8,128)S(1)}, u32[]{:S(2)}, u32[]{:S(2)}) collective-permute-start(f32[256,128]{1,0:T(8,128)S(1)} %get-tuple-element.56), channel_id=1, source_target_pairs={{0,8},{8,0},{1,9},{9,1},{2,10},{10,2},{3,11},{11,3},{4,12},{12,4},... | collective-permute-start | bytes 393224 | tf_op jit(solution)/shard_map/ppermute | solution.py:280
  61.6 3.4 %collective-permute-done.7.b_ref = f32[256,128]{1,0:T(8,128)S(1)} collective-permute-done((f32[256,128]{1,0:T(8,128)S(1)}, f32[256,128]{1,0:T(8,128)S(1)}, u32[]{:S(2)}, u32[]{:S(2)}) %collective-permute-start.7) | collective-permute-done | bytes 131104 | tf_op jit(solution)/shard_map/ppermute | solution.py:280
  65.7 3.3 %collective-permute-start.8 = (f32[256,128]{1,0:T(8,128)S(1)}, f32[256,128]{1,0:T(8,128)S(1)}, u32[]{:S(2)}, u32[]{:S(2)}) collective-permute-start(f32[256,128]{1,0:T(8,128)S(1)} %residual.1.own_ref), channel_id=1, source_target_pairs={{0,8},{8,0},{1,9},{9,1},{2,10},{10,2},{3,11},{11,3},{4,12},{12,4},... | collective-permute-start | bytes 393224 | tf_op jit(solution)/shard_map/ppermute | solution.py:280
  69.0 3.2 %collective-permute-done.8.other_ref = f32[256,128]{1,0:T(8,128)S(1)} collective-permute-done((f32[256,128]{1,0:T(8,128)S(1)}, f32[256,128]{1,0:T(8,128)S(1)}, u32[]{:S(2)}, u32[]{:S(2)}) %collective-permute-start.8) | collective-permute-done | bytes 131104 | tf_op jit(solution)/shard_map/ppermute | solution.py:280
  72.9 3.8 %collective-permute-start.10 = (f32[512,128]{1,0:T(8,128)S(1)}, f32[512,128]{1,0:T(8,128)S(1)}, u32[]{:S(2)}, u32[]{:S(2)}) collective-permute-start(f32[512,128]{1,0:T(8,128)S(1)} %join.1.refs_1_), channel_id=1, source_target_pairs={{0,6},{2,0},{4,2},{6,4},{1,7},{3,1},{5,3},{7,5},{8,14},{10,8},{12,... | collective-permute-start | bytes 786440 | tf_op jit(solution)/shard_map/ppermute | solution.py:276
  76.7 0.9 collective-permute-start.12
  77.6 2.5 %terms.2.refs_12_ = f32[2048,128]{1,0:T(8,128)S(1)} custom-call(f32[512,128]{1,0:T(8,128)S(1)} %collective-permute-done.9.refs_0_, f32[512,128]{1,0:T(8,128)S(1)} %join.1.refs_1_, bf16[1024,2048]{1,0:T(8,128)(2,1)S(1)} %get-tuple-element.57.refs_2_, bf16[1024,2048]{1,0:T(8,128)(2,1)S(1)} %get-tuple-element.58.refs_3_), custom_call_target="tpu_custom_call" | custom-call | flops 2147483648 | bytes 11010048 | tf_op jit(solution)/shard_map/terms/pallas_call | solution.py:241
  80.1 8.3 %collective-permute-done.10.refs_5_ = f32[512,128]{1,0:T(8,128)S(1)} collective-permute-done((f32[512,128]{1,0:T(8,128)S(1)}, f32[512,128]{1,0:T(8,128)S(1)}, u32[]{:S(2)}, u32[]{:S(2)}) %collective-permute-start.10) | collective-permute-done | bytes 262176 | tf_op jit(solution)/shard_map/ppermute | solution.py:276
  88.5 3.4 %collective-permute-done.12.refs_1_ = f32[512,128]{1,0:T(8,128)S(1)} collective-permute-done((f32[512,128]{1,0:T(8,128)S(1)}, f32[512,128]{1,0:T(8,128)S(1)}, u32[]{:S(2)}, u32[]{:S(2)}) %collective-permute-start.12) | collective-permute-done | bytes 262176 | tf_op jit(solution)/shard_map/ppermute | solution.py:276
  92.4 1.0 collective-permute-done.13.refs_0_
  94.2 7.8 %terms.3 = f32[2048,128]{1,0:T(8,128)} custom-call(f32[512,128]{1,0:T(8,128)S(1)} %collective-permute-done.13.refs_0_, f32[512,128]{1,0:T(8,128)S(1)} %collective-permute-done.12.refs_1_, bf16[1024,2048]{1,0:T(8,128)(2,1)S(1)} %get-tuple-element.60.refs_2_, bf16[1024,2048]{1,0:T(8,128)(2,1)S(1)} %get-tuple-element.61.refs_3_, ...), custom_call_target="tpu_custom_call" | custom-call | flops 6442450944 | bytes 28835840 | tf_op jit(solution)/shard_map/terms/pallas_call | solution.py:241
  102.0 5.2 %all-to-all-start = ((f32[8,256,128]{2,1,0:T(8,128)}), f32[8,256,128]{2,1,0:T(8,128)S(1)}, u32[]{:S(2)}, u32[]{:S(2)}) async-start(f32[8,256,128]{2,1,0:T(8,128)} %bitcast.4), calls=%async_computation | async-start | bytes 2097152 | tf_op jit(solution)/shard_map/all_to_all | solution.py:264
  107.2 16.5 %all-to-all-done = f32[8,256,128]{2,1,0:T(8,128)S(1)} async-done(((f32[8,256,128]{2,1,0:T(8,128)}), f32[8,256,128]{2,1,0:T(8,128)S(1)}, u32[]{:S(2)}, u32[]{:S(2)}) %all-to-all-start) | async-done | bytes 1048608 | tf_op jit(solution)/shard_map/all_to_all | solution.py:264
  123.7 0.9 multiply_add_fusion
  124.7 17.3 %all_to_all.10 = f32[8,256,128]{2,1,0:T(8,128)S(1)} all-to-all(f32[8,256,128]{2,1,0:T(8,128)S(1)} %broadcast_in_dim.3), channel_id=1, replica_groups=mesh['y'=4,'zl'=2,'zh'=2,'x'=4,'core'=2] {'y','zl'}, dimensions={0} | all-to-all | bytes 2097152 | tf_op jit(solution)/shard_map/all_to_all | solution.py:270
  142.0 1.0 copy.6
  (31 shorter events, 5.0 us)
Async XLA Ops:
  13.5 10.6 %collective-permute-start = (f32[512,128]{1,0:T(8,128)S(1)}, f32[512,128]{1,0:T(8,128)S(1)}, u32[]{:S(2)}, u32[]{:S(2)}) collective-permute-start(f32[512,128]{1,0:T(8,128)S(1)} %get-tuple-element.42), channel_id=1, source_target_pairs={{0,1},{1,0},{2,3},{3,2},{4,5},{5,4},{6,7},{7,6},{8,9},{9,8},{10,11... | collective-permute-start | bytes 786440 | tf_op jit(solution)/shard_map/ppermute | solution.py:258
  23.5 10.6 %collective-permute-start.1 = (f32[512,128]{1,0:T(8,128)S(1)}, f32[512,128]{1,0:T(8,128)S(1)}, u32[]{:S(2)}, u32[]{:S(2)}) collective-permute-start(f32[512,128]{1,0:T(8,128)S(1)} %get-tuple-element.45), channel_id=1, source_target_pairs={{0,1},{1,0},{2,3},{3,2},{4,5},{5,4},{6,7},{7,6},{8,9},{9,8},{10,11... | collective-permute-start | bytes 786440 | tf_op jit(solution)/shard_map/ppermute | solution.py:258
  34.1 30.9 %copy-start = (s32[4096]{0:T(1024)S(1)}, s32[4096]{0:T(1024)}, u32[]{:S(2)}) copy-start(s32[4096]{0:T(1024)} %param.5) | copy-start | bytes 49156
  34.1 13.9 %collective-permute-start.2 = (f32[512,128]{1,0:T(8,128)S(1)}, f32[512,128]{1,0:T(8,128)S(1)}, u32[]{:S(2)}, u32[]{:S(2)}) collective-permute-start(f32[512,128]{1,0:T(8,128)S(1)} %get-tuple-element.48), channel_id=1, source_target_pairs={{0,1},{1,0},{2,3},{3,2},{4,5},{5,4},{6,7},{7,6},{8,9},{9,8},{10,11... | collective-permute-start | bytes 786440 | tf_op jit(solution)/shard_map/ppermute | solution.py:258
  34.2 16.5 %collective-permute-start.3 = (f32[512,128]{1,0:T(8,128)S(1)}, f32[512,128]{1,0:T(8,128)S(1)}, u32[]{:S(2)}, u32[]{:S(2)}) collective-permute-start(f32[512,128]{1,0:T(8,128)S(1)} %add.18), channel_id=1, source_target_pairs={{0,4},{2,6},{4,0},{6,2},{1,5},{3,7},{5,1},{7,3},{8,12},{10,14},{12... | collective-permute-start | bytes 786440 | tf_op jit(solution)/shard_map/ppermute | solution.py:276
  37.4 13.4 %collective-permute-start.4 = (f32[512,128]{1,0:T(8,128)S(1)}, f32[512,128]{1,0:T(8,128)S(1)}, u32[]{:S(2)}, u32[]{:S(2)}) collective-permute-start(f32[512,128]{1,0:T(8,128)S(1)} %add.19), channel_id=1, source_target_pairs={{0,2},{2,4},{4,6},{6,0},{1,3},{3,5},{5,7},{7,1},{8,10},{10,12},{12... | collective-permute-start | bytes 786440 | tf_op jit(solution)/shard_map/ppermute | solution.py:276
  47.9 2.9 %collective-permute-start.6 = (f32[512,128]{1,0:T(8,128)S(1)}, f32[512,128]{1,0:T(8,128)S(1)}, u32[]{:S(2)}, u32[]{:S(2)}) collective-permute-start(f32[512,128]{1,0:T(8,128)S(1)} %get-tuple-element.54), channel_id=1, source_target_pairs={{0,1},{1,0},{2,3},{3,2},{4,5},{5,4},{6,7},{7,6},{8,9},{9,8},{10,11... | collective-permute-start | bytes 786440 | tf_op jit(solution)/shard_map/ppermute | solution.py:258
  48.1 8.9 %collective-permute-start.5 = (f32[512,128]{1,0:T(8,128)S(1)}, f32[512,128]{1,0:T(8,128)S(1)}, u32[]{:S(2)}, u32[]{:S(2)}) collective-permute-start(f32[512,128]{1,0:T(8,128)S(1)} %add.20), channel_id=1, source_target_pairs={{0,6},{2,0},{4,2},{6,4},{1,7},{3,1},{5,3},{7,5},{8,14},{10,8},{12,... | collective-permute-start | bytes 786440 | tf_op jit(solution)/shard_map/ppermute | solution.py:276
  57.6 7.3 %collective-permute-start.7 = (f32[256,128]{1,0:T(8,128)S(1)}, f32[256,128]{1,0:T(8,128)S(1)}, u32[]{:S(2)}, u32[]{:S(2)}) collective-permute-start(f32[256,128]{1,0:T(8,128)S(1)} %get-tuple-element.56), channel_id=1, source_target_pairs={{0,8},{8,0},{1,9},{9,1},{2,10},{10,2},{3,11},{11,3},{4,12},{12,4},... | collective-permute-start | bytes 393224 | tf_op jit(solution)/shard_map/ppermute | solution.py:280
  65.7 6.6 %collective-permute-start.8 = (f32[256,128]{1,0:T(8,128)S(1)}, f32[256,128]{1,0:T(8,128)S(1)}, u32[]{:S(2)}, u32[]{:S(2)}) collective-permute-start(f32[256,128]{1,0:T(8,128)S(1)} %residual.1.own_ref), channel_id=1, source_target_pairs={{0,8},{8,0},{1,9},{9,1},{2,10},{10,2},{3,11},{11,3},{4,12},{12,4},... | collective-permute-start | bytes 393224 | tf_op jit(solution)/shard_map/ppermute | solution.py:280
  72.8 4.8 %collective-permute-start.9 = (f32[512,128]{1,0:T(8,128)S(1)}, f32[512,128]{1,0:T(8,128)S(1)}, u32[]{:S(2)}, u32[]{:S(2)}) collective-permute-start(f32[512,128]{1,0:T(8,128)S(1)} %join.1.refs_1_), channel_id=1, source_target_pairs={{0,1},{1,0},{2,3},{3,2},{4,5},{5,4},{6,7},{7,6},{8,9},{9,8},{10,11... | collective-permute-start | bytes 786440 | tf_op jit(solution)/shard_map/ppermute | solution.py:258
  72.9 15.6 %collective-permute-start.10 = (f32[512,128]{1,0:T(8,128)S(1)}, f32[512,128]{1,0:T(8,128)S(1)}, u32[]{:S(2)}, u32[]{:S(2)}) collective-permute-start(f32[512,128]{1,0:T(8,128)S(1)} %join.1.refs_1_), channel_id=1, source_target_pairs={{0,6},{2,0},{4,2},{6,4},{1,7},{3,1},{5,3},{7,5},{8,14},{10,8},{12,... | collective-permute-start | bytes 786440 | tf_op jit(solution)/shard_map/ppermute | solution.py:276
  76.7 11.8 %collective-permute-start.11 = (f32[512,128]{1,0:T(8,128)S(1)}, f32[512,128]{1,0:T(8,128)S(1)}, u32[]{:S(2)}, u32[]{:S(2)}) collective-permute-start(f32[512,128]{1,0:T(8,128)S(1)} %join.1.refs_1_), channel_id=1, source_target_pairs={{0,4},{2,6},{4,0},{6,2},{1,5},{3,7},{5,1},{7,3},{8,12},{10,14},{12... | collective-permute-start | bytes 786440 | tf_op jit(solution)/shard_map/ppermute | solution.py:276
  76.7 15.2 %collective-permute-start.12 = (f32[512,128]{1,0:T(8,128)S(1)}, f32[512,128]{1,0:T(8,128)S(1)}, u32[]{:S(2)}, u32[]{:S(2)}) collective-permute-start(f32[512,128]{1,0:T(8,128)S(1)} %join.1.refs_1_), channel_id=1, source_target_pairs={{0,2},{2,4},{4,6},{6,0},{1,3},{3,5},{5,7},{7,1},{8,10},{10,12},{12... | collective-permute-start | bytes 786440 | tf_op jit(solution)/shard_map/ppermute | solution.py:276
  91.9 1.5 %collective-permute-start.13 = (f32[512,128]{1,0:T(8,128)S(1)}, f32[512,128]{1,0:T(8,128)S(1)}, u32[]{:S(2)}, u32[]{:S(2)}) collective-permute-start(f32[512,128]{1,0:T(8,128)S(1)} %collective-permute-done.12.refs_1_), channel_id=1, source_target_pairs={{0,1},{1,0},{2,3},{3,2},{4,5},{5,4},{6,7},{7,6},{8,9},{9,8},{10,11... | collective-permute-start | bytes 786440 | tf_op jit(solution)/shard_map/ppermute | solution.py:258
  91.9 1.9 %collective-permute-start.14 = (f32[512,128]{1,0:T(8,128)S(1)}, f32[512,128]{1,0:T(8,128)S(1)}, u32[]{:S(2)}, u32[]{:S(2)}) collective-permute-start(f32[512,128]{1,0:T(8,128)S(1)} %collective-permute-done.10.refs_5_), channel_id=1, source_target_pairs={{0,1},{1,0},{2,3},{3,2},{4,5},{5,4},{6,7},{7,6},{8,9},{9,8},{10,11... | collective-permute-start | bytes 786440 | tf_op jit(solution)/shard_map/ppermute | solution.py:258
  92.4 1.8 %collective-permute-start.15 = (f32[512,128]{1,0:T(8,128)S(1)}, f32[512,128]{1,0:T(8,128)S(1)}, u32[]{:S(2)}, u32[]{:S(2)}) collective-permute-start(f32[512,128]{1,0:T(8,128)S(1)} %collective-permute-done.11.refs_9_), channel_id=1, source_target_pairs={{0,1},{1,0},{2,3},{3,2},{4,5},{5,4},{6,7},{7,6},{8,9},{9,8},{10,11... | collective-permute-start | bytes 786440 | tf_op jit(solution)/shard_map/ppermute | solution.py:258
  102.0 21.7 %all-to-all-start = ((f32[8,256,128]{2,1,0:T(8,128)}), f32[8,256,128]{2,1,0:T(8,128)S(1)}, u32[]{:S(2)}, u32[]{:S(2)}) async-start(f32[8,256,128]{2,1,0:T(8,128)} %bitcast.4), calls=%async_computation | async-start | bytes 2097152 | tf_op jit(solution)/shard_map/all_to_all | solution.py:264

commit v2 on v1

--- a/solution.py
+++ b/solution.py
@@ -174,35 +174,18 @@
     )(at, *args)
 
 
-def split_body(at_ref, *refs):
-    *ins, send_ref, keep_ref = refs
-    rows = keep_ref.shape[0]
-    for ref, which in ((send_ref, 1 - at_ref[2]), (keep_ref, at_ref[2])):
-        part = pl.ds(pl.multiple_of(which * rows, rows), rows)
-        total = ins[0][part, :]
-        for x in ins[1:]:
-            total = total + x[part, :]
-        ref[...] = total
-
-
 def residual_body(at_ref, labels_ref, a_ref, b_ref, out_ref):
     logits = a_ref[...] + b_ref[...]
     rows, classes = logits.shape
     groups = rows // LANES
     expo = jnp.exp(logits)
     share = expo / jnp.sum(expo, axis=1, keepdims=True)
-    base = (at_ref[0] * 4 + at_ref[1] * 2 + at_ref[2]) * groups
+    base = (at_ref[0] * 2 + at_ref[1]) * groups
     for g in range(groups):
         label = jnp.broadcast_to(labels_ref[pl.ds(base + g, 1), :], (LANES, LANES)).T
         hot = label == lax.broadcasted_iota(jnp.int32, (LANES, classes), 1)
         part = slice(g * LANES, (g + 1) * LANES)
         out_ref[part, :] = share[part, :] - hot.astype(f32)
-
-
-def join_body(at_ref, own_ref, other_ref, out_ref):
-    rows = own_ref.shape[0]
-    for ref, which in ((own_ref, at_ref[2]), (other_ref, 1 - at_ref[2])):
-        out_ref[pl.ds(pl.multiple_of(which * rows, rows), rows), :] = ref[...]
 
 
 def terms_body(*refs, sets, tile):
@@ -281,37 +264,36 @@
 
 
 def per_device(points, labels, landmarks, coefficients):
-    chips, layers = lax.axis_size("x"), lax.axis_size("zh")
+    chips = lax.axis_size("x")
     classes = coefficients.shape[1]
     block = points.shape[0] // (2 * chips)
-    rows = block // layers
-    at = jnp.stack([lax.axis_index(n) for n in ("x", "core", "zh")]).astype(jnp.int32)
+    at = jnp.stack([lax.axis_index(n) for n in ("x", "core")]).astype(jnp.int32)
     points, landmarks, first_coefs = (
         pltpu.with_memory_space_constraint(x, pltpu.HBM) for x in (points, landmarks, coefficients)
     )
     at, landmarks = lax.optimization_barrier((at, landmarks))
     wide_marks, wide_coefs = prep(landmarks, first_coefs)
-    made, sums, waiting = {}, [], None
-    for shift in (2, 1, 3, 0):
+    made, mine, arrived, sums = {}, {}, {}, []
+    for shift, ready in ((2, ()), (1, (2,)), (3, (1, 3)), (0, ())):
         hi, lo, far, own = kernel_and_logits(at, shift, points, wide_marks, wide_coefs, block)
         made[shift] = hi, lo
-        if waiting is not None:
-            there, mine, arrived = waiting
-            ready = mine + arrived
-            at, ready = lax.optimization_barrier((at, ready))
-            sums.append(along_x(ready, there))
-        waiting = shift, own, swapped(far)
-    sums += waiting[1:]
-    half = jax.ShapeDtypeStruct((rows, classes), f32)
-    send, keep = small_kernel(split_body, at, sums, [half, half], "split")
+        mine[shift], arrived[shift] = own, swapped(far)
+        both = [mine[n] + arrived[n] for n in ready]
+        if both:
+            at, both = lax.optimization_barrier((at, both))
+        sums += [along_x(x, n) for x, n in zip(both, ready)]
+    logits = mine[0] + arrived[0] + sums[0] + sums[1] + sums[2]
+    full = jax.ShapeDtypeStruct((block, classes), f32)
     by_group = labels.reshape(-1, LANES)
-    (resid,) = small_kernel(residual_body, at, [by_group, keep, across_z(send)], [half], "residual")
-    full = jax.ShapeDtypeStruct((block, classes), f32)
-    (own,) = small_kernel(join_body, at, [resid, across_z(resid)], [full], "join")
-    resids = {3: along_x(own, 1), 1: along_x(own, 3), 2: along_x(own, 2)}
+    (own,) = small_kernel(residual_body, at, [by_group, logits, across_z(logits)], [full], "residual")
+    near = {3: along_x(own, 1), 1: along_x(own, 3)}
     local = terms([(swapped(own), own, *made[0])])
-    local, resids = lax.optimization_barrier((local, resids))
-    local = terms([(swapped(resids[n]), resids[n], *made[n]) for n in (3, 1, 2)], local)
+    local, near = lax.optimization_barrier((local, near))
+    front, back = along_x(near[3][: block // 2], 1), along_x(near[1][block // 2 :], 3)
+    local = terms([(swapped(near[n]), near[n], *made[n]) for n in (3, 1)], local)
+    local, front, back = lax.optimization_barrier((local, front, back))
+    last = jnp.concatenate([front, back], axis=0)
+    local = terms([(swapped(last), last, *made[2])], local)
     total_points = labels.shape[0] * lax.axis_size(PTS)
     share = summed_share(local, PTS)
     kept = share.shape[0]

time: 143 us -> 130 us (0.909)
  waiting for transfers between devices: 42.9 us -> 32 us
    ppermute x6 -> x7, waiting for transfers between devices: 18 us -> 5.8 us  [along_x(): lax.ppermute(x, 'x', [(i, (i + shift) % chips) for i in range(chips)])]
    ppermute x2 -> x1, starting transfers between devices: 7.29 us -> 3.96 us  [across_z(): return lax.ppermute(x, 'zh', [(0, 1), (1, 0)])]
    ppermute x6 -> x7, starting transfers between devices: 11.2 us -> 12.8 us  [along_x(): lax.ppermute(x, 'x', [(i, (i + shift) % chips) for i in range(chips)])]
    pallas_call x2 -> x3, Pallas kernels: 10.3 us -> 10.6 us  [terms(): pl.pallas_call(functools.partial(terms_body, sets=len(sets), tile=tile),...]
    ppermute x2 -> x1, waiting for transfers between devices: 6.6 us -> 6.61 us  [across_z(): return lax.ppermute(x, 'zh', [(0, 1), (1, 0)])]
  transfers between devices with their start and end apart: 17 -> 17, of which waited for: 9 -> 6; matrix products, arithmetic and copies ran while one was open for 0% -> 0% of each run, Pallas kernels for 23% -> 28%
where the time goes in v2:
time: 130 us
  Pallas kernels  54.5 us (42%)
  waiting for transfers between devices  32 us (25%)
  starting transfers between devices  23.7 us (18%)
  blocking collectives  17.3 us (13%)
    pallas_call x4, Pallas kernels, kernel_and_logits(): pl.pallas_call(functools.partial(logits_body, tile=tile), grid_spec=pltpu...  39.6 us
    all_to_all x1, blocking collectives, all_shares(): lax.all_to_all(copies, axes, split_axis=0, concat_axis=0, tiled=True)  17.3 us
    all_to_all x1, waiting for transfers between devices, summed_share(): lax.all_to_all(parts, axes, split_axis=0, concat_axis=0, tiled=True)  16.5 us
    ppermute x7, starting transfers between devices, along_x(): lax.ppermute(x, 'x', [(i, (i + shift) % chips) for i in range(chips)])  12.8 us
    pallas_call x3, Pallas kernels, terms(): pl.pallas_call(functools.partial(terms_body, sets=len(sets), tile=tile),...  10.6 us
    ppermute x1, waiting for transfers between devices, across_z(): return lax.ppermute(x, 'zh', [(0, 1), (1, 0)])  6.61 us
    ppermute x7, waiting for transfers between devices, along_x(): lax.ppermute(x, 'x', [(i, (i + shift) % chips) for i in range(chips)])  5.8 us
    all_to_all x1, starting transfers between devices, summed_share(): lax.all_to_all(parts, axes, split_axis=0, concat_axis=0, tiled=True)  5.19 us
  transfers between devices with their start and end apart: 17, of which 6 were waited for; matrix products, arithmetic and copies ran while one was open for 0% of the time, Pallas kernels for 28%

profile of v2, /device:TPU:0, one launch (start us, length us, event | category | flops | bytes accessed | tf_op | source)
XLA Modules:
  0.0 129.9 jit_solution(4356179283361849039)
XLA Ops:
  0.1 3.5 %prep.1 = (bf16[2048,1280]{1,0:T(8,128)(2,1)S(1)}, bf16[2048,256]{1,0:T(8,128)(2,1)S(1)}) custom-call(f32[2048,384]{1,0:T(8,128)} %l_ref, f32[2048,128]{1,0:T(8,128)} %c_ref.1), custom_call_target="tpu_custom_call" | custom-call | tf_op jit(solution)/shard_map/prep/pallas_call | solution.py:65
  3.5 9.9 %kernel_and_logits.4 = (bf16[1024,2048]{1,0:T(8,128)(2,1)S(1)}, bf16[1024,2048]{1,0:T(8,128)(2,1)S(1)}, f32[512,128]{1,0:T(8,128)S(1)}, f32[512,128]{1,0:T(8,128)S(1)}) custom-call(s32[2]{0:T(128)S(1)} %pad_add_fusion.at_ref, f32[4096,384]{1,0:T(8,128)} %p_ref.7, bf16[2048,1280]{1,0:T(8,128)(2,1)S(1)} %get-tuple-element.38.b_ref, ...), custom_call_target="tpu_custom_call" | custom-call | flops 7516192768 | bytes 16777216 | tf_op jit(solution)/shard_map/kernel_and_logits/pallas_call | solution.py:124
  13.5 9.9 %kernel_and_logits.5 = (bf16[1024,2048]{1,0:T(8,128)(2,1)S(1)}, bf16[1024,2048]{1,0:T(8,128)(2,1)S(1)}, f32[512,128]{1,0:T(8,128)S(1)}, f32[512,128]{1,0:T(8,128)S(1)}) custom-call(s32[2]{0:T(128)S(1)} %pad_add_fusion.at_ref, f32[4096,384]{1,0:T(8,128)} %p_ref.7, bf16[2048,1280]{1,0:T(8,128)(2,1)S(1)} %get-tuple-element.38.b_ref, ...), custom_call_target="tpu_custom_call" | custom-call | flops 7516192768 | bytes 16777216 | tf_op jit(solution)/shard_map/kernel_and_logits/pallas_call | solution.py:124
  24.1 9.9 %kernel_and_logits.6 = (bf16[1024,2048]{1,0:T(8,128)(2,1)S(1)}, bf16[1024,2048]{1,0:T(8,128)(2,1)S(1)}, f32[512,128]{1,0:T(8,128)S(1)}, f32[512,128]{1,0:T(8,128)S(1)}) custom-call(s32[2]{0:T(128)S(1)} %pad_add_fusion.at_ref, f32[4096,384]{1,0:T(8,128)} %p_ref.7, bf16[2048,1280]{1,0:T(8,128)(2,1)S(1)} %get-tuple-element.38.b_ref, ...), custom_call_target="tpu_custom_call" | custom-call | flops 7516192768 | bytes 16777216 | tf_op jit(solution)/shard_map/kernel_and_logits/pallas_call | solution.py:124
  34.1 3.2 %collective-permute-start.4 = (f32[512,128]{1,0:T(8,128)S(1)}, f32[512,128]{1,0:T(8,128)S(1)}, u32[]{:S(2)}, u32[]{:S(2)}) collective-permute-start(f32[512,128]{1,0:T(8,128)S(1)} %add.30), channel_id=1, source_target_pairs={{0,4},{2,6},{4,0},{6,2},{1,5},{3,7},{5,1},{7,3},{8,12},{10,14},{12... | collective-permute-start | bytes 786440 | tf_op jit(solution)/shard_map/ppermute | solution.py:259
  38.0 2.6 %collective-permute-start.6 = (f32[512,128]{1,0:T(8,128)S(1)}, f32[512,128]{1,0:T(8,128)S(1)}, u32[]{:S(2)}, u32[]{:S(2)}) collective-permute-start(f32[512,128]{1,0:T(8,128)S(1)} %add.32), channel_id=1, source_target_pairs={{0,6},{2,0},{4,2},{6,4},{1,7},{3,1},{5,3},{7,5},{8,14},{10,8},{12,... | collective-permute-start | bytes 786440 | tf_op jit(solution)/shard_map/ppermute | solution.py:259
  40.7 9.9 %kernel_and_logits.7 = (bf16[1024,2048]{1,0:T(8,128)(2,1)S(1)}, bf16[1024,2048]{1,0:T(8,128)(2,1)S(1)}, f32[512,128]{1,0:T(8,128)S(1)}, f32[512,128]{1,0:T(8,128)S(1)}) custom-call(s32[2]{0:T(128)S(1)} %pad_add_fusion.at_ref, f32[4096,384]{1,0:T(8,128)} %p_ref.7, bf16[2048,1280]{1,0:T(8,128)(2,1)S(1)} %get-tuple-element.38.b_ref, ...), custom_call_target="tpu_custom_call" | custom-call | flops 7516192768 | bytes 16777216 | tf_op jit(solution)/shard_map/kernel_and_logits/pallas_call | solution.py:124
  50.7 1.5 %collective-permute-done.3 = f32[512,128]{1,0:T(8,128)S(1)} collective-permute-done((f32[512,128]{1,0:T(8,128)S(1)}, f32[512,128]{1,0:T(8,128)S(1)}, u32[]{:S(2)}, u32[]{:S(2)}) %collective-permute-start.3) | collective-permute-done | bytes 262176 | tf_op jit(solution)/shard_map/ppermute | solution.py:241
  52.3 4.0 %collective-permute-start.7 = (f32[512,128]{1,0:T(8,128)S(1)}, f32[512,128]{1,0:T(8,128)S(1)}, u32[]{:S(2)}, u32[]{:S(2)}) collective-permute-start(f32[512,128]{1,0:T(8,128)S(1)} %add_add_fusion.a_ref), channel_id=1, source_target_pairs={{0,8},{8,0},{1,9},{9,1},{2,10},{10,2},{3,11},{11,3},{4,12},{12,4},... | collective-permute-start | bytes 786440 | tf_op jit(solution)/shard_map/ppermute | solution.py:263
  56.2 6.6 %collective-permute-done.7.b_ref = f32[512,128]{1,0:T(8,128)S(1)} collective-permute-done((f32[512,128]{1,0:T(8,128)S(1)}, f32[512,128]{1,0:T(8,128)S(1)}, u32[]{:S(2)}, u32[]{:S(2)}) %collective-permute-start.7) | collective-permute-done | bytes 262176 | tf_op jit(solution)/shard_map/ppermute | solution.py:263
  62.8 0.8 residual.1.refs_1_
  63.8 3.2 %collective-permute-start.9 = (f32[512,128]{1,0:T(8,128)S(1)}, f32[512,128]{1,0:T(8,128)S(1)}, u32[]{:S(2)}, u32[]{:S(2)}) collective-permute-start(f32[512,128]{1,0:T(8,128)S(1)} %residual.1.refs_1_), channel_id=1, source_target_pairs={{0,6},{2,0},{4,2},{6,4},{1,7},{3,1},{5,3},{7,5},{8,14},{10,8},{12,... | collective-permute-start | bytes 786440 | tf_op jit(solution)/shard_map/ppermute | solution.py:259
  67.0 2.5 %terms.3.refs_8_ = f32[2048,128]{1,0:T(8,128)S(1)} custom-call(f32[512,128]{1,0:T(8,128)S(1)} %collective-permute-done.8.refs_0_, f32[512,128]{1,0:T(8,128)S(1)} %residual.1.refs_1_, bf16[1024,2048]{1,0:T(8,128)(2,1)S(1)} %get-tuple-element.53.refs_2_, bf16[1024,2048]{1,0:T(8,128)(2,1)S(1)} %get-tuple-element.54.refs_3_), custom_call_target="tpu_custom_call" | custom-call | flops 2147483648 | bytes 11010048 | tf_op jit(solution)/shard_map/terms/pallas_call | solution.py:224
  69.5 4.1 %collective-permute-done.10.refs_1_ = f32[512,128]{1,0:T(8,128)S(1)} collective-permute-done((f32[512,128]{1,0:T(8,128)S(1)}, f32[512,128]{1,0:T(8,128)S(1)}, u32[]{:S(2)}, u32[]{:S(2)}) %collective-permute-start.10) | collective-permute-done | bytes 262176 | tf_op jit(solution)/shard_map/ppermute | solution.py:259
  74.2 3.0 %collective-permute-start.14 = (f32[256,128]{1,0:T(8,128)S(1)}, f32[256,128]{1,0:T(8,128)S(1)}, u32[]{:S(2)}, u32[]{:S(2)}) collective-permute-start(f32[256,128]{1,0:T(8,128)S(1)} %slice.7), channel_id=1, source_target_pairs={{0,6},{2,0},{4,2},{6,4},{1,7},{3,1},{5,3},{7,5},{8,14},{10,8},{12,... | collective-permute-start | bytes 393224 | tf_op jit(solution)/shard_map/ppermute | solution.py:259
  77.2 4.6 %terms.4.refs_4_ = f32[2048,128]{1,0:T(8,128)S(1)} custom-call(f32[512,128]{1,0:T(8,128)S(1)} %collective-permute-done.11.refs_0_, f32[512,128]{1,0:T(8,128)S(1)} %collective-permute-done.10.refs_1_, bf16[1024,2048]{1,0:T(8,128)(2,1)S(1)} %get-tuple-element.56.refs_2_, bf16[1024,2048]{1,0:T(8,128)(2,1)S(1)} %get-tuple-element.57.refs_3_, ...), custom_call_target="tpu_custom_call" | custom-call | flops 4294967296 | bytes 19922944 | tf_op jit(solution)/shard_map/terms/pallas_call | solution.py:224
  81.9 1.7 %collective-permute-done.13 = f32[256,128]{1,0:T(8,128)S(1)} collective-permute-done((f32[256,128]{1,0:T(8,128)S(1)}, f32[256,128]{1,0:T(8,128)S(1)}, u32[]{:S(2)}, u32[]{:S(2)}) %collective-permute-start.13) | collective-permute-done | bytes 131104 | tf_op jit(solution)/shard_map/ppermute | solution.py:259
  83.9 1.5 %collective-permute-done.15.refs_0_ = f32[512,128]{1,0:T(8,128)S(1)} collective-permute-done((f32[512,128]{1,0:T(8,128)S(1)}, f32[512,128]{1,0:T(8,128)S(1)}, u32[]{:S(2)}, u32[]{:S(2)}) %collective-permute-start.15) | collective-permute-done | bytes 262176 | tf_op jit(solution)/shard_map/ppermute | solution.py:241
  85.4 3.5 %terms.5 = f32[2048,128]{1,0:T(8,128)} custom-call(f32[512,128]{1,0:T(8,128)S(1)} %collective-permute-done.15.refs_0_, f32[512,128]{1,0:T(8,128)S(1)} %constant_dynamic-update-slice_fusion.refs_1_, bf16[1024,2048]{1,0:T(8,128)(2,1)S(1)} %get-tuple-element.64.refs_2_, bf16[1024,2048]{1,0:T(8,128)(2,1)S(1)} %get-tuple-element.65.refs_3_, ...), custom_call_target="tpu_custom_call" | custom-call | flops 2147483648 | bytes 11010048 | tf_op jit(solution)/shard_map/terms/pallas_call | solution.py:224
  88.9 5.2 %all-to-all-start = ((f32[8,256,128]{2,1,0:T(8,128)}), f32[8,256,128]{2,1,0:T(8,128)S(1)}, u32[]{:S(2)}, u32[]{:S(2)}) async-start(f32[8,256,128]{2,1,0:T(8,128)} %bitcast.3), calls=%async_computation | async-start | bytes 2097152 | tf_op jit(solution)/shard_map/all_to_all | solution.py:247
  94.1 16.5 %all-to-all-done = f32[8,256,128]{2,1,0:T(8,128)S(1)} async-done(((f32[8,256,128]{2,1,0:T(8,128)}), f32[8,256,128]{2,1,0:T(8,128)S(1)}, u32[]{:S(2)}, u32[]{:S(2)}) %all-to-all-start) | async-done | bytes 1048608 | tf_op jit(solution)/shard_map/all_to_all | solution.py:247
  110.6 0.9 multiply_add_fusion
  111.7 17.3 %all_to_all.10 = f32[8,256,128]{2,1,0:T(8,128)S(1)} all-to-all(f32[8,256,128]{2,1,0:T(8,128)S(1)} %broadcast_in_dim.3), channel_id=1, replica_groups=mesh['y'=4,'zl'=2,'zh'=2,'x'=4,'core'=2] {'y','zl'}, dimensions={0} | all-to-all | bytes 2097152 | tf_op jit(solution)/shard_map/all_to_all | solution.py:253
  128.9 1.0 copy.7
  (35 shorter events, 2.9 us)
Async XLA Ops:
  13.5 10.6 %collective-permute-start = (f32[512,128]{1,0:T(8,128)S(1)}, f32[512,128]{1,0:T(8,128)S(1)}, u32[]{:S(2)}, u32[]{:S(2)}) collective-permute-start(f32[512,128]{1,0:T(8,128)S(1)} %get-tuple-element.41), channel_id=1, source_target_pairs={{0,1},{1,0},{2,3},{3,2},{4,5},{5,4},{6,7},{7,6},{8,9},{9,8},{10,11... | collective-permute-start | bytes 786440 | tf_op jit(solution)/shard_map/ppermute | solution.py:241
  23.5 13.8 %collective-permute-start.1 = (f32[512,128]{1,0:T(8,128)S(1)}, f32[512,128]{1,0:T(8,128)S(1)}, u32[]{:S(2)}, u32[]{:S(2)}) collective-permute-start(f32[512,128]{1,0:T(8,128)S(1)} %get-tuple-element.44), channel_id=1, source_target_pairs={{0,1},{1,0},{2,3},{3,2},{4,5},{5,4},{6,7},{7,6},{8,9},{9,8},{10,11... | collective-permute-start | bytes 786440 | tf_op jit(solution)/shard_map/ppermute | solution.py:241
  34.0 3.3 %collective-permute-start.2 = (f32[512,128]{1,0:T(8,128)S(1)}, f32[512,128]{1,0:T(8,128)S(1)}, u32[]{:S(2)}, u32[]{:S(2)}) collective-permute-start(f32[512,128]{1,0:T(8,128)S(1)} %get-tuple-element.46), channel_id=1, source_target_pairs={{0,1},{1,0},{2,3},{3,2},{4,5},{5,4},{6,7},{7,6},{8,9},{9,8},{10,11... | collective-permute-start | bytes 786440 | tf_op jit(solution)/shard_map/ppermute | solution.py:241
  34.1 16.6 %collective-permute-start.4 = (f32[512,128]{1,0:T(8,128)S(1)}, f32[512,128]{1,0:T(8,128)S(1)}, u32[]{:S(2)}, u32[]{:S(2)}) collective-permute-start(f32[512,128]{1,0:T(8,128)S(1)} %add.30), channel_id=1, source_target_pairs={{0,4},{2,6},{4,0},{6,2},{1,5},{3,7},{5,1},{7,3},{8,12},{10,14},{12... | collective-permute-start | bytes 786440 | tf_op jit(solution)/shard_map/ppermute | solution.py:259
  37.4 25.5 %copy-start = (s32[4096]{0:T(1024)S(1)}, s32[4096]{0:T(1024)}, u32[]{:S(2)}) copy-start(s32[4096]{0:T(1024)} %param.5) | copy-start | bytes 49156
  37.4 13.3 %collective-permute-start.5 = (f32[512,128]{1,0:T(8,128)S(1)}, f32[512,128]{1,0:T(8,128)S(1)}, u32[]{:S(2)}, u32[]{:S(2)}) collective-permute-start(f32[512,128]{1,0:T(8,128)S(1)} %add.31), channel_id=1, source_target_pairs={{0,2},{2,4},{4,6},{6,0},{1,3},{3,5},{5,7},{7,1},{8,10},{10,12},{12... | collective-permute-start | bytes 786440 | tf_op jit(solution)/shard_map/ppermute | solution.py:259
  38.0 12.7 %collective-permute-start.6 = (f32[512,128]{1,0:T(8,128)S(1)}, f32[512,128]{1,0:T(8,128)S(1)}, u32[]{:S(2)}, u32[]{:S(2)}) collective-permute-start(f32[512,128]{1,0:T(8,128)S(1)} %add.32), channel_id=1, source_target_pairs={{0,6},{2,0},{4,2},{6,4},{1,7},{3,1},{5,3},{7,5},{8,14},{10,8},{12,... | collective-permute-start | bytes 786440 | tf_op jit(solution)/shard_map/ppermute | solution.py:259
  50.6 1.6 %collective-permute-start.3 = (f32[512,128]{1,0:T(8,128)S(1)}, f32[512,128]{1,0:T(8,128)S(1)}, u32[]{:S(2)}, u32[]{:S(2)}) collective-permute-start(f32[512,128]{1,0:T(8,128)S(1)} %get-tuple-element.49), channel_id=1, source_target_pairs={{0,1},{1,0},{2,3},{3,2},{4,5},{5,4},{6,7},{7,6},{8,9},{9,8},{10,11... | collective-permute-start | bytes 786440 | tf_op jit(solution)/shard_map/ppermute | solution.py:241
  52.3 10.6 %collective-permute-start.7 = (f32[512,128]{1,0:T(8,128)S(1)}, f32[512,128]{1,0:T(8,128)S(1)}, u32[]{:S(2)}, u32[]{:S(2)}) collective-permute-start(f32[512,128]{1,0:T(8,128)S(1)} %add_add_fusion.a_ref), channel_id=1, source_target_pairs={{0,8},{8,0},{1,9},{9,1},{2,10},{10,2},{3,11},{11,3},{4,12},{12,4},... | collective-permute-start | bytes 786440 | tf_op jit(solution)/shard_map/ppermute | solution.py:263
  63.6 3.4 %collective-permute-start.8 = (f32[512,128]{1,0:T(8,128)S(1)}, f32[512,128]{1,0:T(8,128)S(1)}, u32[]{:S(2)}, u32[]{:S(2)}) collective-permute-start(f32[512,128]{1,0:T(8,128)S(1)} %residual.1.refs_1_), channel_id=1, source_target_pairs={{0,1},{1,0},{2,3},{3,2},{4,5},{5,4},{6,7},{7,6},{8,9},{9,8},{10,11... | collective-permute-start | bytes 786440 | tf_op jit(solution)/shard_map/ppermute | solution.py:241
  63.7 9.9 %collective-permute-start.10 = (f32[512,128]{1,0:T(8,128)S(1)}, f32[512,128]{1,0:T(8,128)S(1)}, u32[]{:S(2)}, u32[]{:S(2)}) collective-permute-start(f32[512,128]{1,0:T(8,128)S(1)} %residual.1.refs_1_), channel_id=1, source_target_pairs={{0,2},{2,4},{4,6},{6,0},{1,3},{3,5},{5,7},{7,1},{8,10},{10,12},{12... | collective-permute-start | bytes 786440 | tf_op jit(solution)/shard_map/ppermute | solution.py:259
  63.8 9.9 %collective-permute-start.9 = (f32[512,128]{1,0:T(8,128)S(1)}, f32[512,128]{1,0:T(8,128)S(1)}, u32[]{:S(2)}, u32[]{:S(2)}) collective-permute-start(f32[512,128]{1,0:T(8,128)S(1)} %residual.1.refs_1_), channel_id=1, source_target_pairs={{0,6},{2,0},{4,2},{6,4},{1,7},{3,1},{5,3},{7,5},{8,14},{10,8},{12,... | collective-permute-start | bytes 786440 | tf_op jit(solution)/shard_map/ppermute | solution.py:259
  73.6 3.6 %collective-permute-start.11 = (f32[512,128]{1,0:T(8,128)S(1)}, f32[512,128]{1,0:T(8,128)S(1)}, u32[]{:S(2)}, u32[]{:S(2)}) collective-permute-start(f32[512,128]{1,0:T(8,128)S(1)} %collective-permute-done.10.refs_1_), channel_id=1, source_target_pairs={{0,1},{1,0},{2,3},{3,2},{4,5},{5,4},{6,7},{7,6},{8,9},{9,8},{10,11... | collective-permute-start | bytes 786440 | tf_op jit(solution)/shard_map/ppermute | solution.py:241
  73.7 3.6 %collective-permute-start.12 = (f32[512,128]{1,0:T(8,128)S(1)}, f32[512,128]{1,0:T(8,128)S(1)}, u32[]{:S(2)}, u32[]{:S(2)}) collective-permute-start(f32[512,128]{1,0:T(8,128)S(1)} %collective-permute-done.9.refs_5_), channel_id=1, source_target_pairs={{0,1},{1,0},{2,3},{3,2},{4,5},{5,4},{6,7},{7,6},{8,9},{9,8},{10,11... | collective-permute-start | bytes 786440 | tf_op jit(solution)/shard_map/ppermute | solution.py:241
  74.2 7.7 %collective-permute-start.14 = (f32[256,128]{1,0:T(8,128)S(1)}, f32[256,128]{1,0:T(8,128)S(1)}, u32[]{:S(2)}, u32[]{:S(2)}) collective-permute-start(f32[256,128]{1,0:T(8,128)S(1)} %slice.7), channel_id=1, source_target_pairs={{0,6},{2,0},{4,2},{6,4},{1,7},{3,1},{5,3},{7,5},{8,14},{10,8},{12,... | collective-permute-start | bytes 393224 | tf_op jit(solution)/shard_map/ppermute | solution.py:259
  77.2 6.3 %collective-permute-start.13 = (f32[256,128]{1,0:T(8,128)S(1)}, f32[256,128]{1,0:T(8,128)S(1)}, u32[]{:S(2)}, u32[]{:S(2)}) collective-permute-start(f32[256,128]{1,0:T(8,128)S(1)} %slice.6), channel_id=1, source_target_pairs={{0,2},{2,4},{4,6},{6,0},{1,3},{3,5},{5,7},{7,1},{8,10},{10,12},{12... | collective-permute-start | bytes 393224 | tf_op jit(solution)/shard_map/ppermute | solution.py:259
  83.6 1.8 %collective-permute-start.15 = (f32[512,128]{1,0:T(8,128)S(1)}, f32[512,128]{1,0:T(8,128)S(1)}, u32[]{:S(2)}, u32[]{:S(2)}) collective-permute-start(f32[512,128]{1,0:T(8,128)S(1)} %constant_dynamic-update-slice_fusion.refs_1_), channel_id=1, source_target_pairs={{0,1},{1,0},{2,3},{3,2},{4,5},{5,4},{6,7},{7,6},{8,9},{9,8},{10,11... | collective-permute-start | bytes 786440 | tf_op jit(solution)/shard_map/ppermute | solution.py:241
  88.9 21.7 %all-to-all-start = ((f32[8,256,128]{2,1,0:T(8,128)}), f32[8,256,128]{2,1,0:T(8,128)S(1)}, u32[]{:S(2)}, u32[]{:S(2)}) async-start(f32[8,256,128]{2,1,0:T(8,128)} %bitcast.3), calls=%async_computation | async-start | bytes 2097152 | tf_op jit(solution)/shard_map/all_to_all | solution.py:247

commit v3 on v2

--- a/solution.py
+++ b/solution.py
@@ -11,7 +11,7 @@
 
 LOSS_SCALE = 8192.0
 RIDGE = 0.5
-LIMIT_K1, LIMIT_K2 = 9, 9
+LIMIT_K1, LIMIT_K2 = 8, 6
 LANES = 128
 AXES = ("y", "zl", "zh", "x", "core")
 PTS = ("y", "zl")
@@ -43,7 +43,20 @@
     return out.astype(bf16)
 
 
-def prep_body(l_ref, c_ref, b_ref, cc_ref):
+def fetched(at_ref, shift, points_ref, next_ref, sem):
+    rows = next_ref.shape[0]
+    chips = points_ref.shape[0] // rows
+    first = pl.multiple_of(lax.rem(at_ref[0] + shift, chips) * rows, rows)
+    return pltpu.make_async_copy(points_ref.at[pl.ds(first, rows), :], next_ref, sem)
+
+
+def prep_body(at_ref, l_ref, c_ref, points_ref, b_ref, cc_ref, next_ref, sem, *, shift):
+    copy = fetched(at_ref, shift, points_ref, next_ref, sem)
+
+    @pl.when(pl.program_id(0) == 0)
+    def _():
+        copy.start()
+
     rows, feats = l_ref.shape
     unit = math.log2(math.e) / feats
     mark = l_ref[...]
@@ -57,32 +70,53 @@
     cc_ref[:, : high.shape[1]] = high
     cc_ref[:, high.shape[1] :] = low
 
-
-def prep(landmarks, coefficients, block=512):
+    @pl.when(pl.program_id(0) == pl.num_programs(0) - 1)
+    def _():
+        copy.wait()
+
+
+def prep(at, shift, landmarks, coefficients, points, held_rows, block=512):
     marks, feats = landmarks.shape
     classes = coefficients.shape[1]
     wide = 3 * feats + LANES
     return pl.pallas_call(
-        prep_body,
-        grid=(marks // block,),
-        in_specs=[
-            pl.BlockSpec((block, feats), lambda i: (i, 0)),
-            pl.BlockSpec((block, classes), lambda i: (i, 0)),
-        ],
-        out_specs=[
-            pl.BlockSpec((block, wide), lambda i: (i, 0)),
-            pl.BlockSpec((block, 2 * classes), lambda i: (i, 0)),
-        ],
+        functools.partial(prep_body, shift=shift),
+        grid_spec=pltpu.PrefetchScalarGridSpec(
+            num_scalar_prefetch=1,
+            grid=(marks // block,),
+            in_specs=[
+                pl.BlockSpec((block, feats), lambda i, s: (i, 0)),
+                pl.BlockSpec((block, classes), lambda i, s: (i, 0)),
+                pl.BlockSpec(memory_space=pl.ANY),
+            ],
+            out_specs=[
+                pl.BlockSpec((block, wide), lambda i, s: (i, 0)),
+                pl.BlockSpec((block, 2 * classes), lambda i, s: (i, 0)),
+                pl.BlockSpec((held_rows, feats), lambda i, s: (0, 0)),
+            ],
+            scratch_shapes=[pltpu.SemaphoreType.DMA(())],
+        ),
         out_shape=[
             pltpu.VMEM((marks, wide), bf16),
             pltpu.VMEM((marks, 2 * classes), bf16),
+            pltpu.VMEM((held_rows, feats), f32),
         ],
-        compiler_params=pltpu.CompilerParams(vmem_limit_bytes=12 << 20),
+        compiler_params=pltpu.CompilerParams(vmem_limit_bytes=8 << 20),
         name="prep",
-    )(landmarks, coefficients)
-
-
-def logits_body(at_ref, p_ref, b_ref, c_ref, hi_ref, lo_ref, far_ref, own_ref, a_ref, *, tile):
+    )(at, landmarks, coefficients, points)
+
+
+def logits_body(at_ref, p_ref, b_ref, c_ref, *refs, tile, later):
+    if later is None:
+        hi_ref, lo_ref, far_ref, own_ref, a_ref = refs
+    else:
+        points_ref, hi_ref, lo_ref, far_ref, own_ref, next_ref, a_ref, sem = refs
+        copy = fetched(at_ref, later, points_ref, next_ref, sem)
+
+        @pl.when(pl.program_id(0) == 0)
+        def _():
+            copy.start()
+
     rows, feats = p_ref.shape
     marks = b_ref.shape[0]
     unit = math.log2(math.e) / feats
@@ -113,49 +147,55 @@
     @pl.when(pl.program_id(0) == 1)
     def _():
         own_ref[...] = jnp.concatenate(sums, axis=0)
-
-
-def kernel_and_logits(at, shift, points, wide_marks, wide_coefs, block, tile=512):
-    feats = points.shape[1]
+        if later is not None:
+            copy.wait()
+
+
+def kernel_and_logits(at, held, wide_marks, wide_coefs, points, later, tile=512):
+    rows, feats = held.shape
+    block = rows // 2
     marks, wide = wide_marks.shape
     classes = wide_coefs.shape[1] // 2
-    chips = points.shape[0] // (2 * block)
     fixed = pl.Buffered(1)
-    return pl.pallas_call(
-        functools.partial(logits_body, tile=tile),
+    fetch = later is not None
+    return pl.pallas_call(
+        functools.partial(logits_body, tile=tile, later=later),
         grid_spec=pltpu.PrefetchScalarGridSpec(
             num_scalar_prefetch=1,
             grid=(2,),
             in_specs=[
-                pl.BlockSpec(
-                    (block, feats),
-                    lambda i, s: (lax.rem(s[0] + shift, chips) * 2 + lax.rem(s[1] + 1 + i, 2), 0),
-                ),
+                pl.BlockSpec((block, feats), lambda i, s: (lax.rem(s[1] + 1 + i, 2), 0)),
                 pl.BlockSpec((marks, wide), lambda i, s: (0, 0), pipeline_mode=fixed),
                 pl.BlockSpec((marks, 2 * classes), lambda i, s: (0, 0), pipeline_mode=fixed),
+                *[pl.BlockSpec(memory_space=pl.ANY)] * fetch,
             ],
             out_specs=[
                 pl.BlockSpec((block, marks), lambda i, s: (i, 0)),
                 pl.BlockSpec((block, marks), lambda i, s: (i, 0)),
                 pl.BlockSpec((block, classes), lambda i, s: (0, 0)),
                 pl.BlockSpec((block, classes), lambda i, s: (0, 0)),
-            ],
-            scratch_shapes=[pltpu.VMEM((block, wide), bf16)],
+                *[pl.BlockSpec((rows, feats), lambda i, s: (0, 0))] * fetch,
+            ],
+            scratch_shapes=[
+                pltpu.VMEM((block, wide), bf16),
+                *[pltpu.SemaphoreType.DMA(())] * fetch,
+            ],
         ),
         out_shape=[
-            pltpu.VMEM((2 * block, marks), bf16),
-            pltpu.VMEM((2 * block, marks), bf16),
+            pltpu.VMEM((rows, marks), bf16),
+            pltpu.VMEM((rows, marks), bf16),
             pltpu.VMEM((block, classes), f32),
             pltpu.VMEM((block, classes), f32),
+            *[pltpu.VMEM((rows, feats), f32)] * fetch,
         ],
         compiler_params=pltpu.CompilerParams(vmem_limit_bytes=LIMIT_K1 << 20),
         cost_estimate=pl.CostEstimate(
-            flops=4 * block * marks * (wide + 4 * classes),
-            bytes_accessed=8 * block * (feats + marks + classes) + 2 * marks * (wide + 2 * classes),
-            transcendentals=2 * block * marks,
+            flops=2 * rows * marks * (wide + 4 * classes),
+            bytes_accessed=4 * rows * (feats + marks + classes) + 2 * marks * (wide + 2 * classes),
+            transcendentals=rows * marks,
         ),
         name="kernel_and_logits",
-    )(at, points, wide_marks, wide_coefs)
+    )(at, held, wide_marks, wide_coefs, *[points] * fetch)
 
 
 def small_kernel(body, at, args, outs, name):
@@ -172,6 +212,27 @@
         compiler_params=pltpu.CompilerParams(vmem_limit_bytes=6 << 20),
         name=name,
     )(at, *args)
+
+
+def ridge_body(at_ref, c_ref, out_ref):
+    out_ref[...] = RIDGE * c_ref[...]
+
+
+def own_ridge(at, coefficients):
+    marks, classes = coefficients.shape
+    kept = marks // lax.axis_size(PTS)
+    return pl.pallas_call(
+        ridge_body,
+        grid_spec=pltpu.PrefetchScalarGridSpec(
+            num_scalar_prefetch=1,
+            grid=(1,),
+            in_specs=[pl.BlockSpec((kept, classes), lambda i, s: (s[2], 0))],
+            out_specs=pl.BlockSpec((kept, classes), lambda i, s: (0, 0)),
+        ),
+        out_shape=pltpu.VMEM((kept, classes), f32),
+        compiler_params=pltpu.CompilerParams(vmem_limit_bytes=2 << 20),
+        name="ridge",
+    )(at, pltpu.with_memory_space_constraint(coefficients, pltpu.HBM))
 
 
 def residual_body(at_ref, labels_ref, a_ref, b_ref, out_ref):
@@ -267,15 +328,16 @@
     chips = lax.axis_size("x")
     classes = coefficients.shape[1]
     block = points.shape[0] // (2 * chips)
-    at = jnp.stack([lax.axis_index(n) for n in ("x", "core")]).astype(jnp.int32)
+    at = jnp.stack([lax.axis_index(n) for n in ("x", "core", PTS)]).astype(jnp.int32)
     points, landmarks, first_coefs = (
         pltpu.with_memory_space_constraint(x, pltpu.HBM) for x in (points, landmarks, coefficients)
     )
     at, landmarks = lax.optimization_barrier((at, landmarks))
-    wide_marks, wide_coefs = prep(landmarks, first_coefs)
+    wide_marks, wide_coefs, held = prep(at, 2, landmarks, first_coefs, points, 2 * block)
     made, mine, arrived, sums = {}, {}, {}, []
-    for shift, ready in ((2, ()), (1, (2,)), (3, (1, 3)), (0, ())):
-        hi, lo, far, own = kernel_and_logits(at, shift, points, wide_marks, wide_coefs, block)
+    for shift, later, ready in ((2, 1, ()), (1, 3, (2,)), (3, 0, (1, 3)), (0, None, ())):
+        hi, lo, far, own, *after = kernel_and_logits(at, held, wide_marks, wide_coefs, points, later)
+        held = after[0] if after else None
         made[shift] = hi, lo
         mine[shift], arrived[shift] = own, swapped(far)
         both = [mine[n] + arrived[n] for n in ready]
@@ -288,7 +350,9 @@
     (own,) = small_kernel(residual_body, at, [by_group, logits, across_z(logits)], [full], "residual")
     near = {3: along_x(own, 1), 1: along_x(own, 3)}
     local = terms([(swapped(own), own, *made[0])])
-    local, near = lax.optimization_barrier((local, near))
+    at, local = lax.optimization_barrier((at, local))
+    ridge = own_ridge(at, coefficients)
+    local, near, ridge = lax.optimization_barrier((local, near, ridge))
     front, back = along_x(near[3][: block // 2], 1), along_x(near[1][block // 2 :], 3)
     local = terms([(swapped(near[n]), near[n], *made[n]) for n in (3, 1)], local)
     local, front, back = lax.optimization_barrier((local, front, back))
@@ -296,9 +360,7 @@
     local = terms([(swapped(last), last, *made[2])], local)
     total_points = labels.shape[0] * lax.axis_size(PTS)
     share = summed_share(local, PTS)
-    kept = share.shape[0]
-    own_coefs = lax.dynamic_slice_in_dim(coefficients, lax.axis_index(PTS) * kept, kept, 0)
-    return all_shares(share * (LOSS_SCALE / total_points) + RIDGE * own_coefs, PTS)
+    return all_shares(share * (LOSS_SCALE / total_points) + ridge, PTS)
 
 
 def solution(mesh):

time: 130 us -> 125 us (0.962)
  blocking collectives: 17.3 us -> 38.3 us
  waiting for transfers between devices: 32 us -> 13.9 us
  starting transfers between devices: 23.7 us -> 18.5 us
  Pallas kernels: 54.5 us -> 52.8 us
    all_to_all x0 -> x1, blocking collectives: none -> 20.6 us  [summed_share(): lax.all_to_all(parts, axes, split_axis=0, concat_axis=0, tiled=True)]
    all_to_all x1 -> x0, waiting for transfers between devices: 16.5 us -> none  [summed_share(): lax.all_to_all(parts, axes, split_axis=0, concat_axis=0, tiled=True)]
    all_to_all x1 -> x0, starting transfers between devices: 5.19 us -> none  [summed_share(): lax.all_to_all(parts, axes, split_axis=0, concat_axis=0, tiled=True)]
    pallas_call x5 -> x6, Pallas kernels: 43.1 us -> 42.2 us  [the longest x4 36.4 us: kernel_and_logits(): pl.pallas_call(functools.partial(logits_body, tile=tile, later=later), gr...]
  transfers between devices with their start and end apart: 17 -> 16, of which waited for: 6 -> 7; matrix products, arithmetic and copies ran while one was open for 0% -> 0% of each run, Pallas kernels for 28% -> 29%
where the time goes in v3:
time: 125 us
  Pallas kernels  52.8 us (42%)
  blocking collectives  38.3 us (31%)
  starting transfers between devices  18.5 us (15%)
  waiting for transfers between devices  13.9 us (11%)
    pallas_call x4, Pallas kernels, kernel_and_logits(): pl.pallas_call(functools.partial(logits_body, tile=tile, later=later), gr...  36.4 us
    all_to_all x1, blocking collectives, summed_share(): lax.all_to_all(parts, axes, split_axis=0, concat_axis=0, tiled=True)  20.6 us
    all_to_all x1, blocking collectives, all_shares(): lax.all_to_all(copies, axes, split_axis=0, concat_axis=0, tiled=True)  17.7 us
    ppermute x7, starting transfers between devices, along_x(): lax.ppermute(x, 'x', [(i, (i + shift) % chips) for i in range(chips)])  12.8 us
    pallas_call x3, Pallas kernels, terms(): pl.pallas_call(functools.partial(terms_body, sets=len(sets), tile=tile),...  9.76 us
    ppermute x1, waiting for transfers between devices, across_z(): return lax.ppermute(x, 'zh', [(0, 1), (1, 0)])  6.61 us
    ppermute x7, waiting for transfers between devices, along_x(): lax.ppermute(x, 'x', [(i, (i + shift) % chips) for i in range(chips)])  4.5 us
    pallas_call x1, Pallas kernels, prep(): pl.pallas_call(functools.partial(prep_body, shift=shift), grid_spec=pltpu...  4.37 us
  transfers between devices with their start and end apart: 16, of which 7 were waited for; matrix products, arithmetic and copies ran while one was open for 0% of the time, Pallas kernels for 29%

profile of v3, /device:TPU:0, one launch (start us, length us, event | category | flops | bytes accessed | tf_op | source)
XLA Modules:
  0.0 125.1 jit_solution(3352306214040634726)
XLA Ops:
  0.1 4.4 %prep.1 = (bf16[2048,1280]{1,0:T(8,128)(2,1)S(1)}, bf16[2048,256]{1,0:T(8,128)(2,1)S(1)}, f32[1024,384]{1,0:T(8,128)S(1)}) custom-call(s32[3]{0:T(128)S(1)} %pad_add_fusion.at_ref, f32[2048,384]{1,0:T(8,128)} %l_ref, f32[2048,128]{1,0:T(8,128)} %c_ref.3, f32[4096,384]{1,0:T(8,128)} %refs_0_.5), custom_call_target="tpu_custom_call" | custom-call | tf_op jit(solution)/shard_map/prep/pallas_call | solution.py:82
  4.5 9.1 %kernel_and_logits.4 = (bf16[1024,2048]{1,0:T(8,128)(2,1)S(1)}, bf16[1024,2048]{1,0:T(8,128)(2,1)S(1)}, f32[512,128]{1,0:T(8,128)S(1)}, f32[512,128]{1,0:T(8,128)S(1)}, f32[1024,384]{1,0:T(8,128)S(1)}) custom-call(s32[3]{0:T(128)S(1)} %pad_add_fusion.at_ref, f32[1024,384]{1,0:T(8,128)S(1)} %get-tuple-element.45.p_ref, ...), custom_call_target="tpu_custom_call" | custom-call | flops 7516192768 | bytes 16777216 | tf_op jit(solution)/shard_map/kernel_and_logits/pallas_call | solution.py:161
  13.7 9.1 %kernel_and_logits.5 = (bf16[1024,2048]{1,0:T(8,128)(2,1)S(1)}, bf16[1024,2048]{1,0:T(8,128)(2,1)S(1)}, f32[512,128]{1,0:T(8,128)S(1)}, f32[512,128]{1,0:T(8,128)S(1)}, f32[1024,384]{1,0:T(8,128)S(1)}) custom-call(s32[3]{0:T(128)S(1)} %pad_add_fusion.at_ref, f32[1024,384]{1,0:T(8,128)S(1)} %get-tuple-element.51.p_ref, ...), custom_call_target="tpu_custom_call" | custom-call | flops 7516192768 | bytes 16777216 | tf_op jit(solution)/shard_map/kernel_and_logits/pallas_call | solution.py:161
  23.4 9.1 %kernel_and_logits.6 = (bf16[1024,2048]{1,0:T(8,128)(2,1)S(1)}, bf16[1024,2048]{1,0:T(8,128)(2,1)S(1)}, f32[512,128]{1,0:T(8,128)S(1)}, f32[512,128]{1,0:T(8,128)S(1)}, f32[1024,384]{1,0:T(8,128)S(1)}) custom-call(s32[3]{0:T(128)S(1)} %pad_add_fusion.at_ref, f32[1024,384]{1,0:T(8,128)S(1)} %get-tuple-element.54.p_ref, ...), custom_call_target="tpu_custom_call" | custom-call | flops 7516192768 | bytes 16777216 | tf_op jit(solution)/shard_map/kernel_and_logits/pallas_call | solution.py:161
  32.6 3.2 %collective-permute-start.4 = (f32[512,128]{1,0:T(8,128)S(1)}, f32[512,128]{1,0:T(8,128)S(1)}, u32[]{:S(2)}, u32[]{:S(2)}) collective-permute-start(f32[512,128]{1,0:T(8,128)S(1)} %add.28), channel_id=1, source_target_pairs={{0,4},{2,6},{4,0},{6,2},{1,5},{3,7},{5,1},{7,3},{8,12},{10,14},{12... | collective-permute-start | bytes 786440 | tf_op jit(solution)/shard_map/ppermute | solution.py:320
  35.9 0.7 collective-permute-start.5
  36.5 2.6 %collective-permute-start.6 = (f32[512,128]{1,0:T(8,128)S(1)}, f32[512,128]{1,0:T(8,128)S(1)}, u32[]{:S(2)}, u32[]{:S(2)}) collective-permute-start(f32[512,128]{1,0:T(8,128)S(1)} %add.30), channel_id=1, source_target_pairs={{0,6},{2,0},{4,2},{6,4},{1,7},{3,1},{5,3},{7,5},{8,14},{10,8},{12,... | collective-permute-start | bytes 786440 | tf_op jit(solution)/shard_map/ppermute | solution.py:320
  39.2 9.1 %kernel_and_logits.7 = (bf16[1024,2048]{1,0:T(8,128)(2,1)S(1)}, bf16[1024,2048]{1,0:T(8,128)(2,1)S(1)}, f32[512,128]{1,0:T(8,128)S(1)}, f32[512,128]{1,0:T(8,128)S(1)}) custom-call(s32[3]{0:T(128)S(1)} %pad_add_fusion.at_ref, f32[1024,384]{1,0:T(8,128)S(1)} %get-tuple-element.58.p_ref, bf16[2048,1280]{1,0:T(8,128)(2,1)S(1)} %get-tuple-element.46.b_ref, ...), custom_call_target="tpu_custom_call" | custom-call | flops 7516192768 | bytes 16777216 | tf_op jit(solution)/shard_map/kernel_and_logits/pallas_call | solution.py:161
  48.7 1.2 collective-permute-done.3
  50.0 4.0 %collective-permute-start.7 = (f32[512,128]{1,0:T(8,128)S(1)}, f32[512,128]{1,0:T(8,128)S(1)}, u32[]{:S(2)}, u32[]{:S(2)}) collective-permute-start(f32[512,128]{1,0:T(8,128)S(1)} %add_add_fusion.a_ref), channel_id=1, source_target_pairs={{0,8},{8,0},{1,9},{9,1},{2,10},{10,2},{3,11},{11,3},{4,12},{12,4},... | collective-permute-start | bytes 786440 | tf_op jit(solution)/shard_map/ppermute | solution.py:324
  53.9 6.6 %collective-permute-done.7.b_ref = f32[512,128]{1,0:T(8,128)S(1)} collective-permute-done((f32[512,128]{1,0:T(8,128)S(1)}, f32[512,128]{1,0:T(8,128)S(1)}, u32[]{:S(2)}, u32[]{:S(2)}) %collective-permute-start.7) | collective-permute-done | bytes 262176 | tf_op jit(solution)/shard_map/ppermute | solution.py:324
  60.5 0.8 residual.1.refs_1_
  61.5 3.2 %collective-permute-start.9 = (f32[512,128]{1,0:T(8,128)S(1)}, f32[512,128]{1,0:T(8,128)S(1)}, u32[]{:S(2)}, u32[]{:S(2)}) collective-permute-start(f32[512,128]{1,0:T(8,128)S(1)} %residual.1.refs_1_), channel_id=1, source_target_pairs={{0,6},{2,0},{4,2},{6,4},{1,7},{3,1},{5,3},{7,5},{8,14},{10,8},{12,... | collective-permute-start | bytes 786440 | tf_op jit(solution)/shard_map/ppermute | solution.py:320
  64.7 2.5 %terms.3.refs_8_ = f32[2048,128]{1,0:T(8,128)S(1)} custom-call(f32[512,128]{1,0:T(8,128)S(1)} %collective-permute-done.8.refs_0_, f32[512,128]{1,0:T(8,128)S(1)} %residual.1.refs_1_, bf16[1024,2048]{1,0:T(8,128)(2,1)S(1)} %get-tuple-element.64.refs_2_, bf16[1024,2048]{1,0:T(8,128)(2,1)S(1)} %get-tuple-element.65.refs_3_), custom_call_target="tpu_custom_call" | custom-call | flops 2147483648 | bytes 11010048 | tf_op jit(solution)/shard_map/terms/pallas_call | solution.py:285
  67.2 1.5 %ridge.1 = f32[256,128]{1,0:T(8,128)S(1)} custom-call(s32[3]{0:T(128)S(1)} %pad_add_fusion.at_ref, f32[2048,128]{1,0:T(8,128)} %c_ref.3), custom_call_target="tpu_custom_call" | custom-call | tf_op jit(solution)/shard_map/ridge/pallas_call | solution.py:224
  68.7 2.6 %collective-permute-done.10.refs_1_ = f32[512,128]{1,0:T(8,128)S(1)} collective-permute-done((f32[512,128]{1,0:T(8,128)S(1)}, f32[512,128]{1,0:T(8,128)S(1)}, u32[]{:S(2)}, u32[]{:S(2)}) %collective-permute-start.10) | collective-permute-done | bytes 262176 | tf_op jit(solution)/shard_map/ppermute | solution.py:320
  71.9 3.0 %collective-permute-start.14 = (f32[256,128]{1,0:T(8,128)S(1)}, f32[256,128]{1,0:T(8,128)S(1)}, u32[]{:S(2)}, u32[]{:S(2)}) collective-permute-start(f32[256,128]{1,0:T(8,128)S(1)} %slice.7), channel_id=1, source_target_pairs={{0,6},{2,0},{4,2},{6,4},{1,7},{3,1},{5,3},{7,5},{8,14},{10,8},{12,... | collective-permute-start | bytes 393224 | tf_op jit(solution)/shard_map/ppermute | solution.py:320
  74.9 4.7 %terms.4.refs_4_ = f32[2048,128]{1,0:T(8,128)S(1)} custom-call(f32[512,128]{1,0:T(8,128)S(1)} %collective-permute-done.11.refs_0_, f32[512,128]{1,0:T(8,128)S(1)} %collective-permute-done.10.refs_1_, bf16[1024,2048]{1,0:T(8,128)(2,1)S(1)} %get-tuple-element.69.refs_2_, bf16[1024,2048]{1,0:T(8,128)(2,1)S(1)} %get-tuple-element.70.refs_3_, ...), custom_call_target="tpu_custom_call" | custom-call | flops 4294967296 | bytes 19922944 | tf_op jit(solution)/shard_map/terms/pallas_call | solution.py:285
  79.7 1.6 %collective-permute-done.13 = f32[256,128]{1,0:T(8,128)S(1)} collective-permute-done((f32[256,128]{1,0:T(8,128)S(1)}, f32[256,128]{1,0:T(8,128)S(1)}, u32[]{:S(2)}, u32[]{:S(2)}) %collective-permute-start.13) | collective-permute-done | bytes 131104 | tf_op jit(solution)/shard_map/ppermute | solution.py:320
  81.6 1.5 %collective-permute-done.15.refs_0_ = f32[512,128]{1,0:T(8,128)S(1)} collective-permute-done((f32[512,128]{1,0:T(8,128)S(1)}, f32[512,128]{1,0:T(8,128)S(1)}, u32[]{:S(2)}, u32[]{:S(2)}) %collective-permute-start.15) | collective-permute-done | bytes 262176 | tf_op jit(solution)/shard_map/ppermute | solution.py:302
  83.1 2.5 %terms.5 = f32[2048,128]{1,0:T(8,128)S(1)} custom-call(f32[512,128]{1,0:T(8,128)S(1)} %collective-permute-done.15.refs_0_, f32[512,128]{1,0:T(8,128)S(1)} %constant_dynamic-update-slice_fusion.refs_1_, bf16[1024,2048]{1,0:T(8,128)(2,1)S(1)} %get-tuple-element.77.refs_2_, bf16[1024,2048]{1,0:T(8,128)(2,1)S(1)} %get-tuple-element.78.refs_3_, ...), custom_call_target="tpu_custom_call" | custom-call | flops 2147483648 | bytes 11010048 | tf_op jit(solution)/shard_map/terms/pallas_call | solution.py:285
  85.6 20.6 %all_to_all.10 = f32[8,256,128]{2,1,0:T(8,128)S(1)} all-to-all(f32[8,256,128]{2,1,0:T(8,128)S(1)} %bitcast.6), channel_id=1, replica_groups=mesh['y'=4,'zl'=2,'zh'=2,'x'=4,'core'=2] {'y','zl'}, dimensions={0} | all-to-all | bytes 2097152 | tf_op jit(solution)/shard_map/all_to_all | solution.py:308
  106.4 17.7 %all_to_all.11 = f32[8,256,128]{2,1,0:T(8,128)S(1)} all-to-all(f32[8,256,128]{2,1,0:T(8,128)S(1)} %broadcast_in_dim.3), channel_id=1, replica_groups=mesh['y'=4,'zl'=2,'zh'=2,'x'=4,'core'=2] {'y','zl'}, dimensions={0} | all-to-all | bytes 2097152 | tf_op jit(solution)/shard_map/all_to_all | solution.py:314
  124.2 1.0 copy.7
  (35 shorter events, 2.5 us)
Async XLA Ops:
  13.6 9.8 %collective-permute-start = (f32[512,128]{1,0:T(8,128)S(1)}, f32[512,128]{1,0:T(8,128)S(1)}, u32[]{:S(2)}, u32[]{:S(2)}) collective-permute-start(f32[512,128]{1,0:T(8,128)S(1)} %get-tuple-element.49), channel_id=1, source_target_pairs={{0,1},{1,0},{2,3},{3,2},{4,5},{5,4},{6,7},{7,6},{8,9},{9,8},{10,11... | collective-permute-start | bytes 786440 | tf_op jit(solution)/shard_map/ppermute | solution.py:302
  22.8 13.0 %collective-permute-start.1 = (f32[512,128]{1,0:T(8,128)S(1)}, f32[512,128]{1,0:T(8,128)S(1)}, u32[]{:S(2)}, u32[]{:S(2)}) collective-permute-start(f32[512,128]{1,0:T(8,128)S(1)} %get-tuple-element.53), channel_id=1, source_target_pairs={{0,1},{1,0},{2,3},{3,2},{4,5},{5,4},{6,7},{7,6},{8,9},{9,8},{10,11... | collective-permute-start | bytes 786440 | tf_op jit(solution)/shard_map/ppermute | solution.py:302
  32.5 3.3 %collective-permute-start.2 = (f32[512,128]{1,0:T(8,128)S(1)}, f32[512,128]{1,0:T(8,128)S(1)}, u32[]{:S(2)}, u32[]{:S(2)}) collective-permute-start(f32[512,128]{1,0:T(8,128)S(1)} %get-tuple-element.56), channel_id=1, source_target_pairs={{0,1},{1,0},{2,3},{3,2},{4,5},{5,4},{6,7},{7,6},{8,9},{9,8},{10,11... | collective-permute-start | bytes 786440 | tf_op jit(solution)/shard_map/ppermute | solution.py:302
  32.6 15.8 %collective-permute-start.4 = (f32[512,128]{1,0:T(8,128)S(1)}, f32[512,128]{1,0:T(8,128)S(1)}, u32[]{:S(2)}, u32[]{:S(2)}) collective-permute-start(f32[512,128]{1,0:T(8,128)S(1)} %add.28), channel_id=1, source_target_pairs={{0,4},{2,6},{4,0},{6,2},{1,5},{3,7},{5,1},{7,3},{8,12},{10,14},{12... | collective-permute-start | bytes 786440 | tf_op jit(solution)/shard_map/ppermute | solution.py:320
  35.9 12.6 %collective-permute-start.5 = (f32[512,128]{1,0:T(8,128)S(1)}, f32[512,128]{1,0:T(8,128)S(1)}, u32[]{:S(2)}, u32[]{:S(2)}) collective-permute-start(f32[512,128]{1,0:T(8,128)S(1)} %add.29), channel_id=1, source_target_pairs={{0,2},{2,4},{4,6},{6,0},{1,3},{3,5},{5,7},{7,1},{8,10},{10,12},{12... | collective-permute-start | bytes 786440 | tf_op jit(solution)/shard_map/ppermute | solution.py:320
  36.5 12.1 %collective-permute-start.6 = (f32[512,128]{1,0:T(8,128)S(1)}, f32[512,128]{1,0:T(8,128)S(1)}, u32[]{:S(2)}, u32[]{:S(2)}) collective-permute-start(f32[512,128]{1,0:T(8,128)S(1)} %add.30), channel_id=1, source_target_pairs={{0,6},{2,0},{4,2},{6,4},{1,7},{3,1},{5,3},{7,5},{8,14},{10,8},{12,... | collective-permute-start | bytes 786440 | tf_op jit(solution)/shard_map/ppermute | solution.py:320
  39.2 21.4 %copy-start = (s32[4096]{0:T(1024)S(1)}, s32[4096]{0:T(1024)}, u32[]{:S(2)}) copy-start(s32[4096]{0:T(1024)} %param.5) | copy-start | bytes 49156
  48.3 1.6 %collective-permute-start.3 = (f32[512,128]{1,0:T(8,128)S(1)}, f32[512,128]{1,0:T(8,128)S(1)}, u32[]{:S(2)}, u32[]{:S(2)}) collective-permute-start(f32[512,128]{1,0:T(8,128)S(1)} %get-tuple-element.60), channel_id=1, source_target_pairs={{0,1},{1,0},{2,3},{3,2},{4,5},{5,4},{6,7},{7,6},{8,9},{9,8},{10,11... | collective-permute-start | bytes 786440 | tf_op jit(solution)/shard_map/ppermute | solution.py:302
  50.0 10.6 %collective-permute-start.7 = (f32[512,128]{1,0:T(8,128)S(1)}, f32[512,128]{1,0:T(8,128)S(1)}, u32[]{:S(2)}, u32[]{:S(2)}) collective-permute-start(f32[512,128]{1,0:T(8,128)S(1)} %add_add_fusion.a_ref), channel_id=1, source_target_pairs={{0,8},{8,0},{1,9},{9,1},{2,10},{10,2},{3,11},{11,3},{4,12},{12,4},... | collective-permute-start | bytes 786440 | tf_op jit(solution)/shard_map/ppermute | solution.py:324
  61.3 3.4 %collective-permute-start.8 = (f32[512,128]{1,0:T(8,128)S(1)}, f32[512,128]{1,0:T(8,128)S(1)}, u32[]{:S(2)}, u32[]{:S(2)}) collective-permute-start(f32[512,128]{1,0:T(8,128)S(1)} %residual.1.refs_1_), channel_id=1, source_target_pairs={{0,1},{1,0},{2,3},{3,2},{4,5},{5,4},{6,7},{7,6},{8,9},{9,8},{10,11... | collective-permute-start | bytes 786440 | tf_op jit(solution)/shard_map/ppermute | solution.py:302
  61.4 9.9 %collective-permute-start.10 = (f32[512,128]{1,0:T(8,128)S(1)}, f32[512,128]{1,0:T(8,128)S(1)}, u32[]{:S(2)}, u32[]{:S(2)}) collective-permute-start(f32[512,128]{1,0:T(8,128)S(1)} %residual.1.refs_1_), channel_id=1, source_target_pairs={{0,2},{2,4},{4,6},{6,0},{1,3},{3,5},{5,7},{7,1},{8,10},{10,12},{12... | collective-permute-start | bytes 786440 | tf_op jit(solution)/shard_map/ppermute | solution.py:320
  61.5 9.9 %collective-permute-start.9 = (f32[512,128]{1,0:T(8,128)S(1)}, f32[512,128]{1,0:T(8,128)S(1)}, u32[]{:S(2)}, u32[]{:S(2)}) collective-permute-start(f32[512,128]{1,0:T(8,128)S(1)} %residual.1.refs_1_), channel_id=1, source_target_pairs={{0,6},{2,0},{4,2},{6,4},{1,7},{3,1},{5,3},{7,5},{8,14},{10,8},{12,... | collective-permute-start | bytes 786440 | tf_op jit(solution)/shard_map/ppermute | solution.py:320
  71.3 3.6 %collective-permute-start.11 = (f32[512,128]{1,0:T(8,128)S(1)}, f32[512,128]{1,0:T(8,128)S(1)}, u32[]{:S(2)}, u32[]{:S(2)}) collective-permute-start(f32[512,128]{1,0:T(8,128)S(1)} %collective-permute-done.10.refs_1_), channel_id=1, source_target_pairs={{0,1},{1,0},{2,3},{3,2},{4,5},{5,4},{6,7},{7,6},{8,9},{9,8},{10,11... | collective-permute-start | bytes 786440 | tf_op jit(solution)/shard_map/ppermute | solution.py:302
  71.3 3.6 %collective-permute-start.12 = (f32[512,128]{1,0:T(8,128)S(1)}, f32[512,128]{1,0:T(8,128)S(1)}, u32[]{:S(2)}, u32[]{:S(2)}) collective-permute-start(f32[512,128]{1,0:T(8,128)S(1)} %collective-permute-done.9.refs_5_), channel_id=1, source_target_pairs={{0,1},{1,0},{2,3},{3,2},{4,5},{5,4},{6,7},{7,6},{8,9},{9,8},{10,11... | collective-permute-start | bytes 786440 | tf_op jit(solution)/shard_map/ppermute | solution.py:302
  71.9 7.8 %collective-permute-start.14 = (f32[256,128]{1,0:T(8,128)S(1)}, f32[256,128]{1,0:T(8,128)S(1)}, u32[]{:S(2)}, u32[]{:S(2)}) collective-permute-start(f32[256,128]{1,0:T(8,128)S(1)} %slice.7), channel_id=1, source_target_pairs={{0,6},{2,0},{4,2},{6,4},{1,7},{3,1},{5,3},{7,5},{8,14},{10,8},{12,... | collective-permute-start | bytes 393224 | tf_op jit(solution)/shard_map/ppermute | solution.py:320
  74.9 6.3 %collective-permute-start.13 = (f32[256,128]{1,0:T(8,128)S(1)}, f32[256,128]{1,0:T(8,128)S(1)}, u32[]{:S(2)}, u32[]{:S(2)}) collective-permute-start(f32[256,128]{1,0:T(8,128)S(1)} %slice.6), channel_id=1, source_target_pairs={{0,2},{2,4},{4,6},{6,0},{1,3},{3,5},{5,7},{7,1},{8,10},{10,12},{12... | collective-permute-start | bytes 393224 | tf_op jit(solution)/shard_map/ppermute | solution.py:320
  81.3 1.8 %collective-permute-start.15 = (f32[512,128]{1,0:T(8,128)S(1)}, f32[512,128]{1,0:T(8,128)S(1)}, u32[]{:S(2)}, u32[]{:S(2)}) collective-permute-start(f32[512,128]{1,0:T(8,128)S(1)} %constant_dynamic-update-slice_fusion.refs_1_), channel_id=1, source_target_pairs={{0,1},{1,0},{2,3},{3,2},{4,5},{5,4},{6,7},{7,6},{8,9},{9,8},{10,11... | collective-permute-start | bytes 786440 | tf_op jit(solution)/shard_map/ppermute | solution.py:302

commit v4 on v3

--- a/solution.py
+++ b/solution.py
@@ -75,7 +75,7 @@
         copy.wait()
 
 
-def prep(at, shift, landmarks, coefficients, points, held_rows, block=512):
+def prep(at, shift, landmarks, coefficients, points, held_rows, block=1024):
     marks, feats = landmarks.shape
     classes = coefficients.shape[1]
     wide = 3 * feats + LANES
@@ -101,7 +101,7 @@
             pltpu.VMEM((marks, 2 * classes), bf16),
             pltpu.VMEM((held_rows, feats), f32),
         ],
-        compiler_params=pltpu.CompilerParams(vmem_limit_bytes=8 << 20),
+        compiler_params=pltpu.CompilerParams(vmem_limit_bytes=12 << 20),
         name="prep",
     )(at, landmarks, coefficients, points)
 
@@ -263,13 +263,14 @@
             rt_ref[classes:, rows] = (resid - high).T.astype(bf16)
     for j in range(marks // tile):
         cols = slice(j * tile, (j + 1) * tile)
-        both = None
+        both, small = None, None
         for n in range(sets):
-            left = rt_ref[:, 2 * n * block : 2 * (n + 1) * block]
-            for ref in parts[4 * n + 2 : 4 * n + 4]:
-                term = dot(left, ref[:, cols])
-                both = term if both is None else both + term
-        out = (both[:classes, :] + both[classes:, :]).T
+            rows = slice(2 * n * block, 2 * (n + 1) * block)
+            term = dot(rt_ref[:, rows], parts[4 * n + 2][:, cols])
+            both = term if both is None else both + term
+            term = dot(rt_ref[:classes, rows], parts[4 * n + 3][:, cols])
+            small = term if small is None else small + term
+        out = (both[:classes, :] + both[classes:, :] + small).T
         for ref in before:
             out = out + ref[cols, :]
         out_ref[cols, :] = out

time: 125 us -> 124 us (level)
  Pallas kernels: 52.8 us -> 50.1 us
  waiting for transfers between devices: 13.9 us -> 15.5 us
    pallas_call x3, Pallas kernels: 9.76 us -> 7.58 us  [terms(): pl.pallas_call(functools.partial(terms_body, sets=len(sets), tile=tile),...]
    ppermute x7, waiting for transfers between devices: 4.5 us -> 6.18 us  [along_x(): lax.ppermute(x, 'x', [(i, (i + shift) % chips) for i in range(chips)])]
  transfers between devices with their start and end apart: 16 -> 16, of which waited for: 7 -> 7; matrix products, arithmetic and copies ran while one was open for 0% -> 0% of each run, Pallas kernels for 29% -> 28%
where the time goes in v4:
time: 124 us
  Pallas kernels  50.1 us (40%)
  blocking collectives  38.4 us (31%)
  starting transfers between devices  18.3 us (15%)
  waiting for transfers between devices  15.5 us (12%)
    pallas_call x4, Pallas kernels, kernel_and_logits(): pl.pallas_call(functools.partial(logits_body, tile=tile, later=later), gr...  36.3 us
    all_to_all x1, blocking collectives, summed_share(): lax.all_to_all(parts, axes, split_axis=0, concat_axis=0, tiled=True)  20.6 us
    all_to_all x1, blocking collectives, all_shares(): lax.all_to_all(copies, axes, split_axis=0, concat_axis=0, tiled=True)  17.7 us
    ppermute x7, starting transfers between devices, along_x(): lax.ppermute(x, 'x', [(i, (i + shift) % chips) for i in range(chips)])  12.8 us
    pallas_call x3, Pallas kernels, terms(): pl.pallas_call(functools.partial(terms_body, sets=len(sets), tile=tile),...  7.58 us
    ppermute x1, waiting for transfers between devices, across_z(): return lax.ppermute(x, 'zh', [(0, 1), (1, 0)])  6.61 us
    ppermute x7, waiting for transfers between devices, along_x(): lax.ppermute(x, 'x', [(i, (i + shift) % chips) for i in range(chips)])  6.18 us
    pallas_call x1, Pallas kernels, prep(): pl.pallas_call(functools.partial(prep_body, shift=shift), grid_spec=pltpu...  4.05 us
  transfers between devices with their start and end apart: 16, of which 7 were waited for; matrix products, arithmetic and copies ran while one was open for 0% of the time, Pallas kernels for 28%

profile of v4, /device:TPU:0, one launch (start us, length us, event | category | flops | bytes accessed | tf_op | source)
XLA Modules:
  0.0 123.9 jit_solution(5720305872841967376)
XLA Ops:
  0.1 4.1 %prep.1 = (bf16[2048,1280]{1,0:T(8,128)(2,1)S(1)}, bf16[2048,256]{1,0:T(8,128)(2,1)S(1)}, f32[1024,384]{1,0:T(8,128)S(1)}) custom-call(s32[3]{0:T(128)S(1)} %pad_add_fusion.at_ref, f32[2048,384]{1,0:T(8,128)} %l_ref, f32[2048,128]{1,0:T(8,128)} %c_ref.3, f32[4096,384]{1,0:T(8,128)} %refs_0_.5), custom_call_target="tpu_custom_call" | custom-call | tf_op jit(solution)/shard_map/prep/pallas_call | solution.py:82
  4.1 9.1 %kernel_and_logits.4 = (bf16[1024,2048]{1,0:T(8,128)(2,1)S(1)}, bf16[1024,2048]{1,0:T(8,128)(2,1)S(1)}, f32[512,128]{1,0:T(8,128)S(1)}, f32[512,128]{1,0:T(8,128)S(1)}, f32[1024,384]{1,0:T(8,128)S(1)}) custom-call(s32[3]{0:T(128)S(1)} %pad_add_fusion.at_ref, f32[1024,384]{1,0:T(8,128)S(1)} %get-tuple-element.45.p_ref, ...), custom_call_target="tpu_custom_call" | custom-call | flops 7516192768 | bytes 16777216 | tf_op jit(solution)/shard_map/kernel_and_logits/pallas_call | solution.py:161
  13.3 9.1 %kernel_and_logits.5 = (bf16[1024,2048]{1,0:T(8,128)(2,1)S(1)}, bf16[1024,2048]{1,0:T(8,128)(2,1)S(1)}, f32[512,128]{1,0:T(8,128)S(1)}, f32[512,128]{1,0:T(8,128)S(1)}, f32[1024,384]{1,0:T(8,128)S(1)}) custom-call(s32[3]{0:T(128)S(1)} %pad_add_fusion.at_ref, f32[1024,384]{1,0:T(8,128)S(1)} %get-tuple-element.51.p_ref, ...), custom_call_target="tpu_custom_call" | custom-call | flops 7516192768 | bytes 16777216 | tf_op jit(solution)/shard_map/kernel_and_logits/pallas_call | solution.py:161
  23.0 9.1 %kernel_and_logits.6 = (bf16[1024,2048]{1,0:T(8,128)(2,1)S(1)}, bf16[1024,2048]{1,0:T(8,128)(2,1)S(1)}, f32[512,128]{1,0:T(8,128)S(1)}, f32[512,128]{1,0:T(8,128)S(1)}, f32[1024,384]{1,0:T(8,128)S(1)}) custom-call(s32[3]{0:T(128)S(1)} %pad_add_fusion.at_ref, f32[1024,384]{1,0:T(8,128)S(1)} %get-tuple-element.54.p_ref, ...), custom_call_target="tpu_custom_call" | custom-call | flops 7516192768 | bytes 16777216 | tf_op jit(solution)/shard_map/kernel_and_logits/pallas_call | solution.py:161
  32.2 3.2 %collective-permute-start.4 = (f32[512,128]{1,0:T(8,128)S(1)}, f32[512,128]{1,0:T(8,128)S(1)}, u32[]{:S(2)}, u32[]{:S(2)}) collective-permute-start(f32[512,128]{1,0:T(8,128)S(1)} %add.28), channel_id=1, source_target_pairs={{0,4},{2,6},{4,0},{6,2},{1,5},{3,7},{5,1},{7,3},{8,12},{10,14},{12... | collective-permute-start | bytes 786440 | tf_op jit(solution)/shard_map/ppermute | solution.py:321
  35.5 0.7 collective-permute-start.5
  36.1 2.6 %collective-permute-start.6 = (f32[512,128]{1,0:T(8,128)S(1)}, f32[512,128]{1,0:T(8,128)S(1)}, u32[]{:S(2)}, u32[]{:S(2)}) collective-permute-start(f32[512,128]{1,0:T(8,128)S(1)} %add.30), channel_id=1, source_target_pairs={{0,6},{2,0},{4,2},{6,4},{1,7},{3,1},{5,3},{7,5},{8,14},{10,8},{12,... | collective-permute-start | bytes 786440 | tf_op jit(solution)/shard_map/ppermute | solution.py:321
  38.8 9.0 %kernel_and_logits.7 = (bf16[1024,2048]{1,0:T(8,128)(2,1)S(1)}, bf16[1024,2048]{1,0:T(8,128)(2,1)S(1)}, f32[512,128]{1,0:T(8,128)S(1)}, f32[512,128]{1,0:T(8,128)S(1)}) custom-call(s32[3]{0:T(128)S(1)} %pad_add_fusion.at_ref, f32[1024,384]{1,0:T(8,128)S(1)} %get-tuple-element.58.p_ref, bf16[2048,1280]{1,0:T(8,128)(2,1)S(1)} %get-tuple-element.46.b_ref, ...), custom_call_target="tpu_custom_call" | custom-call | flops 7516192768 | bytes 16777216 | tf_op jit(solution)/shard_map/kernel_and_logits/pallas_call | solution.py:161
  48.3 1.2 collective-permute-done.3
  49.5 4.0 %collective-permute-start.7 = (f32[512,128]{1,0:T(8,128)S(1)}, f32[512,128]{1,0:T(8,128)S(1)}, u32[]{:S(2)}, u32[]{:S(2)}) collective-permute-start(f32[512,128]{1,0:T(8,128)S(1)} %add_add_fusion.a_ref), channel_id=1, source_target_pairs={{0,8},{8,0},{1,9},{9,1},{2,10},{10,2},{3,11},{11,3},{4,12},{12,4},... | collective-permute-start | bytes 786440 | tf_op jit(solution)/shard_map/ppermute | solution.py:325
  53.5 6.6 %collective-permute-done.7.b_ref = f32[512,128]{1,0:T(8,128)S(1)} collective-permute-done((f32[512,128]{1,0:T(8,128)S(1)}, f32[512,128]{1,0:T(8,128)S(1)}, u32[]{:S(2)}, u32[]{:S(2)}) %collective-permute-start.7) | collective-permute-done | bytes 262176 | tf_op jit(solution)/shard_map/ppermute | solution.py:325
  60.1 0.8 residual.1.refs_1_
  61.1 3.2 %collective-permute-start.9 = (f32[512,128]{1,0:T(8,128)S(1)}, f32[512,128]{1,0:T(8,128)S(1)}, u32[]{:S(2)}, u32[]{:S(2)}) collective-permute-start(f32[512,128]{1,0:T(8,128)S(1)} %residual.1.refs_1_), channel_id=1, source_target_pairs={{0,6},{2,0},{4,2},{6,4},{1,7},{3,1},{5,3},{7,5},{8,14},{10,8},{12,... | collective-permute-start | bytes 786440 | tf_op jit(solution)/shard_map/ppermute | solution.py:321
  64.3 2.0 %terms.3.refs_8_ = f32[2048,128]{1,0:T(8,128)S(1)} custom-call(f32[512,128]{1,0:T(8,128)S(1)} %collective-permute-done.8.refs_0_, f32[512,128]{1,0:T(8,128)S(1)} %residual.1.refs_1_, bf16[1024,2048]{1,0:T(8,128)(2,1)S(1)} %get-tuple-element.64.refs_2_, bf16[1024,2048]{1,0:T(8,128)(2,1)S(1)} %get-tuple-element.65.refs_3_), custom_call_target="tpu_custom_call" | custom-call | flops 2147483648 | bytes 11010048 | tf_op jit(solution)/shard_map/terms/pallas_call | solution.py:286
  66.2 1.5 %ridge.1 = f32[256,128]{1,0:T(8,128)S(1)} custom-call(s32[3]{0:T(128)S(1)} %pad_add_fusion.at_ref, f32[2048,128]{1,0:T(8,128)} %c_ref.3), custom_call_target="tpu_custom_call" | custom-call | tf_op jit(solution)/shard_map/ridge/pallas_call | solution.py:224
  67.7 3.2 %collective-permute-done.10.refs_1_ = f32[512,128]{1,0:T(8,128)S(1)} collective-permute-done((f32[512,128]{1,0:T(8,128)S(1)}, f32[512,128]{1,0:T(8,128)S(1)}, u32[]{:S(2)}, u32[]{:S(2)}) %collective-permute-start.10) | collective-permute-done | bytes 262176 | tf_op jit(solution)/shard_map/ppermute | solution.py:321
  71.4 3.0 %collective-permute-start.14 = (f32[256,128]{1,0:T(8,128)S(1)}, f32[256,128]{1,0:T(8,128)S(1)}, u32[]{:S(2)}, u32[]{:S(2)}) collective-permute-start(f32[256,128]{1,0:T(8,128)S(1)} %slice.7), channel_id=1, source_target_pairs={{0,6},{2,0},{4,2},{6,4},{1,7},{3,1},{5,3},{7,5},{8,14},{10,8},{12,... | collective-permute-start | bytes 393224 | tf_op jit(solution)/shard_map/ppermute | solution.py:321
  74.5 3.6 %terms.4.refs_4_ = f32[2048,128]{1,0:T(8,128)S(1)} custom-call(f32[512,128]{1,0:T(8,128)S(1)} %collective-permute-done.11.refs_0_, f32[512,128]{1,0:T(8,128)S(1)} %collective-permute-done.10.refs_1_, bf16[1024,2048]{1,0:T(8,128)(2,1)S(1)} %get-tuple-element.69.refs_2_, bf16[1024,2048]{1,0:T(8,128)(2,1)S(1)} %get-tuple-element.70.refs_3_, ...), custom_call_target="tpu_custom_call" | custom-call | flops 4294967296 | bytes 19922944 | tf_op jit(solution)/shard_map/terms/pallas_call | solution.py:286
  78.1 2.7 %collective-permute-done.13 = f32[256,128]{1,0:T(8,128)S(1)} collective-permute-done((f32[256,128]{1,0:T(8,128)S(1)}, f32[256,128]{1,0:T(8,128)S(1)}, u32[]{:S(2)}, u32[]{:S(2)}) %collective-permute-start.13) | collective-permute-done | bytes 131104 | tf_op jit(solution)/shard_map/ppermute | solution.py:321
  80.9 1.5 %collective-permute-done.15.refs_0_ = f32[512,128]{1,0:T(8,128)S(1)} collective-permute-done((f32[512,128]{1,0:T(8,128)S(1)}, f32[512,128]{1,0:T(8,128)S(1)}, u32[]{:S(2)}, u32[]{:S(2)}) %collective-permute-start.15) | collective-permute-done | bytes 262176 | tf_op jit(solution)/shard_map/ppermute | solution.py:303
  82.4 2.0 %terms.5 = f32[2048,128]{1,0:T(8,128)S(1)} custom-call(f32[512,128]{1,0:T(8,128)S(1)} %collective-permute-done.15.refs_0_, f32[512,128]{1,0:T(8,128)S(1)} %constant_dynamic-update-slice_fusion.refs_1_, bf16[1024,2048]{1,0:T(8,128)(2,1)S(1)} %get-tuple-element.77.refs_2_, bf16[1024,2048]{1,0:T(8,128)(2,1)S(1)} %get-tuple-element.78.refs_3_, ...), custom_call_target="tpu_custom_call" | custom-call | flops 2147483648 | bytes 11010048 | tf_op jit(solution)/shard_map/terms/pallas_call | solution.py:286
  84.4 20.6 %all_to_all.10 = f32[8,256,128]{2,1,0:T(8,128)S(1)} all-to-all(f32[8,256,128]{2,1,0:T(8,128)S(1)} %bitcast.6), channel_id=1, replica_groups=mesh['y'=4,'zl'=2,'zh'=2,'x'=4,'core'=2] {'y','zl'}, dimensions={0} | all-to-all | bytes 2097152 | tf_op jit(solution)/shard_map/all_to_all | solution.py:309
  105.2 17.7 %all_to_all.11 = f32[8,256,128]{2,1,0:T(8,128)S(1)} all-to-all(f32[8,256,128]{2,1,0:T(8,128)S(1)} %broadcast_in_dim.3), channel_id=1, replica_groups=mesh['y'=4,'zl'=2,'zh'=2,'x'=4,'core'=2] {'y','zl'}, dimensions={0} | all-to-all | bytes 2097152 | tf_op jit(solution)/shard_map/all_to_all | solution.py:315
  122.9 1.0 copy.7
  (35 shorter events, 2.4 us)
Async XLA Ops:
  13.2 9.8 %collective-permute-start = (f32[512,128]{1,0:T(8,128)S(1)}, f32[512,128]{1,0:T(8,128)S(1)}, u32[]{:S(2)}, u32[]{:S(2)}) collective-permute-start(f32[512,128]{1,0:T(8,128)S(1)} %get-tuple-element.49), channel_id=1, source_target_pairs={{0,1},{1,0},{2,3},{3,2},{4,5},{5,4},{6,7},{7,6},{8,9},{9,8},{10,11... | collective-permute-start | bytes 786440 | tf_op jit(solution)/shard_map/ppermute | solution.py:303
  22.4 13.0 %collective-permute-start.1 = (f32[512,128]{1,0:T(8,128)S(1)}, f32[512,128]{1,0:T(8,128)S(1)}, u32[]{:S(2)}, u32[]{:S(2)}) collective-permute-start(f32[512,128]{1,0:T(8,128)S(1)} %get-tuple-element.53), channel_id=1, source_target_pairs={{0,1},{1,0},{2,3},{3,2},{4,5},{5,4},{6,7},{7,6},{8,9},{9,8},{10,11... | collective-permute-start | bytes 786440 | tf_op jit(solution)/shard_map/ppermute | solution.py:303
  32.1 3.3 %collective-permute-start.2 = (f32[512,128]{1,0:T(8,128)S(1)}, f32[512,128]{1,0:T(8,128)S(1)}, u32[]{:S(2)}, u32[]{:S(2)}) collective-permute-start(f32[512,128]{1,0:T(8,128)S(1)} %get-tuple-element.56), channel_id=1, source_target_pairs={{0,1},{1,0},{2,3},{3,2},{4,5},{5,4},{6,7},{7,6},{8,9},{9,8},{10,11... | collective-permute-start | bytes 786440 | tf_op jit(solution)/shard_map/ppermute | solution.py:303
  32.2 15.7 %collective-permute-start.4 = (f32[512,128]{1,0:T(8,128)S(1)}, f32[512,128]{1,0:T(8,128)S(1)}, u32[]{:S(2)}, u32[]{:S(2)}) collective-permute-start(f32[512,128]{1,0:T(8,128)S(1)} %add.28), channel_id=1, source_target_pairs={{0,4},{2,6},{4,0},{6,2},{1,5},{3,7},{5,1},{7,3},{8,12},{10,14},{12... | collective-permute-start | bytes 786440 | tf_op jit(solution)/shard_map/ppermute | solution.py:321
  35.5 12.6 %collective-permute-start.5 = (f32[512,128]{1,0:T(8,128)S(1)}, f32[512,128]{1,0:T(8,128)S(1)}, u32[]{:S(2)}, u32[]{:S(2)}) collective-permute-start(f32[512,128]{1,0:T(8,128)S(1)} %add.29), channel_id=1, source_target_pairs={{0,2},{2,4},{4,6},{6,0},{1,3},{3,5},{5,7},{7,1},{8,10},{10,12},{12... | collective-permute-start | bytes 786440 | tf_op jit(solution)/shard_map/ppermute | solution.py:321
  36.1 12.1 %collective-permute-start.6 = (f32[512,128]{1,0:T(8,128)S(1)}, f32[512,128]{1,0:T(8,128)S(1)}, u32[]{:S(2)}, u32[]{:S(2)}) collective-permute-start(f32[512,128]{1,0:T(8,128)S(1)} %add.30), channel_id=1, source_target_pairs={{0,6},{2,0},{4,2},{6,4},{1,7},{3,1},{5,3},{7,5},{8,14},{10,8},{12,... | collective-permute-start | bytes 786440 | tf_op jit(solution)/shard_map/ppermute | solution.py:321
  38.8 21.3 %copy-start = (s32[4096]{0:T(1024)S(1)}, s32[4096]{0:T(1024)}, u32[]{:S(2)}) copy-start(s32[4096]{0:T(1024)} %param.5) | copy-start | bytes 49156
  47.8 1.6 %collective-permute-start.3 = (f32[512,128]{1,0:T(8,128)S(1)}, f32[512,128]{1,0:T(8,128)S(1)}, u32[]{:S(2)}, u32[]{:S(2)}) collective-permute-start(f32[512,128]{1,0:T(8,128)S(1)} %get-tuple-element.60), channel_id=1, source_target_pairs={{0,1},{1,0},{2,3},{3,2},{4,5},{5,4},{6,7},{7,6},{8,9},{9,8},{10,11... | collective-permute-start | bytes 786440 | tf_op jit(solution)/shard_map/ppermute | solution.py:303
  49.5 10.6 %collective-permute-start.7 = (f32[512,128]{1,0:T(8,128)S(1)}, f32[512,128]{1,0:T(8,128)S(1)}, u32[]{:S(2)}, u32[]{:S(2)}) collective-permute-start(f32[512,128]{1,0:T(8,128)S(1)} %add_add_fusion.a_ref), channel_id=1, source_target_pairs={{0,8},{8,0},{1,9},{9,1},{2,10},{10,2},{3,11},{11,3},{4,12},{12,4},... | collective-permute-start | bytes 786440 | tf_op jit(solution)/shard_map/ppermute | solution.py:325
  60.9 3.4 %collective-permute-start.8 = (f32[512,128]{1,0:T(8,128)S(1)}, f32[512,128]{1,0:T(8,128)S(1)}, u32[]{:S(2)}, u32[]{:S(2)}) collective-permute-start(f32[512,128]{1,0:T(8,128)S(1)} %residual.1.refs_1_), channel_id=1, source_target_pairs={{0,1},{1,0},{2,3},{3,2},{4,5},{5,4},{6,7},{7,6},{8,9},{9,8},{10,11... | collective-permute-start | bytes 786440 | tf_op jit(solution)/shard_map/ppermute | solution.py:303
  61.0 9.9 %collective-permute-start.10 = (f32[512,128]{1,0:T(8,128)S(1)}, f32[512,128]{1,0:T(8,128)S(1)}, u32[]{:S(2)}, u32[]{:S(2)}) collective-permute-start(f32[512,128]{1,0:T(8,128)S(1)} %residual.1.refs_1_), channel_id=1, source_target_pairs={{0,2},{2,4},{4,6},{6,0},{1,3},{3,5},{5,7},{7,1},{8,10},{10,12},{12... | collective-permute-start | bytes 786440 | tf_op jit(solution)/shard_map/ppermute | solution.py:321
  61.1 9.8 %collective-permute-start.9 = (f32[512,128]{1,0:T(8,128)S(1)}, f32[512,128]{1,0:T(8,128)S(1)}, u32[]{:S(2)}, u32[]{:S(2)}) collective-permute-start(f32[512,128]{1,0:T(8,128)S(1)} %residual.1.refs_1_), channel_id=1, source_target_pairs={{0,6},{2,0},{4,2},{6,4},{1,7},{3,1},{5,3},{7,5},{8,14},{10,8},{12,... | collective-permute-start | bytes 786440 | tf_op jit(solution)/shard_map/ppermute | solution.py:321
  70.9 3.6 %collective-permute-start.11 = (f32[512,128]{1,0:T(8,128)S(1)}, f32[512,128]{1,0:T(8,128)S(1)}, u32[]{:S(2)}, u32[]{:S(2)}) collective-permute-start(f32[512,128]{1,0:T(8,128)S(1)} %collective-permute-done.10.refs_1_), channel_id=1, source_target_pairs={{0,1},{1,0},{2,3},{3,2},{4,5},{5,4},{6,7},{7,6},{8,9},{9,8},{10,11... | collective-permute-start | bytes 786440 | tf_op jit(solution)/shard_map/ppermute | solution.py:303
  70.9 3.6 %collective-permute-start.12 = (f32[512,128]{1,0:T(8,128)S(1)}, f32[512,128]{1,0:T(8,128)S(1)}, u32[]{:S(2)}, u32[]{:S(2)}) collective-permute-start(f32[512,128]{1,0:T(8,128)S(1)} %collective-permute-done.9.refs_5_), channel_id=1, source_target_pairs={{0,1},{1,0},{2,3},{3,2},{4,5},{5,4},{6,7},{7,6},{8,9},{9,8},{10,11... | collective-permute-start | bytes 786440 | tf_op jit(solution)/shard_map/ppermute | solution.py:303
  71.4 6.7 %collective-permute-start.14 = (f32[256,128]{1,0:T(8,128)S(1)}, f32[256,128]{1,0:T(8,128)S(1)}, u32[]{:S(2)}, u32[]{:S(2)}) collective-permute-start(f32[256,128]{1,0:T(8,128)S(1)} %slice.7), channel_id=1, source_target_pairs={{0,6},{2,0},{4,2},{6,4},{1,7},{3,1},{5,3},{7,5},{8,14},{10,8},{12,... | collective-permute-start | bytes 393224 | tf_op jit(solution)/shard_map/ppermute | solution.py:321
  74.5 6.3 %collective-permute-start.13 = (f32[256,128]{1,0:T(8,128)S(1)}, f32[256,128]{1,0:T(8,128)S(1)}, u32[]{:S(2)}, u32[]{:S(2)}) collective-permute-start(f32[256,128]{1,0:T(8,128)S(1)} %slice.6), channel_id=1, source_target_pairs={{0,2},{2,4},{4,6},{6,0},{1,3},{3,5},{5,7},{7,1},{8,10},{10,12},{12... | collective-permute-start | bytes 393224 | tf_op jit(solution)/shard_map/ppermute | solution.py:321
  80.8 1.6 %collective-permute-start.15 = (f32[512,128]{1,0:T(8,128)S(1)}, f32[512,128]{1,0:T(8,128)S(1)}, u32[]{:S(2)}, u32[]{:S(2)}) collective-permute-start(f32[512,128]{1,0:T(8,128)S(1)} %constant_dynamic-update-slice_fusion.refs_1_), channel_id=1, source_target_pairs={{0,1},{1,0},{2,3},{3,2},{4,5},{5,4},{6,7},{7,6},{8,9},{9,8},{10,11... | collective-permute-start | bytes 786440 | tf_op jit(solution)/shard_map/ppermute | solution.py:303

commit v5 on v4

--- a/solution.py
+++ b/solution.py
@@ -198,6 +198,48 @@
     )(at, held, wide_marks, wide_coefs, *[points] * fetch)
 
 
+def block_and_logits(at, which, held, wide_marks, wide_coefs, tile=512):
+    feats = held.shape[1]
+    block = held.shape[0] // 2
+    marks, wide = wide_marks.shape
+    classes = wide_coefs.shape[1] // 2
+    fixed = pl.Buffered(1)
+
+    def body(at_ref, p_ref, b_ref, c_ref, hi_ref, lo_ref, out_ref, a_ref):
+        logits_body(
+            at_ref, p_ref, b_ref, c_ref, hi_ref, lo_ref, out_ref, out_ref, a_ref, tile=tile, later=None
+        )
+
+    return pl.pallas_call(
+        body,
+        grid_spec=pltpu.PrefetchScalarGridSpec(
+            num_scalar_prefetch=1,
+            grid=(1,),
+            in_specs=[
+                pl.BlockSpec((block, feats), lambda i, s: (lax.rem(s[1] + 1 + which, 2), 0)),
+                pl.BlockSpec((marks, wide), lambda i, s: (0, 0), pipeline_mode=fixed),
+                pl.BlockSpec((marks, 2 * classes), lambda i, s: (0, 0), pipeline_mode=fixed),
+            ],
+            out_specs=[
+                pl.BlockSpec((block, marks), lambda i, s: (0, 0)),
+                pl.BlockSpec((block, marks), lambda i, s: (0, 0)),
+                pl.BlockSpec((block, classes), lambda i, s: (0, 0)),
+            ],
+            scratch_shapes=[pltpu.VMEM((block, wide), bf16)],
+        ),
+        out_shape=[
+            pltpu.VMEM((block, marks), bf16),
+            pltpu.VMEM((block, marks), bf16),
+            pltpu.VMEM((block, classes), f32),
+        ],
+        compiler_params=pltpu.CompilerParams(vmem_limit_bytes=LIMIT_K1 << 20),
+        cost_estimate=pl.CostEstimate(
+            flops=2 * block * classes, bytes_accessed=4 * block * classes, transcendentals=0
+        ),
+        name="block_and_logits",
+    )(at, held, wide_marks, wide_coefs)
+
+
 def small_kernel(body, at, args, outs, name):
     whole = [pl.BlockSpec(x.shape, lambda i, s: (0, 0)) for x in (*args, *outs)]
     return pl.pallas_call(
@@ -249,26 +291,26 @@
         out_ref[part, :] = share[part, :] - hot.astype(f32)
 
 
-def terms_body(*refs, sets, tile):
-    parts, (*before, out_ref, rt_ref) = refs[: 4 * sets], refs[4 * sets :]
-    classes = parts[0].shape[1]
-    block = parts[0].shape[0]
-    marks = parts[2].shape[1]
+def terms_body(*refs, sets, pieces, tile):
+    width = pieces + 2
+    parts, (*before, out_ref, rt_ref) = refs[: width * sets], refs[width * sets :]
+    block, classes = parts[0].shape
+    marks = parts[pieces].shape[1]
     for n in range(sets):
-        for h in range(2):
-            resid = parts[4 * n + h][...]
+        for h in range(pieces):
+            resid = parts[width * n + h][...]
             high = resid.astype(bf16).astype(f32)
-            rows = slice((2 * n + h) * block, (2 * n + h + 1) * block)
+            rows = slice((pieces * n + h) * block, (pieces * n + h + 1) * block)
             rt_ref[:classes, rows] = high.T.astype(bf16)
             rt_ref[classes:, rows] = (resid - high).T.astype(bf16)
     for j in range(marks // tile):
         cols = slice(j * tile, (j + 1) * tile)
         both, small = None, None
         for n in range(sets):
-            rows = slice(2 * n * block, 2 * (n + 1) * block)
-            term = dot(rt_ref[:, rows], parts[4 * n + 2][:, cols])
+            rows = slice(pieces * n * block, pieces * (n + 1) * block)
+            term = dot(rt_ref[:, rows], parts[width * n + pieces][:, cols])
             both = term if both is None else both + term
-            term = dot(rt_ref[:classes, rows], parts[4 * n + 3][:, cols])
+            term = dot(rt_ref[:classes, rows], parts[width * n + pieces + 1][:, cols])
             small = term if small is None else small + term
         out = (both[:classes, :] + both[classes:, :] + small).T
         for ref in before:
@@ -279,12 +321,13 @@
 def terms(sets, before=None, tile=512):
     args = [x for one in sets for x in one]
     block, classes = args[0].shape
-    marks = args[2].shape[1]
-    rows = 2 * block * len(sets)
+    pieces = len(sets[0]) - 2
+    marks = args[pieces].shape[1]
+    rows = pieces * block * len(sets)
     if before is not None:
         args.append(before)
     return pl.pallas_call(
-        functools.partial(terms_body, sets=len(sets), tile=tile),
+        functools.partial(terms_body, sets=len(sets), pieces=pieces, tile=tile),
         in_specs=[pl.BlockSpec(memory_space=pltpu.VMEM)] * len(args),
         out_specs=pl.BlockSpec(memory_space=pltpu.VMEM),
         out_shape=pltpu.VMEM((marks, classes), f32),
@@ -336,21 +379,25 @@
     at, landmarks = lax.optimization_barrier((at, landmarks))
     wide_marks, wide_coefs, held = prep(at, 2, landmarks, first_coefs, points, 2 * block)
     made, mine, arrived, sums = {}, {}, {}, []
-    for shift, later, ready in ((2, 1, ()), (1, 3, (2,)), (3, 0, (1, 3)), (0, None, ())):
+    for shift, later, ready in ((2, 1, ()), (1, 3, (2,)), (3, 0, (1, 3))):
         hi, lo, far, own, *after = kernel_and_logits(at, held, wide_marks, wide_coefs, points, later)
-        held = after[0] if after else None
+        held = after[0]
         made[shift] = hi, lo
         mine[shift], arrived[shift] = own, swapped(far)
         both = [mine[n] + arrived[n] for n in ready]
         if both:
             at, both = lax.optimization_barrier((at, both))
         sums += [along_x(x, n) for x, n in zip(both, ready)]
-    logits = mine[0] + arrived[0] + sums[0] + sums[1] + sums[2]
+    *far_made, far = block_and_logits(at, 0, held, wide_marks, wide_coefs)
+    over = swapped(far)
+    at, far = lax.optimization_barrier((at, far))
+    *own_made, own = block_and_logits(at, 1, held, wide_marks, wide_coefs)
+    logits = own + over + sums[0] + sums[1] + sums[2]
     full = jax.ShapeDtypeStruct((block, classes), f32)
     by_group = labels.reshape(-1, LANES)
     (own,) = small_kernel(residual_body, at, [by_group, logits, across_z(logits)], [full], "residual")
     near = {3: along_x(own, 1), 1: along_x(own, 3)}
-    local = terms([(swapped(own), own, *made[0])])
+    local = terms([(swapped(own), *far_made), (own, *own_made)])
     at, local = lax.optimization_barrier((at, local))
     ridge = own_ridge(at, coefficients)
     local, near, ridge = lax.optimization_barrier((local, near, ridge))

time: 124 us -> 124 us (level)
    pallas_call x3 -> x5, Pallas kernels: 7.58 us -> 17.2 us  [the longest x2 9.57 us: block_and_logits(): pl.pallas_call(body, grid_spec=pltpu.PrefetchScalarGridSpec(num_scalar_pr...]
    pallas_call x4 -> x3, Pallas kernels: 36.3 us -> 27.2 us  [kernel_and_logits(): pl.pallas_call(functools.partial(logits_body, tile=tile, later=later), gr...]
  transfers between devices with their start and end apart: 16 -> 16, of which waited for: 7 -> 4; matrix products, arithmetic and copies ran while one was open for 0% -> 0% of each run, Pallas kernels for 28% -> 28%
where the time goes in v5:
time: 124 us; the launch traced here: 123 us
  Pallas kernels  50.6 us (41%)
  blocking collectives  38.3 us (31%)
  starting transfers between devices  18.3 us (15%)
  waiting for transfers between devices  14.4 us (12%)
    pallas_call x3, Pallas kernels, kernel_and_logits(): pl.pallas_call(functools.partial(logits_body, tile=tile, later=later), gr...  27.2 us
    all_to_all x1, blocking collectives, summed_share(): lax.all_to_all(parts, axes, split_axis=0, concat_axis=0, tiled=True)  20.6 us
    all_to_all x1, blocking collectives, all_shares(): lax.all_to_all(copies, axes, split_axis=0, concat_axis=0, tiled=True)  17.7 us
    ppermute x7, starting transfers between devices, along_x(): lax.ppermute(x, 'x', [(i, (i + shift) % chips) for i in range(chips)])  12.8 us
    pallas_call x2, Pallas kernels, block_and_logits(): pl.pallas_call(body, grid_spec=pltpu.PrefetchScalarGridSpec(num_scalar_pr...  9.57 us
    pallas_call x3, Pallas kernels, terms(): pl.pallas_call(functools.partial(terms_body, sets=len(sets), pieces=piece...  7.59 us
    ppermute x1, waiting for transfers between devices, across_z(): return lax.ppermute(x, 'zh', [(0, 1), (1, 0)])  6.96 us
    ppermute x7, waiting for transfers between devices, along_x(): lax.ppermute(x, 'x', [(i, (i + shift) % chips) for i in range(chips)])  5.86 us
  transfers between devices with their start and end apart: 16, of which 4 were waited for; matrix products, arithmetic and copies ran while one was open for 0% of the time, Pallas kernels for 28%

profile of v5, /device:TPU:0, one launch (start us, length us, event | category | flops | bytes accessed | tf_op | source)
XLA Modules:
  0.0 123.3 jit_solution(9660723874459390471)
XLA Ops:
  0.1 4.1 %prep.1 = (bf16[2048,1280]{1,0:T(8,128)(2,1)S(1)}, bf16[2048,256]{1,0:T(8,128)(2,1)S(1)}, f32[1024,384]{1,0:T(8,128)S(1)}) custom-call(s32[3]{0:T(128)S(1)} %pad_add_fusion.at_ref, f32[2048,384]{1,0:T(8,128)} %l_ref, f32[2048,128]{1,0:T(8,128)} %c_ref.3, f32[4096,384]{1,0:T(8,128)} %refs_0_.5), custom_call_target="tpu_custom_call" | custom-call | tf_op jit(solution)/shard_map/prep/pallas_call | solution.py:82
  4.1 9.1 %kernel_and_logits.3 = (bf16[1024,2048]{1,0:T(8,128)(2,1)S(1)}, bf16[1024,2048]{1,0:T(8,128)(2,1)S(1)}, f32[512,128]{1,0:T(8,128)S(1)}, f32[512,128]{1,0:T(8,128)S(1)}, f32[1024,384]{1,0:T(8,128)S(1)}) custom-call(s32[3]{0:T(128)S(1)} %pad_add_fusion.at_ref, f32[1024,384]{1,0:T(8,128)S(1)} %get-tuple-element.48.p_ref, ...), custom_call_target="tpu_custom_call" | custom-call | flops 7516192768 | bytes 16777216 | tf_op jit(solution)/shard_map/kernel_and_logits/pallas_call | solution.py:161
  13.3 9.0 %kernel_and_logits.4 = (bf16[1024,2048]{1,0:T(8,128)(2,1)S(1)}, bf16[1024,2048]{1,0:T(8,128)(2,1)S(1)}, f32[512,128]{1,0:T(8,128)S(1)}, f32[512,128]{1,0:T(8,128)S(1)}, f32[1024,384]{1,0:T(8,128)S(1)}) custom-call(s32[3]{0:T(128)S(1)} %pad_add_fusion.at_ref, f32[1024,384]{1,0:T(8,128)S(1)} %get-tuple-element.54.p_ref, ...), custom_call_target="tpu_custom_call" | custom-call | flops 7516192768 | bytes 16777216 | tf_op jit(solution)/shard_map/kernel_and_logits/pallas_call | solution.py:161
  23.0 9.1 %kernel_and_logits.5 = (bf16[1024,2048]{1,0:T(8,128)(2,1)S(1)}, bf16[1024,2048]{1,0:T(8,128)(2,1)S(1)}, f32[512,128]{1,0:T(8,128)S(1)}, f32[512,128]{1,0:T(8,128)S(1)}, f32[1024,384]{1,0:T(8,128)S(1)}) custom-call(s32[3]{0:T(128)S(1)} %pad_add_fusion.at_ref, f32[1024,384]{1,0:T(8,128)S(1)} %get-tuple-element.57.p_ref, ...), custom_call_target="tpu_custom_call" | custom-call | flops 7516192768 | bytes 16777216 | tf_op jit(solution)/shard_map/kernel_and_logits/pallas_call | solution.py:161
  32.1 3.2 %collective-permute-start.4 = (f32[512,128]{1,0:T(8,128)S(1)}, f32[512,128]{1,0:T(8,128)S(1)}, u32[]{:S(2)}, u32[]{:S(2)}) collective-permute-start(f32[512,128]{1,0:T(8,128)S(1)} %add.28), channel_id=1, source_target_pairs={{0,4},{2,6},{4,0},{6,2},{1,5},{3,7},{5,1},{7,3},{8,12},{10,14},{12... | collective-permute-start | bytes 786440 | tf_op jit(solution)/shard_map/ppermute | solution.py:364
  36.1 2.7 %collective-permute-start.6 = (f32[512,128]{1,0:T(8,128)S(1)}, f32[512,128]{1,0:T(8,128)S(1)}, u32[]{:S(2)}, u32[]{:S(2)}) collective-permute-start(f32[512,128]{1,0:T(8,128)S(1)} %add.30), channel_id=1, source_target_pairs={{0,6},{2,0},{4,2},{6,4},{1,7},{3,1},{5,3},{7,5},{8,14},{10,8},{12,... | collective-permute-start | bytes 786440 | tf_op jit(solution)/shard_map/ppermute | solution.py:364
  38.7 4.8 %block_and_logits.2 = (bf16[512,2048]{1,0:T(8,128)(2,1)S(1)}, bf16[512,2048]{1,0:T(8,128)(2,1)S(1)}, f32[512,128]{1,0:T(8,128)S(1)}) custom-call(s32[3]{0:T(128)S(1)} %pad_add_fusion.at_ref, f32[1024,384]{1,0:T(8,128)S(1)} %get-tuple-element.61.p_ref, bf16[2048,1280]{1,0:T(8,128)(2,1)S(1)} %get-tuple-element.49.b_ref, ...), custom_call_target="tpu_custom_call" | custom-call | flops 131072 | bytes 262144 | tf_op jit(solution)/shard_map/block_and_logits/pallas_call | solution.py:213
  43.6 4.8 %block_and_logits.3 = (bf16[512,2048]{1,0:T(8,128)(2,1)S(1)}, bf16[512,2048]{1,0:T(8,128)(2,1)S(1)}, f32[512,128]{1,0:T(8,128)S(1)}) custom-call(s32[3]{0:T(128)S(1)} %pad_add_fusion.at_ref, f32[1024,384]{1,0:T(8,128)S(1)} %get-tuple-element.61.p_ref, bf16[2048,1280]{1,0:T(8,128)(2,1)S(1)} %get-tuple-element.49.b_ref, ...), custom_call_target="tpu_custom_call" | custom-call | flops 131072 | bytes 262144 | tf_op jit(solution)/shard_map/block_and_logits/pallas_call | solution.py:213
  48.6 3.9 %collective-permute-start.7 = (f32[512,128]{1,0:T(8,128)S(1)}, f32[512,128]{1,0:T(8,128)S(1)}, u32[]{:S(2)}, u32[]{:S(2)}) collective-permute-start(f32[512,128]{1,0:T(8,128)S(1)} %add_add_fusion.a_ref), channel_id=1, source_target_pairs={{0,8},{8,0},{1,9},{9,1},{2,10},{10,2},{3,11},{11,3},{4,12},{12,4},... | collective-permute-start | bytes 786440 | tf_op jit(solution)/shard_map/ppermute | solution.py:368
  52.5 7.0 %collective-permute-done.7.b_ref = f32[512,128]{1,0:T(8,128)S(1)} collective-permute-done((f32[512,128]{1,0:T(8,128)S(1)}, f32[512,128]{1,0:T(8,128)S(1)}, u32[]{:S(2)}, u32[]{:S(2)}) %collective-permute-start.7) | collective-permute-done | bytes 262176 | tf_op jit(solution)/shard_map/ppermute | solution.py:368
  59.5 0.8 residual.1.refs_3_
  60.3 0.7 collective-permute-start.10
  61.0 2.6 %collective-permute-start.9 = (f32[512,128]{1,0:T(8,128)S(1)}, f32[512,128]{1,0:T(8,128)S(1)}, u32[]{:S(2)}, u32[]{:S(2)}) collective-permute-start(f32[512,128]{1,0:T(8,128)S(1)} %residual.1.refs_3_), channel_id=1, source_target_pairs={{0,6},{2,0},{4,2},{6,4},{1,7},{3,1},{5,3},{7,5},{8,14},{10,8},{12,... | collective-permute-start | bytes 786440 | tf_op jit(solution)/shard_map/ppermute | solution.py:364
  63.7 2.0 %terms.3.refs_8_ = f32[2048,128]{1,0:T(8,128)S(1)} custom-call(f32[512,128]{1,0:T(8,128)S(1)} %collective-permute-done.8.refs_0_, bf16[512,2048]{1,0:T(8,128)(2,1)S(1)} %get-tuple-element.68.refs_1_, bf16[512,2048]{1,0:T(8,128)(2,1)S(1)} %get-tuple-element.69.refs_2_, f32[512,128]{1,0:T(8,128)S(1)} %residual.1.refs_3_, ...), custom_call_target="tpu_custom_call" | custom-call | flops 2147483648 | bytes 11010048 | tf_op jit(solution)/shard_map/terms/pallas_call | solution.py:329
  65.6 1.5 %ridge.1 = f32[256,128]{1,0:T(8,128)S(1)} custom-call(s32[3]{0:T(128)S(1)} %pad_add_fusion.at_ref, f32[2048,128]{1,0:T(8,128)} %c_ref.3), custom_call_target="tpu_custom_call" | custom-call | tf_op jit(solution)/shard_map/ridge/pallas_call | solution.py:266
  67.1 3.2 %collective-permute-done.10.refs_1_ = f32[512,128]{1,0:T(8,128)S(1)} collective-permute-done((f32[512,128]{1,0:T(8,128)S(1)}, f32[512,128]{1,0:T(8,128)S(1)}, u32[]{:S(2)}, u32[]{:S(2)}) %collective-permute-start.10) | collective-permute-done | bytes 262176 | tf_op jit(solution)/shard_map/ppermute | solution.py:364
  70.8 3.0 %collective-permute-start.14 = (f32[256,128]{1,0:T(8,128)S(1)}, f32[256,128]{1,0:T(8,128)S(1)}, u32[]{:S(2)}, u32[]{:S(2)}) collective-permute-start(f32[256,128]{1,0:T(8,128)S(1)} %slice.7), channel_id=1, source_target_pairs={{0,6},{2,0},{4,2},{6,4},{1,7},{3,1},{5,3},{7,5},{8,14},{10,8},{12,... | collective-permute-start | bytes 393224 | tf_op jit(solution)/shard_map/ppermute | solution.py:364
  73.9 3.7 %terms.4.refs_4_ = f32[2048,128]{1,0:T(8,128)S(1)} custom-call(f32[512,128]{1,0:T(8,128)S(1)} %collective-permute-done.11.refs_0_, f32[512,128]{1,0:T(8,128)S(1)} %collective-permute-done.10.refs_1_, bf16[1024,2048]{1,0:T(8,128)(2,1)S(1)} %get-tuple-element.75.refs_2_, bf16[1024,2048]{1,0:T(8,128)(2,1)S(1)} %get-tuple-element.76.refs_3_, ...), custom_call_target="tpu_custom_call" | custom-call | flops 4294967296 | bytes 19922944 | tf_op jit(solution)/shard_map/terms/pallas_call | solution.py:329
  77.5 2.6 %collective-permute-done.13 = f32[256,128]{1,0:T(8,128)S(1)} collective-permute-done((f32[256,128]{1,0:T(8,128)S(1)}, f32[256,128]{1,0:T(8,128)S(1)}, u32[]{:S(2)}, u32[]{:S(2)}) %collective-permute-start.13) | collective-permute-done | bytes 131104 | tf_op jit(solution)/shard_map/ppermute | solution.py:364
  80.3 1.5 %collective-permute-done.15.refs_0_ = f32[512,128]{1,0:T(8,128)S(1)} collective-permute-done((f32[512,128]{1,0:T(8,128)S(1)}, f32[512,128]{1,0:T(8,128)S(1)}, u32[]{:S(2)}, u32[]{:S(2)}) %collective-permute-start.15) | collective-permute-done | bytes 262176 | tf_op jit(solution)/shard_map/ppermute | solution.py:346
  81.8 2.0 %terms.5 = f32[2048,128]{1,0:T(8,128)S(1)} custom-call(f32[512,128]{1,0:T(8,128)S(1)} %collective-permute-done.15.refs_0_, f32[512,128]{1,0:T(8,128)S(1)} %constant_dynamic-update-slice_fusion.refs_1_, bf16[1024,2048]{1,0:T(8,128)(2,1)S(1)} %get-tuple-element.83.refs_2_, bf16[1024,2048]{1,0:T(8,128)(2,1)S(1)} %get-tuple-element.84.refs_3_, ...), custom_call_target="tpu_custom_call" | custom-call | flops 2147483648 | bytes 11010048 | tf_op jit(solution)/shard_map/terms/pallas_call | solution.py:329
  83.8 20.6 %all_to_all.10 = f32[8,256,128]{2,1,0:T(8,128)S(1)} all-to-all(f32[8,256,128]{2,1,0:T(8,128)S(1)} %bitcast.6), channel_id=1, replica_groups=mesh['y'=4,'zl'=2,'zh'=2,'x'=4,'core'=2] {'y','zl'}, dimensions={0} | all-to-all | bytes 2097152 | tf_op jit(solution)/shard_map/all_to_all | solution.py:352
  104.6 17.7 %all_to_all.11 = f32[8,256,128]{2,1,0:T(8,128)S(1)} all-to-all(f32[8,256,128]{2,1,0:T(8,128)S(1)} %broadcast_in_dim.3), channel_id=1, replica_groups=mesh['y'=4,'zl'=2,'zh'=2,'x'=4,'core'=2] {'y','zl'}, dimensions={0} | all-to-all | bytes 2097152 | tf_op jit(solution)/shard_map/all_to_all | solution.py:358
  122.3 1.0 copy.7
  (36 shorter events, 2.6 us)
Async XLA Ops:
  13.2 9.7 %collective-permute-start = (f32[512,128]{1,0:T(8,128)S(1)}, f32[512,128]{1,0:T(8,128)S(1)}, u32[]{:S(2)}, u32[]{:S(2)}) collective-permute-start(f32[512,128]{1,0:T(8,128)S(1)} %get-tuple-element.52), channel_id=1, source_target_pairs={{0,1},{1,0},{2,3},{3,2},{4,5},{5,4},{6,7},{7,6},{8,9},{9,8},{10,11... | collective-permute-start | bytes 786440 | tf_op jit(solution)/shard_map/ppermute | solution.py:346
  22.4 13.0 %collective-permute-start.1 = (f32[512,128]{1,0:T(8,128)S(1)}, f32[512,128]{1,0:T(8,128)S(1)}, u32[]{:S(2)}, u32[]{:S(2)}) collective-permute-start(f32[512,128]{1,0:T(8,128)S(1)} %get-tuple-element.56), channel_id=1, source_target_pairs={{0,1},{1,0},{2,3},{3,2},{4,5},{5,4},{6,7},{7,6},{8,9},{9,8},{10,11... | collective-permute-start | bytes 786440 | tf_op jit(solution)/shard_map/ppermute | solution.py:346
  32.1 3.3 %collective-permute-start.2 = (f32[512,128]{1,0:T(8,128)S(1)}, f32[512,128]{1,0:T(8,128)S(1)}, u32[]{:S(2)}, u32[]{:S(2)}) collective-permute-start(f32[512,128]{1,0:T(8,128)S(1)} %get-tuple-element.59), channel_id=1, source_target_pairs={{0,1},{1,0},{2,3},{3,2},{4,5},{5,4},{6,7},{7,6},{8,9},{9,8},{10,11... | collective-permute-start | bytes 786440 | tf_op jit(solution)/shard_map/ppermute | solution.py:346
  32.1 16.3 %collective-permute-start.4 = (f32[512,128]{1,0:T(8,128)S(1)}, f32[512,128]{1,0:T(8,128)S(1)}, u32[]{:S(2)}, u32[]{:S(2)}) collective-permute-start(f32[512,128]{1,0:T(8,128)S(1)} %add.28), channel_id=1, source_target_pairs={{0,4},{2,6},{4,0},{6,2},{1,5},{3,7},{5,1},{7,3},{8,12},{10,14},{12... | collective-permute-start | bytes 786440 | tf_op jit(solution)/shard_map/ppermute | solution.py:364
  35.4 13.0 %collective-permute-start.5 = (f32[512,128]{1,0:T(8,128)S(1)}, f32[512,128]{1,0:T(8,128)S(1)}, u32[]{:S(2)}, u32[]{:S(2)}) collective-permute-start(f32[512,128]{1,0:T(8,128)S(1)} %add.29), channel_id=1, source_target_pairs={{0,2},{2,4},{4,6},{6,0},{1,3},{3,5},{5,7},{7,1},{8,10},{10,12},{12... | collective-permute-start | bytes 786440 | tf_op jit(solution)/shard_map/ppermute | solution.py:364
  36.1 12.4 %collective-permute-start.6 = (f32[512,128]{1,0:T(8,128)S(1)}, f32[512,128]{1,0:T(8,128)S(1)}, u32[]{:S(2)}, u32[]{:S(2)}) collective-permute-start(f32[512,128]{1,0:T(8,128)S(1)} %add.30), channel_id=1, source_target_pairs={{0,6},{2,0},{4,2},{6,4},{1,7},{3,1},{5,3},{7,5},{8,14},{10,8},{12,... | collective-permute-start | bytes 786440 | tf_op jit(solution)/shard_map/ppermute | solution.py:364
  43.5 15.9 %copy-start = (s32[4096]{0:T(1024)S(1)}, s32[4096]{0:T(1024)}, u32[]{:S(2)}) copy-start(s32[4096]{0:T(1024)} %param.5) | copy-start | bytes 49156
  43.6 4.9 %collective-permute-start.3 = (f32[512,128]{1,0:T(8,128)S(1)}, f32[512,128]{1,0:T(8,128)S(1)}, u32[]{:S(2)}, u32[]{:S(2)}) collective-permute-start(f32[512,128]{1,0:T(8,128)S(1)} %get-tuple-element.62), channel_id=1, source_target_pairs={{0,1},{1,0},{2,3},{3,2},{4,5},{5,4},{6,7},{7,6},{8,9},{9,8},{10,11... | collective-permute-start | bytes 786440 | tf_op jit(solution)/shard_map/ppermute | solution.py:346
  48.6 10.9 %collective-permute-start.7 = (f32[512,128]{1,0:T(8,128)S(1)}, f32[512,128]{1,0:T(8,128)S(1)}, u32[]{:S(2)}, u32[]{:S(2)}) collective-permute-start(f32[512,128]{1,0:T(8,128)S(1)} %add_add_fusion.a_ref), channel_id=1, source_target_pairs={{0,8},{8,0},{1,9},{9,1},{2,10},{10,2},{3,11},{11,3},{4,12},{12,4},... | collective-permute-start | bytes 786440 | tf_op jit(solution)/shard_map/ppermute | solution.py:368
  60.3 3.4 %collective-permute-start.8 = (f32[512,128]{1,0:T(8,128)S(1)}, f32[512,128]{1,0:T(8,128)S(1)}, u32[]{:S(2)}, u32[]{:S(2)}) collective-permute-start(f32[512,128]{1,0:T(8,128)S(1)} %residual.1.refs_3_), channel_id=1, source_target_pairs={{0,1},{1,0},{2,3},{3,2},{4,5},{5,4},{6,7},{7,6},{8,9},{9,8},{10,11... | collective-permute-start | bytes 786440 | tf_op jit(solution)/shard_map/ppermute | solution.py:346
  60.3 9.9 %collective-permute-start.10 = (f32[512,128]{1,0:T(8,128)S(1)}, f32[512,128]{1,0:T(8,128)S(1)}, u32[]{:S(2)}, u32[]{:S(2)}) collective-permute-start(f32[512,128]{1,0:T(8,128)S(1)} %residual.1.refs_3_), channel_id=1, source_target_pairs={{0,2},{2,4},{4,6},{6,0},{1,3},{3,5},{5,7},{7,1},{8,10},{10,12},{12... | collective-permute-start | bytes 786440 | tf_op jit(solution)/shard_map/ppermute | solution.py:364
  61.0 9.3 %collective-permute-start.9 = (f32[512,128]{1,0:T(8,128)S(1)}, f32[512,128]{1,0:T(8,128)S(1)}, u32[]{:S(2)}, u32[]{:S(2)}) collective-permute-start(f32[512,128]{1,0:T(8,128)S(1)} %residual.1.refs_3_), channel_id=1, source_target_pairs={{0,6},{2,0},{4,2},{6,4},{1,7},{3,1},{5,3},{7,5},{8,14},{10,8},{12,... | collective-permute-start | bytes 786440 | tf_op jit(solution)/shard_map/ppermute | solution.py:364
  70.3 3.6 %collective-permute-start.11 = (f32[512,128]{1,0:T(8,128)S(1)}, f32[512,128]{1,0:T(8,128)S(1)}, u32[]{:S(2)}, u32[]{:S(2)}) collective-permute-start(f32[512,128]{1,0:T(8,128)S(1)} %collective-permute-done.10.refs_1_), channel_id=1, source_target_pairs={{0,1},{1,0},{2,3},{3,2},{4,5},{5,4},{6,7},{7,6},{8,9},{9,8},{10,11... | collective-permute-start | bytes 786440 | tf_op jit(solution)/shard_map/ppermute | solution.py:346
  70.3 3.6 %collective-permute-start.12 = (f32[512,128]{1,0:T(8,128)S(1)}, f32[512,128]{1,0:T(8,128)S(1)}, u32[]{:S(2)}, u32[]{:S(2)}) collective-permute-start(f32[512,128]{1,0:T(8,128)S(1)} %collective-permute-done.9.refs_5_), channel_id=1, source_target_pairs={{0,1},{1,0},{2,3},{3,2},{4,5},{5,4},{6,7},{7,6},{8,9},{9,8},{10,11... | collective-permute-start | bytes 786440 | tf_op jit(solution)/shard_map/ppermute | solution.py:346
  70.8 6.7 %collective-permute-start.14 = (f32[256,128]{1,0:T(8,128)S(1)}, f32[256,128]{1,0:T(8,128)S(1)}, u32[]{:S(2)}, u32[]{:S(2)}) collective-permute-start(f32[256,128]{1,0:T(8,128)S(1)} %slice.7), channel_id=1, source_target_pairs={{0,6},{2,0},{4,2},{6,4},{1,7},{3,1},{5,3},{7,5},{8,14},{10,8},{12,... | collective-permute-start | bytes 393224 | tf_op jit(solution)/shard_map/ppermute | solution.py:364
  73.8 6.3 %collective-permute-start.13 = (f32[256,128]{1,0:T(8,128)S(1)}, f32[256,128]{1,0:T(8,128)S(1)}, u32[]{:S(2)}, u32[]{:S(2)}) collective-permute-start(f32[256,128]{1,0:T(8,128)S(1)} %slice.6), channel_id=1, source_target_pairs={{0,2},{2,4},{4,6},{6,0},{1,3},{3,5},{5,7},{7,1},{8,10},{10,12},{12... | collective-permute-start | bytes 393224 | tf_op jit(solution)/shard_map/ppermute | solution.py:364
  80.2 1.6 %collective-permute-start.15 = (f32[512,128]{1,0:T(8,128)S(1)}, f32[512,128]{1,0:T(8,128)S(1)}, u32[]{:S(2)}, u32[]{:S(2)}) collective-permute-start(f32[512,128]{1,0:T(8,128)S(1)} %constant_dynamic-update-slice_fusion.refs_1_), channel_id=1, source_target_pairs={{0,1},{1,0},{2,3},{3,2},{4,5},{5,4},{6,7},{7,6},{8,9},{9,8},{10,11... | collective-permute-start | bytes 786440 | tf_op jit(solution)/shard_map/ppermute | solution.py:346

commit v6 on v5

--- a/solution.py
+++ b/solution.py
@@ -318,7 +318,7 @@
         out_ref[cols, :] = out
 
 
-def terms(sets, before=None, tile=512):
+def terms(sets, before=None, tile=1024):
     args = [x for one in sets for x in one]
     block, classes = args[0].shape
     pieces = len(sets[0]) - 2

time: 124 us -> 124 us (level)
  no operation moved by 1% of the time
where the time goes in v6:
time: 124 us; the launch traced here: 123 us
  Pallas kernels  50.6 us (41%)
  blocking collectives  38.4 us (31%)
  starting transfers between devices  18.3 us (15%)
  waiting for transfers between devices  14.4 us (12%)
    pallas_call x3, Pallas kernels, kernel_and_logits(): pl.pallas_call(functools.partial(logits_body, tile=tile, later=later), gr...  27.2 us
    all_to_all x1, blocking collectives, summed_share(): lax.all_to_all(parts, axes, split_axis=0, concat_axis=0, tiled=True)  20.6 us
    all_to_all x1, blocking collectives, all_shares(): lax.all_to_all(copies, axes, split_axis=0, concat_axis=0, tiled=True)  17.7 us
    ppermute x7, starting transfers between devices, along_x(): lax.ppermute(x, 'x', [(i, (i + shift) % chips) for i in range(chips)])  12.8 us
    pallas_call x2, Pallas kernels, block_and_logits(): pl.pallas_call(body, grid_spec=pltpu.PrefetchScalarGridSpec(num_scalar_pr...  9.57 us
    pallas_call x3, Pallas kernels, terms(): pl.pallas_call(functools.partial(terms_body, sets=len(sets), pieces=piece...  7.59 us
    ppermute x1, waiting for transfers between devices, across_z(): return lax.ppermute(x, 'zh', [(0, 1), (1, 0)])  6.96 us
    ppermute x7, waiting for transfers between devices, along_x(): lax.ppermute(x, 'x', [(i, (i + shift) % chips) for i in range(chips)])  5.87 us
  transfers between devices with their start and end apart: 16, of which 4 were waited for; matrix products, arithmetic and copies ran while one was open for 0% of the time, Pallas kernels for 28%

profile of v6, /device:TPU:0, one launch (start us, length us, event | category | flops | bytes accessed | tf_op | source)
XLA Modules:
  0.0 123.3 jit_solution(9244760235687875851)
XLA Ops:
  0.1 4.1 %prep.1 = (bf16[2048,1280]{1,0:T(8,128)(2,1)S(1)}, bf16[2048,256]{1,0:T(8,128)(2,1)S(1)}, f32[1024,384]{1,0:T(8,128)S(1)}) custom-call(s32[3]{0:T(128)S(1)} %pad_add_fusion.at_ref, f32[2048,384]{1,0:T(8,128)} %l_ref, f32[2048,128]{1,0:T(8,128)} %c_ref.3, f32[4096,384]{1,0:T(8,128)} %refs_0_.5), custom_call_target="tpu_custom_call" | custom-call | tf_op jit(solution)/shard_map/prep/pallas_call | solution.py:82
  4.1 9.1 %kernel_and_logits.3 = (bf16[1024,2048]{1,0:T(8,128)(2,1)S(1)}, bf16[1024,2048]{1,0:T(8,128)(2,1)S(1)}, f32[512,128]{1,0:T(8,128)S(1)}, f32[512,128]{1,0:T(8,128)S(1)}, f32[1024,384]{1,0:T(8,128)S(1)}) custom-call(s32[3]{0:T(128)S(1)} %pad_add_fusion.at_ref, f32[1024,384]{1,0:T(8,128)S(1)} %get-tuple-element.48.p_ref, ...), custom_call_target="tpu_custom_call" | custom-call | flops 7516192768 | bytes 16777216 | tf_op jit(solution)/shard_map/kernel_and_logits/pallas_call | solution.py:161
  13.3 9.0 %kernel_and_logits.4 = (bf16[1024,2048]{1,0:T(8,128)(2,1)S(1)}, bf16[1024,2048]{1,0:T(8,128)(2,1)S(1)}, f32[512,128]{1,0:T(8,128)S(1)}, f32[512,128]{1,0:T(8,128)S(1)}, f32[1024,384]{1,0:T(8,128)S(1)}) custom-call(s32[3]{0:T(128)S(1)} %pad_add_fusion.at_ref, f32[1024,384]{1,0:T(8,128)S(1)} %get-tuple-element.54.p_ref, ...), custom_call_target="tpu_custom_call" | custom-call | flops 7516192768 | bytes 16777216 | tf_op jit(solution)/shard_map/kernel_and_logits/pallas_call | solution.py:161
  23.0 9.1 %kernel_and_logits.5 = (bf16[1024,2048]{1,0:T(8,128)(2,1)S(1)}, bf16[1024,2048]{1,0:T(8,128)(2,1)S(1)}, f32[512,128]{1,0:T(8,128)S(1)}, f32[512,128]{1,0:T(8,128)S(1)}, f32[1024,384]{1,0:T(8,128)S(1)}) custom-call(s32[3]{0:T(128)S(1)} %pad_add_fusion.at_ref, f32[1024,384]{1,0:T(8,128)S(1)} %get-tuple-element.57.p_ref, ...), custom_call_target="tpu_custom_call" | custom-call | flops 7516192768 | bytes 16777216 | tf_op jit(solution)/shard_map/kernel_and_logits/pallas_call | solution.py:161
  32.1 3.2 %collective-permute-start.4 = (f32[512,128]{1,0:T(8,128)S(1)}, f32[512,128]{1,0:T(8,128)S(1)}, u32[]{:S(2)}, u32[]{:S(2)}) collective-permute-start(f32[512,128]{1,0:T(8,128)S(1)} %add.28), channel_id=1, source_target_pairs={{0,4},{2,6},{4,0},{6,2},{1,5},{3,7},{5,1},{7,3},{8,12},{10,14},{12... | collective-permute-start | bytes 786440 | tf_op jit(solution)/shard_map/ppermute | solution.py:364
  36.1 2.7 %collective-permute-start.6 = (f32[512,128]{1,0:T(8,128)S(1)}, f32[512,128]{1,0:T(8,128)S(1)}, u32[]{:S(2)}, u32[]{:S(2)}) collective-permute-start(f32[512,128]{1,0:T(8,128)S(1)} %add.30), channel_id=1, source_target_pairs={{0,6},{2,0},{4,2},{6,4},{1,7},{3,1},{5,3},{7,5},{8,14},{10,8},{12,... | collective-permute-start | bytes 786440 | tf_op jit(solution)/shard_map/ppermute | solution.py:364
  38.7 4.8 %block_and_logits.2 = (bf16[512,2048]{1,0:T(8,128)(2,1)S(1)}, bf16[512,2048]{1,0:T(8,128)(2,1)S(1)}, f32[512,128]{1,0:T(8,128)S(1)}) custom-call(s32[3]{0:T(128)S(1)} %pad_add_fusion.at_ref, f32[1024,384]{1,0:T(8,128)S(1)} %get-tuple-element.61.p_ref, bf16[2048,1280]{1,0:T(8,128)(2,1)S(1)} %get-tuple-element.49.b_ref, ...), custom_call_target="tpu_custom_call" | custom-call | flops 131072 | bytes 262144 | tf_op jit(solution)/shard_map/block_and_logits/pallas_call | solution.py:213
  43.6 4.8 %block_and_logits.3 = (bf16[512,2048]{1,0:T(8,128)(2,1)S(1)}, bf16[512,2048]{1,0:T(8,128)(2,1)S(1)}, f32[512,128]{1,0:T(8,128)S(1)}) custom-call(s32[3]{0:T(128)S(1)} %pad_add_fusion.at_ref, f32[1024,384]{1,0:T(8,128)S(1)} %get-tuple-element.61.p_ref, bf16[2048,1280]{1,0:T(8,128)(2,1)S(1)} %get-tuple-element.49.b_ref, ...), custom_call_target="tpu_custom_call" | custom-call | flops 131072 | bytes 262144 | tf_op jit(solution)/shard_map/block_and_logits/pallas_call | solution.py:213
  48.6 3.9 %collective-permute-start.7 = (f32[512,128]{1,0:T(8,128)S(1)}, f32[512,128]{1,0:T(8,128)S(1)}, u32[]{:S(2)}, u32[]{:S(2)}) collective-permute-start(f32[512,128]{1,0:T(8,128)S(1)} %add_add_fusion.a_ref), channel_id=1, source_target_pairs={{0,8},{8,0},{1,9},{9,1},{2,10},{10,2},{3,11},{11,3},{4,12},{12,4},... | collective-permute-start | bytes 786440 | tf_op jit(solution)/shard_map/ppermute | solution.py:368
  52.5 7.0 %collective-permute-done.7.b_ref = f32[512,128]{1,0:T(8,128)S(1)} collective-permute-done((f32[512,128]{1,0:T(8,128)S(1)}, f32[512,128]{1,0:T(8,128)S(1)}, u32[]{:S(2)}, u32[]{:S(2)}) %collective-permute-start.7) | collective-permute-done | bytes 262176 | tf_op jit(solution)/shard_map/ppermute | solution.py:368
  59.5 0.8 residual.1.refs_3_
  60.3 0.7 collective-permute-start.10
  61.0 2.6 %collective-permute-start.9 = (f32[512,128]{1,0:T(8,128)S(1)}, f32[512,128]{1,0:T(8,128)S(1)}, u32[]{:S(2)}, u32[]{:S(2)}) collective-permute-start(f32[512,128]{1,0:T(8,128)S(1)} %residual.1.refs_3_), channel_id=1, source_target_pairs={{0,6},{2,0},{4,2},{6,4},{1,7},{3,1},{5,3},{7,5},{8,14},{10,8},{12,... | collective-permute-start | bytes 786440 | tf_op jit(solution)/shard_map/ppermute | solution.py:364
  63.7 2.0 %terms.3.refs_8_ = f32[2048,128]{1,0:T(8,128)S(1)} custom-call(f32[512,128]{1,0:T(8,128)S(1)} %collective-permute-done.8.refs_0_, bf16[512,2048]{1,0:T(8,128)(2,1)S(1)} %get-tuple-element.68.refs_1_, bf16[512,2048]{1,0:T(8,128)(2,1)S(1)} %get-tuple-element.69.refs_2_, f32[512,128]{1,0:T(8,128)S(1)} %residual.1.refs_3_, ...), custom_call_target="tpu_custom_call" | custom-call | flops 2147483648 | bytes 11010048 | tf_op jit(solution)/shard_map/terms/pallas_call | solution.py:329
  65.6 1.5 %ridge.1 = f32[256,128]{1,0:T(8,128)S(1)} custom-call(s32[3]{0:T(128)S(1)} %pad_add_fusion.at_ref, f32[2048,128]{1,0:T(8,128)} %c_ref.3), custom_call_target="tpu_custom_call" | custom-call | tf_op jit(solution)/shard_map/ridge/pallas_call | solution.py:266
  67.1 3.2 %collective-permute-done.10.refs_1_ = f32[512,128]{1,0:T(8,128)S(1)} collective-permute-done((f32[512,128]{1,0:T(8,128)S(1)}, f32[512,128]{1,0:T(8,128)S(1)}, u32[]{:S(2)}, u32[]{:S(2)}) %collective-permute-start.10) | collective-permute-done | bytes 262176 | tf_op jit(solution)/shard_map/ppermute | solution.py:364
  70.8 3.0 %collective-permute-start.14 = (f32[256,128]{1,0:T(8,128)S(1)}, f32[256,128]{1,0:T(8,128)S(1)}, u32[]{:S(2)}, u32[]{:S(2)}) collective-permute-start(f32[256,128]{1,0:T(8,128)S(1)} %slice.7), channel_id=1, source_target_pairs={{0,6},{2,0},{4,2},{6,4},{1,7},{3,1},{5,3},{7,5},{8,14},{10,8},{12,... | collective-permute-start | bytes 393224 | tf_op jit(solution)/shard_map/ppermute | solution.py:364
  73.9 3.6 %terms.4.refs_4_ = f32[2048,128]{1,0:T(8,128)S(1)} custom-call(f32[512,128]{1,0:T(8,128)S(1)} %collective-permute-done.11.refs_0_, f32[512,128]{1,0:T(8,128)S(1)} %collective-permute-done.10.refs_1_, bf16[1024,2048]{1,0:T(8,128)(2,1)S(1)} %get-tuple-element.75.refs_2_, bf16[1024,2048]{1,0:T(8,128)(2,1)S(1)} %get-tuple-element.76.refs_3_, ...), custom_call_target="tpu_custom_call" | custom-call | flops 4294967296 | bytes 19922944 | tf_op jit(solution)/shard_map/terms/pallas_call | solution.py:329
  77.5 2.7 %collective-permute-done.13 = f32[256,128]{1,0:T(8,128)S(1)} collective-permute-done((f32[256,128]{1,0:T(8,128)S(1)}, f32[256,128]{1,0:T(8,128)S(1)}, u32[]{:S(2)}, u32[]{:S(2)}) %collective-permute-start.13) | collective-permute-done | bytes 131104 | tf_op jit(solution)/shard_map/ppermute | solution.py:364
  80.3 1.5 %collective-permute-done.15.refs_0_ = f32[512,128]{1,0:T(8,128)S(1)} collective-permute-done((f32[512,128]{1,0:T(8,128)S(1)}, f32[512,128]{1,0:T(8,128)S(1)}, u32[]{:S(2)}, u32[]{:S(2)}) %collective-permute-start.15) | collective-permute-done | bytes 262176 | tf_op jit(solution)/shard_map/ppermute | solution.py:346
  81.8 2.0 %terms.5 = f32[2048,128]{1,0:T(8,128)S(1)} custom-call(f32[512,128]{1,0:T(8,128)S(1)} %collective-permute-done.15.refs_0_, f32[512,128]{1,0:T(8,128)S(1)} %constant_dynamic-update-slice_fusion.refs_1_, bf16[1024,2048]{1,0:T(8,128)(2,1)S(1)} %get-tuple-element.83.refs_2_, bf16[1024,2048]{1,0:T(8,128)(2,1)S(1)} %get-tuple-element.84.refs_3_, ...), custom_call_target="tpu_custom_call" | custom-call | flops 2147483648 | bytes 11010048 | tf_op jit(solution)/shard_map/terms/pallas_call | solution.py:329
  83.8 20.6 %all_to_all.10 = f32[8,256,128]{2,1,0:T(8,128)S(1)} all-to-all(f32[8,256,128]{2,1,0:T(8,128)S(1)} %bitcast.6), channel_id=1, replica_groups=mesh['y'=4,'zl'=2,'zh'=2,'x'=4,'core'=2] {'y','zl'}, dimensions={0} | all-to-all | bytes 2097152 | tf_op jit(solution)/shard_map/all_to_all | solution.py:352
  104.6 17.7 %all_to_all.11 = f32[8,256,128]{2,1,0:T(8,128)S(1)} all-to-all(f32[8,256,128]{2,1,0:T(8,128)S(1)} %broadcast_in_dim.3), channel_id=1, replica_groups=mesh['y'=4,'zl'=2,'zh'=2,'x'=4,'core'=2] {'y','zl'}, dimensions={0} | all-to-all | bytes 2097152 | tf_op jit(solution)/shard_map/all_to_all | solution.py:358
  122.3 1.0 copy.7
  (36 shorter events, 2.6 us)
Async XLA Ops:
  13.2 9.7 %collective-permute-start = (f32[512,128]{1,0:T(8,128)S(1)}, f32[512,128]{1,0:T(8,128)S(1)}, u32[]{:S(2)}, u32[]{:S(2)}) collective-permute-start(f32[512,128]{1,0:T(8,128)S(1)} %get-tuple-element.52), channel_id=1, source_target_pairs={{0,1},{1,0},{2,3},{3,2},{4,5},{5,4},{6,7},{7,6},{8,9},{9,8},{10,11... | collective-permute-start | bytes 786440 | tf_op jit(solution)/shard_map/ppermute | solution.py:346
  22.4 13.0 %collective-permute-start.1 = (f32[512,128]{1,0:T(8,128)S(1)}, f32[512,128]{1,0:T(8,128)S(1)}, u32[]{:S(2)}, u32[]{:S(2)}) collective-permute-start(f32[512,128]{1,0:T(8,128)S(1)} %get-tuple-element.56), channel_id=1, source_target_pairs={{0,1},{1,0},{2,3},{3,2},{4,5},{5,4},{6,7},{7,6},{8,9},{9,8},{10,11... | collective-permute-start | bytes 786440 | tf_op jit(solution)/shard_map/ppermute | solution.py:346
  32.1 3.3 %collective-permute-start.2 = (f32[512,128]{1,0:T(8,128)S(1)}, f32[512,128]{1,0:T(8,128)S(1)}, u32[]{:S(2)}, u32[]{:S(2)}) collective-permute-start(f32[512,128]{1,0:T(8,128)S(1)} %get-tuple-element.59), channel_id=1, source_target_pairs={{0,1},{1,0},{2,3},{3,2},{4,5},{5,4},{6,7},{7,6},{8,9},{9,8},{10,11... | collective-permute-start | bytes 786440 | tf_op jit(solution)/shard_map/ppermute | solution.py:346
  32.1 16.3 %collective-permute-start.4 = (f32[512,128]{1,0:T(8,128)S(1)}, f32[512,128]{1,0:T(8,128)S(1)}, u32[]{:S(2)}, u32[]{:S(2)}) collective-permute-start(f32[512,128]{1,0:T(8,128)S(1)} %add.28), channel_id=1, source_target_pairs={{0,4},{2,6},{4,0},{6,2},{1,5},{3,7},{5,1},{7,3},{8,12},{10,14},{12... | collective-permute-start | bytes 786440 | tf_op jit(solution)/shard_map/ppermute | solution.py:364
  35.4 13.0 %collective-permute-start.5 = (f32[512,128]{1,0:T(8,128)S(1)}, f32[512,128]{1,0:T(8,128)S(1)}, u32[]{:S(2)}, u32[]{:S(2)}) collective-permute-start(f32[512,128]{1,0:T(8,128)S(1)} %add.29), channel_id=1, source_target_pairs={{0,2},{2,4},{4,6},{6,0},{1,3},{3,5},{5,7},{7,1},{8,10},{10,12},{12... | collective-permute-start | bytes 786440 | tf_op jit(solution)/shard_map/ppermute | solution.py:364
  36.1 12.4 %collective-permute-start.6 = (f32[512,128]{1,0:T(8,128)S(1)}, f32[512,128]{1,0:T(8,128)S(1)}, u32[]{:S(2)}, u32[]{:S(2)}) collective-permute-start(f32[512,128]{1,0:T(8,128)S(1)} %add.30), channel_id=1, source_target_pairs={{0,6},{2,0},{4,2},{6,4},{1,7},{3,1},{5,3},{7,5},{8,14},{10,8},{12,... | collective-permute-start | bytes 786440 | tf_op jit(solution)/shard_map/ppermute | solution.py:364
  43.5 15.9 %copy-start = (s32[4096]{0:T(1024)S(1)}, s32[4096]{0:T(1024)}, u32[]{:S(2)}) copy-start(s32[4096]{0:T(1024)} %param.5) | copy-start | bytes 49156
  43.6 4.9 %collective-permute-start.3 = (f32[512,128]{1,0:T(8,128)S(1)}, f32[512,128]{1,0:T(8,128)S(1)}, u32[]{:S(2)}, u32[]{:S(2)}) collective-permute-start(f32[512,128]{1,0:T(8,128)S(1)} %get-tuple-element.62), channel_id=1, source_target_pairs={{0,1},{1,0},{2,3},{3,2},{4,5},{5,4},{6,7},{7,6},{8,9},{9,8},{10,11... | collective-permute-start | bytes 786440 | tf_op jit(solution)/shard_map/ppermute | solution.py:346
  48.6 10.9 %collective-permute-start.7 = (f32[512,128]{1,0:T(8,128)S(1)}, f32[512,128]{1,0:T(8,128)S(1)}, u32[]{:S(2)}, u32[]{:S(2)}) collective-permute-start(f32[512,128]{1,0:T(8,128)S(1)} %add_add_fusion.a_ref), channel_id=1, source_target_pairs={{0,8},{8,0},{1,9},{9,1},{2,10},{10,2},{3,11},{11,3},{4,12},{12,4},... | collective-permute-start | bytes 786440 | tf_op jit(solution)/shard_map/ppermute | solution.py:368
  60.3 3.4 %collective-permute-start.8 = (f32[512,128]{1,0:T(8,128)S(1)}, f32[512,128]{1,0:T(8,128)S(1)}, u32[]{:S(2)}, u32[]{:S(2)}) collective-permute-start(f32[512,128]{1,0:T(8,128)S(1)} %residual.1.refs_3_), channel_id=1, source_target_pairs={{0,1},{1,0},{2,3},{3,2},{4,5},{5,4},{6,7},{7,6},{8,9},{9,8},{10,11... | collective-permute-start | bytes 786440 | tf_op jit(solution)/shard_map/ppermute | solution.py:346
  60.3 9.9 %collective-permute-start.10 = (f32[512,128]{1,0:T(8,128)S(1)}, f32[512,128]{1,0:T(8,128)S(1)}, u32[]{:S(2)}, u32[]{:S(2)}) collective-permute-start(f32[512,128]{1,0:T(8,128)S(1)} %residual.1.refs_3_), channel_id=1, source_target_pairs={{0,2},{2,4},{4,6},{6,0},{1,3},{3,5},{5,7},{7,1},{8,10},{10,12},{12... | collective-permute-start | bytes 786440 | tf_op jit(solution)/shard_map/ppermute | solution.py:364
  61.0 9.3 %collective-permute-start.9 = (f32[512,128]{1,0:T(8,128)S(1)}, f32[512,128]{1,0:T(8,128)S(1)}, u32[]{:S(2)}, u32[]{:S(2)}) collective-permute-start(f32[512,128]{1,0:T(8,128)S(1)} %residual.1.refs_3_), channel_id=1, source_target_pairs={{0,6},{2,0},{4,2},{6,4},{1,7},{3,1},{5,3},{7,5},{8,14},{10,8},{12,... | collective-permute-start | bytes 786440 | tf_op jit(solution)/shard_map/ppermute | solution.py:364
  70.3 3.6 %collective-permute-start.11 = (f32[512,128]{1,0:T(8,128)S(1)}, f32[512,128]{1,0:T(8,128)S(1)}, u32[]{:S(2)}, u32[]{:S(2)}) collective-permute-start(f32[512,128]{1,0:T(8,128)S(1)} %collective-permute-done.10.refs_1_), channel_id=1, source_target_pairs={{0,1},{1,0},{2,3},{3,2},{4,5},{5,4},{6,7},{7,6},{8,9},{9,8},{10,11... | collective-permute-start | bytes 786440 | tf_op jit(solution)/shard_map/ppermute | solution.py:346
  70.3 3.6 %collective-permute-start.12 = (f32[512,128]{1,0:T(8,128)S(1)}, f32[512,128]{1,0:T(8,128)S(1)}, u32[]{:S(2)}, u32[]{:S(2)}) collective-permute-start(f32[512,128]{1,0:T(8,128)S(1)} %collective-permute-done.9.refs_5_), channel_id=1, source_target_pairs={{0,1},{1,0},{2,3},{3,2},{4,5},{5,4},{6,7},{7,6},{8,9},{9,8},{10,11... | collective-permute-start | bytes 786440 | tf_op jit(solution)/shard_map/ppermute | solution.py:346
  70.8 6.7 %collective-permute-start.14 = (f32[256,128]{1,0:T(8,128)S(1)}, f32[256,128]{1,0:T(8,128)S(1)}, u32[]{:S(2)}, u32[]{:S(2)}) collective-permute-start(f32[256,128]{1,0:T(8,128)S(1)} %slice.7), channel_id=1, source_target_pairs={{0,6},{2,0},{4,2},{6,4},{1,7},{3,1},{5,3},{7,5},{8,14},{10,8},{12,... | collective-permute-start | bytes 393224 | tf_op jit(solution)/shard_map/ppermute | solution.py:364
  73.8 6.3 %collective-permute-start.13 = (f32[256,128]{1,0:T(8,128)S(1)}, f32[256,128]{1,0:T(8,128)S(1)}, u32[]{:S(2)}, u32[]{:S(2)}) collective-permute-start(f32[256,128]{1,0:T(8,128)S(1)} %slice.6), channel_id=1, source_target_pairs={{0,2},{2,4},{4,6},{6,0},{1,3},{3,5},{5,7},{7,1},{8,10},{10,12},{12... | collective-permute-start | bytes 393224 | tf_op jit(solution)/shard_map/ppermute | solution.py:364
  80.2 1.6 %collective-permute-start.15 = (f32[512,128]{1,0:T(8,128)S(1)}, f32[512,128]{1,0:T(8,128)S(1)}, u32[]{:S(2)}, u32[]{:S(2)}) collective-permute-start(f32[512,128]{1,0:T(8,128)S(1)} %constant_dynamic-update-slice_fusion.refs_1_), channel_id=1, source_target_pairs={{0,1},{1,0},{2,3},{3,2},{4,5},{5,4},{6,7},{7,6},{8,9},{9,8},{10,11... | collective-permute-start | bytes 786440 | tf_op jit(solution)/shard_map/ppermute | solution.py:346
